TPU v7x, 128 devices: a whole 4x4x4 slice. The times are simulated.
128 devices in a mesh: dom: 32 (over z, y, core), sub: 4 (over x).
Axes of the slice: x: 4, y: 4, z: 4, core: 2. Of those that a mesh axis runs over, the one named last changes fastest.
Arguments:
- charges: float32 [16384, 256], P(('dom', 'sub')), may hold values from -0.3 to 0.3
- points: float32 [3, 16384, 256], P(None, ('dom', 'sub')), may hold values from -1 to 1
- leaf_basis: float32 [16384, 64, 256], P(('dom', 'sub')), may hold values from -0.375 to 0.375
- child_transfer: float32 [16384, 64, 64], P(('dom', 'sub')), may hold values from -0.75 to 0.75
- parent_transfer: float32 [2048, 64, 64], P(('dom', 'sub')), may hold values from -0.75 to 0.75
- nodes_leaf: float32 [3, 16384, 64], P(None, ('dom', 'sub')), may hold values from -2 to 2
- nodes_mid: float32 [3, 2048, 64], P(None, ('dom', 'sub')), may hold values from -2 to 2
- nodes_top: float32 [3, 256, 64], P(None, ('dom', 'sub')), may hold values from -2 to 2
- near_list: int32 [16384, 6], P(('dom', 'sub')), may hold values from -1 to 16383, as said below
- far_leaf: int32 [16384, 16], P(('dom', 'sub')), may hold values from -1 to 16383, as said below
- far_mid: int32 [2048, 16], P(('dom', 'sub')), may hold values from -1 to 2047, as said below
- far_top: int32 [256, 16], P(('dom', 'sub')), may hold values from -1 to 255, as said below
Outputs:
- potential: float32 [16384, 256], P(('dom', 'sub'))
Inputs may be any that keep to these rules, and one draw needn't show every extreme that they name: `near_list`: -1 marks an empty entry; a row's live entries come first, and its first entry is the leaf itself. Row l names only leaves of the aligned block of 128 leaves that holds l or of the blocks beside it. Some rows have all 6 entries live. `far_leaf`: -1 marks an empty entry; a row's live entries come first. Within each aligned block of 128 rows, the entries, empty ones counted, name clusters of each aligned block of 128 clusters exactly 16 times; in some row blocks all entries are live. `far_mid`: -1 marks an empty entry; a row's live entries come first. Within each aligned block of 16 rows, the entries, empty ones counted, name clusters of each aligned block of 16 clusters exactly 2 times; in some row blocks all entries are live. `far_top`: -1 marks an empty entry; a row's live entries come first; in some aligned blocks of 2 rows all entries are live.
All inputs are finite; a program needn't handle non-finite values.
Results may differ from a plain program's by a relative error of at most 0.0003.
Values sent between devices are 32-bit elements; how exact they have to be, the bound alone decides.
No kernel may reach another device: no remote copies, remote signals or barrier semaphores. Data moves between devices by JAX's collectives and lax.ppermute only.
A program may use at most 64 MiB of HBM per device.

v0:
```python
import jax
import jax.numpy as jnp
from jax import lax
from jax.experimental import pallas as pl
from jax.experimental.pallas import tpu as pltpu
from jax.sharding import PartitionSpec as P


f32 = jnp.float32
bf16 = jnp.bfloat16
i32 = jnp.int32
soften = 0.25
AXES = ("dom", "sub")
NB = 4
TRANS = (((1,), (1,)), ((), ()))


def dot(a, b):
    return jnp.dot(a, b, preferred_element_type=f32)


def dot_t(a, b):
    return lax.dot_general(a, b, TRANS, preferred_element_type=f32)


def split3(v):
    h = v.astype(bf16).astype(f32)
    r = v - h
    m = r.astype(bf16).astype(f32)
    return h, m, (r - m).astype(bf16).astype(f32)


def iota(shape, dim):
    return lax.broadcasted_iota(i32, shape, dim)


def upper(n):
    return jnp.where(iota((n, n), 0) <= iota((n, n), 1), 1.0, 0.0).astype(bf16)


def slots(owner_rows, wanted_rows, ids, caps):
    width = owner_rows[0].shape[1]
    tri = upper(width)
    half = caps // 2
    r = iota((caps, width), 0)
    slot = jnp.where(r < half, 2 * r, 2 * (r - half) + 1)
    row = jnp.zeros((2 * caps, 128), f32)
    carry = jnp.zeros((128, 1), f32)
    for own, want in zip(owner_rows, wanted_rows):
        hit = jnp.where(own == iota((128, width), 0), 1.0, 0.0)
        hit_b = hit.astype(bf16)
        cum = dot(hit_b, tri) + carry
        carry = cum[:, width - 1 : width]
        rank = jnp.sum(hit * cum, axis=0, keepdims=True).astype(i32) - 1
        place = jnp.where(rank == slot, 1.0, 0.0)
        vals = jnp.concatenate([place * (ids + 1.0), place * (want + 1.0)], axis=0).astype(bf16)
        row = row + dot_t(vals, hit_b)
    return row, carry


def plan_kernel(
    me_ref, far_ref, mid_ref, near_ref, nl_ref, nm_ref, nt_ref, pts_ref, pay_ref, tab_ref, own_ref, hl_ref, hr_ref, oh_ref
):
    me = me_ref[0]
    lane = iota((1, 128), 1)
    ids = lane.astype(f32)
    far = far_ref[...]
    own = far >> 7
    want = (far & 127).astype(f32)
    row, live = slots([own[c : c + 1] for c in range(16)], [want[c : c + 1] for c in range(16)], ids, 16)
    eye = jnp.where(iota((16, 16), 0) == iota((16, 16), 1), 1.0, 0.0).astype(bf16)
    mid = mid_ref[...]
    mown = dot_t(eye, (mid >> 4).astype(f32).astype(bf16)).astype(i32)
    mwant = dot_t(eye, (mid & 15).astype(f32).astype(bf16))
    mrow, mlive = slots(
        [mown[c : c + 1] for c in range(16)], [mwant[c : c + 1] for c in range(16)], ids[:, 0:16], 2
    )
    col = jnp.concatenate([row, mrow, jnp.zeros((92, 128), f32)], axis=0).T
    mcol = col[:, 32:36]
    tab_ref[0:16, :] = row[0:16]
    tab_ref[16:18, :] = mrow[0:2]
    tab_ref[18:32, :] = jnp.zeros((14, 128), f32)
    even, odd = row[0:8], row[8:16]
    line = jnp.broadcast_to(ids + 1.0, (8, 128))
    for o in range(128):
        a = jnp.broadcast_to(even[:, o : o + 1], (8, 128))
        b = jnp.broadcast_to(odd[:, o : o + 1], (8, 128))
        oh_ref[o * 8 : o * 8 + 8, 0:128] = jnp.where(a == line, 1.0, 0.0)
        oh_ref[o * 8 : o * 8 + 8, 128:256] = jnp.where(b == line, 1.0, 0.0)
    oh = oh_ref[...].astype(bf16)
    z = jnp.zeros((64, 128), f32)
    blocks = []
    for c in range(3):
        x = nl_ref[c]
        big = jnp.concatenate([jnp.concatenate([x, z], axis=1), jnp.concatenate([z, x], axis=1)], axis=0)
        blocks += [v.astype(bf16) for v in split3(big)]
    for c in range(3):
        h, m, l = blocks[3 * c : 3 * c + 3]
        both = dot_t(oh, jnp.concatenate([h, m], axis=0))
        pay_ref[:, c * 8 : c * 8 + 8, :] = (both[:, 0:128] + both[:, 128:256]).reshape(128, 8, 128)
    both = dot_t(oh, jnp.concatenate([blocks[2], blocks[5]], axis=0))
    pay_ref[:, 0:8, :] = pay_ref[:, 0:8, :] + both[:, 0:128].reshape(128, 8, 128)
    pay_ref[:, 8:16, :] = pay_ref[:, 8:16, :] + both[:, 128:256].reshape(128, 8, 128)
    pay_ref[:, 16:24, :] = pay_ref[:, 16:24, :] + dot_t(oh, blocks[8]).reshape(128, 8, 128)
    tops = [jnp.concatenate([nt_ref[c, 0:1], nt_ref[c, 1:2]], axis=1) for c in range(3)]
    zero = jnp.zeros((1, 128), f32)
    last = jnp.concatenate([zero] * 4 + tops + [zero], axis=0)
    pay_ref[:, 24:32, :] = jnp.broadcast_to(last[None], (128, 8, 128))
    la = jnp.where(mcol[:, 0:1] == ids[:, 0:16] + 1.0, 1.0, 0.0)
    lb = jnp.where(mcol[:, 1:2] == ids[:, 0:16] + 1.0, 1.0, 0.0)
    ohm = jnp.concatenate([la, lb], axis=1).astype(bf16)
    for c in range(3):
        xm = nm_ref[c]
        zm = jnp.zeros((16, 64), f32)
        bigm = jnp.concatenate([jnp.concatenate([xm, zm], axis=1), jnp.concatenate([zm, xm], axis=1)], axis=0)
        h, m, l = split3(bigm)
        resm = dot(ohm, h.astype(bf16)) + dot(ohm, m.astype(bf16)) + dot(ohm, l.astype(bf16))
        pay_ref[:, 24 + c : 25 + c, :] = resm[:, None, :]
    idrow = jnp.concatenate(
        [col[:, 16:32] - 1.0, mcol[:, 2:4] - 1.0, live, mlive, jnp.zeros((128, 108), f32)], axis=1
    )
    pay_ref[:, 27:28, :] = idrow[:, None, :]
    near = near_ref[...]
    nown = near >> 7
    nloc = (near & 127).astype(f32)
    tri = upper(128)
    outs = []
    for d in (-1, 0, 1):
        hit = jnp.where((nown == me + d) & (near >= 0), 1.0, 0.0)
        cum = dot(hit.astype(bf16), tri)
        base = jnp.zeros((1, 1), f32)
        acc = jnp.zeros((16, 128), f32)
        for c in range(6):
            pos = (cum[c : c + 1] + base).astype(i32) - 1
            base = base + cum[c : c + 1, 127:128]
            bm = jnp.where((pos & 127) == iota((128, 128), 0), hit[c : c + 1], 0.0).astype(bf16)
            am = jnp.where((pos >> 7) == iota((8, 128), 0), 1.0, 0.0)
            vals = jnp.concatenate([am * (ids + 1.0), am * nloc[c : c + 1]], axis=0).astype(bf16)
            acc = acc + dot_t(vals, bm)
        outs.append((jnp.where(iota((8, 128), 0) == 7, base, acc[0:8]), acc[8:16]))
    own_ref[:, 0:128] = outs[1][0].astype(i32)
    own_ref[:, 128:256] = outs[1][1].astype(i32)
    for ref, k in ((hl_ref, 0), (hr_ref, 2)):
        for c in range(3):
            ref[c * 128 : (c + 1) * 128, :] = pts_ref[c]
        ref[384:392, 0:128] = outs[k][0]
        ref[384:392, 128:256] = outs[k][1]


def plan(me, far_t, far_mid, near_t, nodes_t, nodes_mid, nodes_top, points):
    vm = pl.BlockSpec(memory_space=pltpu.VMEM)
    return pl.pallas_call(
        plan_kernel,
        out_shape=(
            jax.ShapeDtypeStruct((128, 32, 128), f32),
            jax.ShapeDtypeStruct((32, 128), f32),
            jax.ShapeDtypeStruct((8, 256), i32),
            jax.ShapeDtypeStruct((392, 256), f32),
            jax.ShapeDtypeStruct((392, 256), f32),
        ),
        in_specs=[pl.BlockSpec(memory_space=pltpu.SMEM)] + [vm] * 7,
        out_specs=(vm,) * 5,
        scratch_shapes=[pltpu.VMEM((1024, 256), f32)],
        name="plan",
    )(me, far_t, far_mid, near_t, nodes_t, nodes_mid, nodes_top, points)


def tile_rows(x, y, z, a, b):
    r = iota((8, 256), 0)
    v = jnp.where(r == 0, x, jnp.where(r == 1, y, jnp.where(r == 2, z, jnp.where(r == 3, a, b))))
    return jnp.where(r < 5, v, 0.0)


def near_tables(pts_ref, q_ref, sf_ref, qb_ref):
    r = iota((64, 128), 0)
    spread = jnp.where((r >= 48) & (r < 51), 1.0, 0.0).astype(bf16)
    r8 = iota((8, 256), 0)

    def prepare(it, carry):
        for u in range(8):
            n = it * 8 + u
            x = pts_ref[pl.ds(n, 1), :]
            y = pts_ref[pl.ds(128 + n, 1), :]
            z = pts_ref[pl.ds(256 + n, 1), :]
            norm = x * x + y * y + z * z + soften
            h, m, l = split3(tile_rows(x, y, z, jnp.ones_like(x), norm))
            qh, qm, ql = split3(jnp.broadcast_to(q_ref[pl.ds(n, 1), :], (8, 256)))
            q = jnp.where(r8 == 0, qh, jnp.where(r8 == 1, qm, jnp.where(r8 == 2, ql, 0.0)))
            t = jnp.concatenate([h, m, l, h, m, h, q, jnp.zeros_like(q)], axis=0).T.astype(bf16)
            sf_ref[n] = t
            qb_ref[n] = dot(t, spread)
        return carry

    lax.fori_loop(0, 16, prepare, 0)


def near_pairs(lst, base, tgt, sf_ref, qb_ref, d_refs, acc_ref):
    def entry(i):
        return lst[base + i], lst[base + 1024 + i]

    def distances(i, u, ref):
        lv, n = entry(i)
        lrow = jnp.maximum(lv - 1, 0)
        x = tgt[pl.ds(lrow, 1), :]
        y = tgt[pl.ds(128 + lrow, 1), :]
        z = tgt[pl.ds(256 + lrow, 1), :]
        norm = x * x + y * y + z * z
        h, m, l = split3(tile_rows(-2.0 * x, -2.0 * y, -2.0 * z, norm, jnp.ones_like(x)))
        rhs = jnp.concatenate([h, h, h, m, m, l], axis=0).astype(bf16)
        ref[u] = dot(sf_ref[n, :, 0:48], rhs)

    def sums(i, u, ref):
        lv, n = entry(i)
        acc = jnp.zeros((8, 256), f32)
        for j in range(0, 256, 64):
            w = lax.rsqrt(ref[u, j : j + 64, :])
            q = qb_ref[n, j : j + 64, :]
            acc = acc + jnp.sum((w * jnp.concatenate([q, q], axis=1)).reshape(8, 8, 256), axis=0)
        row = jnp.where(lv > 0, lv - 1, 128)
        acc_ref[pl.ds(row, 1), :] = acc_ref[pl.ds(row, 1), :] + jnp.sum(acc, axis=0, keepdims=True)

    d0, d1 = d_refs
    for u in range(NB):
        distances(u, u, d0)

    def step(it, carry):
        i = it * (2 * NB)
        for u in range(NB):
            distances(i + NB + u, u, d1)
        for u in range(NB):
            sums(i + u, u, d0)
        for u in range(NB):
            distances(i + 2 * NB + u, u, d0)
        for u in range(NB):
            sums(i + NB + u, u, d1)
        return carry

    lax.fori_loop(0, (lst[base + 896] + 2 * NB - 1) // (2 * NB), step, 0)


def near_kernel(lst, tgt_l, tgt_r, pts_ref, q_ref, out_own, out_l, out_r, sf_ref, qb_ref, d0_ref, d1_ref, acc_ref):
    near_tables(pts_ref, q_ref, sf_ref, qb_ref)
    for k, (tgt, out) in enumerate(((pts_ref, out_own), (tgt_l, out_l), (tgt_r, out_r))):
        acc_ref[...] = jnp.zeros((136, 256), f32)
        near_pairs(lst, k * 2048, tgt, sf_ref, qb_ref, (d0_ref, d1_ref), acc_ref)
        out[...] = acc_ref[0:128, :]


def near(lists, arrays):
    vm = pl.BlockSpec(memory_space=pltpu.VMEM)
    return pl.pallas_call(
        near_kernel,
        out_shape=tuple(jax.ShapeDtypeStruct((128, 256), f32) for _ in range(3)),
        in_specs=[pl.BlockSpec(memory_space=pltpu.SMEM)] + [vm] * 4,
        out_specs=(vm,) * 3,
        scratch_shapes=[
            pltpu.VMEM((128, 256, 64), bf16),
            pltpu.VMEM((128, 256, 128), f32),
            pltpu.VMEM((NB, 256, 256), f32),
            pltpu.VMEM((NB, 256, 256), f32),
            pltpu.VMEM((136, 256), f32),
        ],
        compiler_params=pltpu.CompilerParams(vmem_limit_bytes=40 << 20),
        name="near",
    )(lists, *arrays)


def halves(x):
    h = x.astype(bf16).astype(f32)
    return h, (x - h).astype(bf16).astype(f32)


def features(x, y, z, source):
    parts = [halves(v) for v in (x, y, z)]
    norm = sum((h + m) * (h + m) for h, m in parts)
    one = jnp.ones_like(x)
    if source:
        nh, nm = halves(norm + soften)
        return [v for h, m in parts for v in (h, m, h, m)] + [one, one, nh, nm]
    nh, nm = halves(norm)
    return [v for h, m in parts for v in (-2.0 * h, -2.0 * h, -2.0 * m, -2.0 * m)] + [nh, nm, one, one]


def far_kernel(
    ids_ref, r1_ref, nl_ref, nm_ref, lm_ref, mm_ref, top_ref, out_ref, v_ref, u_ref, rep_ref, one_ref, mask_ref, ra_ref, mb_ref
):
    for c in range(8):
        r = iota((128, 128), 0) - c * 16
        k = iota((128, 128), 1)
        rep_ref[c] = jnp.where(r == (k >> 3), 1.0, 0.0).astype(bf16)
        one_ref[c] = jnp.where((r >= 0) & (r < 3), 1.0, 0.0).astype(bf16)
        mask_ref[c] = jnp.where((iota((64, 128), 1) & 7) == c, 1.0, 0.0).astype(bf16)
    u_ref[...] = jnp.zeros((18 * 128, 64), f32)
    leaf = features(nl_ref[0].T, nl_ref[1].T, nl_ref[2].T, True)
    mid = features(nm_ref[0], nm_ref[1], nm_ref[2], True)
    for f in range(16):
        for blk in range(16):
            v_ref[pl.ds(blk * 128 + f, 8, stride=16), :] = leaf[f][blk * 8 : blk * 8 + 8]
        for blk in range(2):
            v_ref[pl.ds((16 + blk) * 128 + f, 8, stride=16), :] = mid[f][blk * 8 : blk * 8 + 8]

    for blk in range(18):
        src = lm_ref[blk * 8 : blk * 8 + 8, :] if blk < 16 else mm_ref[blk * 8 - 128 : blk * 8 - 120, :]
        for f, v in enumerate(split3(src)):
            u_ref[pl.ds(blk * 128 + f, 8, stride=16), :] = v

    def prepare(blk, carry):
        rows = pl.ds(pl.multiple_of(blk * 128, 128), 128)
        t = v_ref[rows, :].T.astype(bf16)
        u = u_ref[rows, :].T.astype(bf16)
        for i in range(8):
            ra_ref[blk * 8 + i] = dot(t, rep_ref[i]).astype(bf16)
            mb_ref[blk * 8 + i] = dot(u, one_ref[i])
        return carry

    lax.fori_loop(0, 18, prepare, 0)
    low = iota((128, 128), 1) < 64
    low64 = iota((64, 128), 1) < 64

    def weights(x, y, z):
        tf = jnp.concatenate(features(x, y, z, False), axis=0)
        return jnp.concatenate([jnp.where(low, tf, 0.0), jnp.where(low, 0.0, tf)], axis=0).astype(bf16)

    def group(rhs, g, t0, t1):
        t0 = jnp.maximum(t0, 0)
        t1 = jnp.maximum(t1, 0)
        mask = mask_ref[g]
        lhs = jnp.concatenate([ra_ref[t0] * mask, ra_ref[t1] * mask], axis=1)
        m = jnp.where(low64, mb_ref[t0], mb_ref[t1])
        w = lax.rsqrt(dot(lhs, rhs)) * m
        return jnp.sum(jnp.sum(w.reshape(8, 8, 128), axis=0), axis=0, keepdims=True)

    def leaf_groups(p, groups):
        rhs = weights(*(r1_ref[pl.ds(pl.multiple_of(p * 32 + 8 * c, 8), 8), :] for c in range(3)))
        return [(p, g, group(rhs, g, ids_ref[p, g], ids_ref[p, 8 + g])) for g in groups]

    out_ref[...] = jnp.zeros((128 * 16, 128), f32)
    out_ref[pl.ds(9, 128, stride=16), :] = jnp.broadcast_to(top_ref[...], (128, 128))

    def first(it, carry):
        got = []
        for u in range(4):
            got += leaf_groups(it * 4 + u, range(4))
        for p, g, val in got:
            out_ref[pl.ds(p * 16 + g, 1), :] = val
        return carry

    lax.fori_loop(0, 32, first, 0)

    def second(p, carry):
        @pl.when(ids_ref[p, 18] > 8)
        def _():
            for q, g, val in leaf_groups(p, range(4, 8)):
                out_ref[pl.ds(q * 16 + g, 1), :] = val

        return carry

    lax.fori_loop(0, 128, second, 0)

    def mids(it, carry):
        got = []
        for u in range(2):
            b = (it * 2 + u) * 256 + 24
            rhs = weights(*(r1_ref[pl.ds(b + c, 8, stride=32), :] for c in range(3)))
            for g in range(8):
                p = (it * 2 + u) * 8 + g
                got.append((p, group(rhs, g, 128 + ids_ref[p, 16], 128 + ids_ref[p, 17])))
        for p, val in got:
            out_ref[pl.ds(p * 16 + 8, 1), :] = val
        return carry

    lax.fori_loop(0, 8, mids, 0)


def far(ids, r1, nodes_t, nodes_mid, moments, mid_moments, top_row):
    vm = pl.BlockSpec(memory_space=pltpu.VMEM)
    return pl.pallas_call(
        far_kernel,
        out_shape=jax.ShapeDtypeStruct((128 * 16, 128), f32),
        in_specs=[pl.BlockSpec(memory_space=pltpu.SMEM)] + [vm] * 6,
        out_specs=vm,
        scratch_shapes=[
            pltpu.VMEM((18 * 128, 64), f32),
            pltpu.VMEM((18 * 128, 64), f32),
            pltpu.VMEM((8, 128, 128), bf16),
            pltpu.VMEM((8, 128, 128), bf16),
            pltpu.VMEM((8, 64, 128), bf16),
            pltpu.VMEM((144, 64, 128), bf16),
            pltpu.VMEM((144, 64, 128), f32),
        ],
        compiler_params=pltpu.CompilerParams(vmem_limit_bytes=40 << 20),
        name="far",
    )(ids, r1, nodes_t, nodes_mid, moments, mid_moments, top_row)


def combine_kernel(top_ids, tab_ref, r1_ref, r2_ref, nt_ref, leaf_ref, mid_ref, top_out):
    acc = [jnp.zeros((128, 128), f32), jnp.zeros((128, 128), f32)]
    tag = (iota((128, 128), 0) + 1).astype(f32)
    for g in range(8):
        parts = [p.astype(bf16) for p in split3(r2_ref[pl.ds(g, 128, stride=16), :])]
        for h in range(2):
            oh = jnp.where(tab_ref[8 * h + g : 8 * h + g + 1, :] == tag, 1.0, 0.0).astype(bf16)
            acc[h] = acc[h] + (dot(oh, parts[0]) + dot(oh, parts[1]) + dot(oh, parts[2]))
    leaf_ref[...] = acc[0][:, 0:64] + acc[1][:, 64:128]
    parts = [p.astype(bf16) for p in split3(r2_ref[pl.ds(8, 128, stride=16), :])]
    res = []
    for h in range(2):
        oh = jnp.where(tab_ref[16 + h : 17 + h, :] == tag[0:16], 1.0, 0.0).astype(bf16)
        res.append(dot(oh, parts[0]) + dot(oh, parts[1]) + dot(oh, parts[2]))
    mid_ref[...] = res[0][:, 0:64] + res[1][:, 64:128]
    half = iota((1, 128), 1) >> 6
    pad = jnp.zeros((6, 64), f32)
    cols = [jnp.concatenate([nt_ref[c], pad], axis=0).T for c in range(3)]
    for g in range(2):
        tx, ty, tz = (jnp.broadcast_to(cols[c][:, g : g + 1], (64, 128)) for c in range(3))

        def entry(e, total):
            t = top_ids[g, e]
            p = jnp.maximum(t, 0) >> 1
            h = jnp.where(t < 0, 2, t & 1)
            m = jnp.where(half == h, r2_ref[pl.ds(p * 16 + 9, 1), :], 0.0)
            dx = tx - r1_ref[pl.ds(p * 32 + 28, 1), :]
            dy = ty - r1_ref[pl.ds(p * 32 + 29, 1), :]
            dz = tz - r1_ref[pl.ds(p * 32 + 30, 1), :]
            return total + lax.rsqrt(dx * dx + dy * dy + dz * dz + soften) * m

        total = lax.fori_loop(0, 16, entry, jnp.zeros((64, 128), f32))
        top_out[g * 64 : g * 64 + 64, :] = jnp.broadcast_to(jnp.sum(total, axis=1, keepdims=True), (64, 128))


def combine(far_top, tab, r1, r2, nodes_top):
    vm = pl.BlockSpec(memory_space=pltpu.VMEM)
    return pl.pallas_call(
        combine_kernel,
        out_shape=(
            jax.ShapeDtypeStruct((128, 64), f32),
            jax.ShapeDtypeStruct((16, 64), f32),
            jax.ShapeDtypeStruct((128, 128), f32),
        ),
        in_specs=[pl.BlockSpec(memory_space=pltpu.SMEM)] + [vm] * 4,
        out_specs=(vm,) * 3,
        name="combine",
    )(far_top, tab, r1, r2, nodes_top)


def swap(x):
    return lax.all_to_all(x, AXES, split_axis=0, concat_axis=0, tiled=True)


def local(
    charges,
    points,
    leaf_basis,
    child_transfer,
    parent_transfer,
    nodes_leaf,
    nodes_mid,
    nodes_top,
    near_list,
    far_leaf,
    far_mid,
    far_top,
):
    shards = lax.axis_size(AXES)
    me = lax.axis_index(AXES).astype(i32).reshape(1)
    down_perm = [(i + 1, i) for i in range(shards - 1)]
    up_perm = [(i, i + 1) for i in range(shards - 1)]
    nodes_t = jnp.transpose(nodes_leaf, (0, 2, 1))
    pay, tab, own_list, to_left, to_right = plan(
        me, far_leaf.T, far_mid, near_list.T, nodes_t, nodes_mid, nodes_top, points
    )
    from_right = lax.ppermute(to_left, AXES, down_perm)
    from_left = lax.ppermute(to_right, AXES, up_perm)
    r1 = swap(pay)
    leaf_moments = jnp.sum(leaf_basis * charges[:, None, :], axis=2)
    mid_moments = jnp.sum(child_transfer * leaf_moments[:, None, :], axis=2).reshape(16, 8, 64).sum(axis=1)
    top_moments = jnp.sum(parent_transfer * mid_moments[:, None, :], axis=2).reshape(2, 8, 64).sum(axis=1)
    lists = jnp.stack([own_list, from_left[384:392].astype(i32), from_right[384:392].astype(i32)])
    lists = jnp.transpose(lists.reshape(3, 8, 2, 128), (0, 2, 1, 3)).reshape(6144)
    flat = points.reshape(384, 256)
    near_own, near_l, near_r = near(lists, [from_left, from_right, flat, charges])
    back_l = lax.ppermute(near_l, AXES, down_perm)
    back_r = lax.ppermute(near_r, AXES, up_perm)
    r1, near_own, leaf_moments, mid_moments, top_moments = lax.optimization_barrier(
        (r1, near_own, leaf_moments, mid_moments, top_moments)
    )
    ids = r1[:, 27, :].astype(i32)
    r1 = r1.reshape(4096, 128)
    pay2 = far(ids, r1, nodes_t, nodes_mid, leaf_moments, mid_moments, top_moments.reshape(1, 128))
    r2 = swap(pay2.reshape(128, 16, 128)).reshape(2048, 128)
    back = back_l + back_r
    leaf_local, mid_local, top_cols = combine(far_top, tab, r1, r2, nodes_top)
    top_local = top_cols[:, 0].reshape(2, 64)
    mid_down = mid_local + jnp.sum(parent_transfer * jnp.repeat(top_local, 8, axis=0)[:, :, None], axis=1)
    leaf_down = leaf_local + jnp.sum(child_transfer * jnp.repeat(mid_down, 8, axis=0)[:, :, None], axis=1)
    return jnp.sum(leaf_basis * leaf_down[:, :, None], axis=1) + near_own + back


def solution(mesh):
    placed = (
        P(AXES, None),
        P(None, AXES, None),
        P(AXES, None, None),
        P(AXES, None, None),
        P(AXES, None, None),
        P(None, AXES, None),
        P(None, AXES, None),
        P(None, AXES, None),
        P(AXES, None),
        P(AXES, None),
        P(AXES, None),
        P(AXES, None),
    )
    return jax.shard_map(local, mesh=mesh, in_specs=placed, out_specs=P(AXES, None), check_vma=False)
```

profile of v0, /device:TPU:1, one launch (start us, length us, event | category | flops | bytes accessed | tf_op | source)
XLA Modules:
  0.0 176.5 jit_solution(17964510845694038151)
XLA Ops:
  0.0 7.0 %plan.1 = (f32[128,32,128]{2,1,0:T(8,128)}, f32[32,128]{1,0:T(8,128)}, s32[8,256]{1,0:T(8,128)}, f32[392,256]{1,0:T(8,128)}, f32[392,256]{1,0:T(8,128)}) custom-call(s32[1]{0:T(128)} %bitcast.me_ref, s32[16,128]{1,0:T(8,128)} %bitcast.32, s32[16,16]{1,0:T(8,128)} %mid_ref.1, s32[6,128]{1,0:T(8,128)} %bitcast.34, f32[3,64,128]{2,1,0:T(8,128)} %bitcast.29, ...), custom_call_target="tpu_custom_call" | custom-call | tf_op jit(solution)/shard_map/plan/pallas_call | solution.py:152
  7.0 11.5 %all-to-all-start = ((f32[128,32,128]{2,1,0:T(8,128)}), f32[128,32,128]{2,1,0:T(8,128)S(1)}, u32[]{:S(2)}, u32[]{:S(2)}) async-start(f32[128,32,128]{2,1,0:T(8,128)} %get-tuple-element.22), calls=%async_computation | async-start | bytes 4194304 | tf_op jit(solution)/shard_map/all_to_all | solution.py:447
  18.5 4.8 %collective-permute-start.1 = (f32[392,256]{1,0:T(8,128)}, f32[392,256]{1,0:T(8,128)S(1)}, u32[]{:S(2)}, u32[]{:S(2)}) collective-permute-start(f32[392,256]{1,0:T(8,128)} %get-tuple-element.25), channel_id=1, source_target_pairs={{1,0},{2,1},{3,2},{4,3},{5,4},{6,5},{7,6},{8,7},{9,8},{10,9},{11,1... | collective-permute-start | bytes 1204232 | tf_op jit(solution)/shard_map/ppermute | solution.py:472
  23.3 1.9 %collective-permute-start = (f32[392,256]{1,0:T(8,128)}, f32[392,256]{1,0:T(8,128)S(1)}, u32[]{:S(2)}, u32[]{:S(2)}) collective-permute-start(f32[392,256]{1,0:T(8,128)} %get-tuple-element.24), channel_id=1, source_target_pairs={{0,1},{1,2},{2,3},{3,4},{4,5},{5,6},{6,7},{7,8},{8,9},{9,10},{10,1... | collective-permute-start | bytes 1204232 | tf_op jit(solution)/shard_map/ppermute | solution.py:473
  25.2 0.0 copy-done.2
  25.2 4.5 %multiply_reduce_fusion.1.lm_ref = f32[128,64]{1,0:T(8,128)S(1)} fusion(f32[128,64,256]{2,1,0:T(8,128)} %param.14, f32[128,256]{1,0:T(8,128)S(1)} %copy-done.2), kind=kLoop, calls=%fused_computation.1 | loop fusion | flops 4186112 | bytes 8552448 | tf_op jit(solution)/shard_map/reduce_sum | solution.py:475
  29.7 0.0 copy-start.1
  29.8 0.1 copy.30
  29.8 2.0 %multiply_reduce_fusion.3 = f32[128,64]{0,1:T(8,128)S(1)} fusion(f32[128,64,64]{0,2,1:T(8,128)} %param.15, f32[128,64]{0,1:T(8,128)S(1)} %copy.30), kind=kLoop, calls=%fused_computation.3 | loop fusion | flops 1040384 | bytes 2162688 | tf_op jit(solution)/shard_map/reduce_sum | solution.py:476
  31.8 0.7 copy.31
  32.5 0.9 bitcast_reduce_fusion.mm_ref
  33.4 1.3 multiply_reduce_fusion.5
  34.7 16.3 %collective-permute-done.1.tgt_r = f32[392,256]{1,0:T(8,128)S(1)} collective-permute-done((f32[392,256]{1,0:T(8,128)}, f32[392,256]{1,0:T(8,128)S(1)}, u32[]{:S(2)}, u32[]{:S(2)}) %collective-permute-start.1) | collective-permute-done | bytes 401440 | tf_op jit(solution)/shard_map/ppermute | solution.py:472
  50.9 1.5 collective-permute-done.tgt_l
  52.4 0.7 pad_add_fusion
  53.1 0.0 copy-done.1
  53.1 33.6 %near.1 = (f32[128,256]{1,0:T(8,128)S(1)}, f32[128,256]{1,0:T(8,128)S(1)}, f32[128,256]{1,0:T(8,128)S(1)}) custom-call(s32[6144]{0:T(1024)S(1)} %bitcast.31, f32[392,256]{1,0:T(8,128)S(1)} %collective-permute-done.tgt_l, f32[392,256]{1,0:T(8,128)S(1)} %collective-permute-done.1.tgt_r, f32[384,256]{1,0:T(8,128)S(1)} %bitcast.28, f32[128,256]{1,0:T(8,128)S(1)} %copy-done.2), custom_call_target="tpu_custom_call" | custom-call | tf_op jit(solution)/shard_map/near/pallas_call | solution.py:251
  86.7 0.0 copy-start.4
  86.7 0.6 copy-done.4
  87.4 0.6 copy-done.7
  88.0 0.7 copy-done.9
  88.7 0.0 all-to-all-done
  88.7 1.2 copy.32
  89.9 0.1 reshape.47.top_ref
  90.0 0.0 copy-done
  90.0 35.4 %far.1 = f32[2048,128]{1,0:T(8,128)} custom-call(s32[128,128]{1,0:T(8,128)S(1)} %fusion.ids_ref, f32[4096,128]{1,0:T(8,128)S(1)} %bitcast.26, f32[3,64,128]{2,1,0:T(8,128)S(1)} %bitcast.30, f32[3,16,64]{2,1,0:T(8,128)S(1)} %copy-done.6, f32[128,64]{1,0:T(8,128)S(1)} %multiply_reduce_fusion.1.lm_ref, f32[16,64]{1,0:T(8,128)S(1)} %bitcast_reduce_fusion.mm_ref, ...), custom_call_target="tpu_custom_call" | custom-call | tf_op jit(solution)/shard_map/far/pallas_call | solution.py:377
  125.4 19.6 %all-to-all-start.1 = ((f32[128,16,128]{2,1,0:T(8,128)}), f32[128,16,128]{2,1,0:T(8,128)}, u32[]{:S(2)}, u32[]{:S(2)}) async-start(f32[128,16,128]{2,1,0:T(8,128)} %bitcast.14), calls=%async_computation.1 | async-start | bytes 2097152 | tf_op jit(solution)/shard_map/all_to_all | solution.py:447
  145.0 0.0 copy-start.12
  145.0 0.0 copy-start.11
  145.1 4.9 %collective-permute-start.2 = (f32[128,256]{1,0:T(8,128)S(1)}, f32[128,256]{1,0:T(8,128)S(1)}, u32[]{:S(2)}, u32[]{:S(2)}) collective-permute-start(f32[128,256]{1,0:T(8,128)S(1)} %copy-done.10), channel_id=1, source_target_pairs={{1,0},{2,1},{3,2},{4,3},{5,4},{6,5},{7,6},{8,7},{9,8},{10,9},{11,1... | collective-permute-start | bytes 393224 | tf_op jit(solution)/shard_map/ppermute | solution.py:482
  149.9 0.0 copy-done.8
  150.0 1.9 %collective-permute-start.3 = (f32[128,256]{1,0:T(8,128)S(1)}, f32[128,256]{1,0:T(8,128)S(1)}, u32[]{:S(2)}, u32[]{:S(2)}) collective-permute-start(f32[128,256]{1,0:T(8,128)S(1)} %copy-done.8), channel_id=1, source_target_pairs={{0,1},{1,2},{2,3},{3,4},{4,5},{5,6},{6,7},{7,8},{8,9},{9,10},{10,1... | collective-permute-start | bytes 393224 | tf_op jit(solution)/shard_map/ppermute | solution.py:483
  151.9 12.9 %all-to-all-done.1 = f32[128,16,128]{2,1,0:T(8,128)} async-done(((f32[128,16,128]{2,1,0:T(8,128)}), f32[128,16,128]{2,1,0:T(8,128)}, u32[]{:S(2)}, u32[]{:S(2)}) %all-to-all-start.1) | async-done | bytes 1048608 | tf_op jit(solution)/shard_map/all_to_all | solution.py:447
  164.8 4.4 %combine.1 = (f32[128,64]{1,0:T(8,128)}, f32[16,64]{1,0:T(8,128)}, f32[128,128]{1,0:T(8,128)}) custom-call(s32[2,16]{1,0:T(2,128)} %top_ids.1, f32[32,128]{1,0:T(8,128)} %get-tuple-element.21.tab_ref, f32[4096,128]{1,0:T(8,128)} %bitcast.27, f32[2048,128]{1,0:T(8,128)} %bitcast.15.r2_ref, f32[3,2,64]{2,1,0:T(2,128)} %nt_ref.3), custom_call_target="tpu_custom_call" | custom-call | tf_op jit(solution)/shard_map/combine/pallas_call | solution.py:433
  169.1 1.0 slice_reduce_fusion
  170.1 0.1 reshape_squeeze.3
  170.2 0.0 copy-done.12
  170.2 0.2 multiply_reduce_fusion.4
  170.4 0.7 add.19
  171.2 0.1 copy.33
  171.2 0.0 copy-done.11
  171.2 0.2 multiply_reduce_fusion.2
  171.5 0.1 copy.34
  171.6 4.2 %multiply_reduce_fusion = f32[128,256]{1,0:T(8,128)S(1)} fusion(f32[128,64,256]{2,1,0:T(8,128)} %param.14, f32[128,64]{1,0:T(8,128)S(1)} %add.20), kind=kLoop, calls=%fused_computation | loop fusion | flops 4161536 | bytes 8552448 | tf_op jit(solution)/shard_map/reduce_sum | solution.py:496
  175.8 0.0 collective-permute-done.2
  175.8 0.0 collective-permute-done.3
  175.8 0.0 copy-done.5
  175.8 0.7 add_add_fusion
  (21 shorter events, 0.1 us)
Async XLA Ops:
  7.0 18.2 %copy-start.2 = (f32[128,256]{1,0:T(8,128)S(1)}, f32[128,256]{1,0:T(8,128)}, u32[]{:S(2)}) copy-start(f32[128,256]{1,0:T(8,128)} %q_ref.1) | copy-start | bytes 393220
  7.0 81.7 %all-to-all-start = ((f32[128,32,128]{2,1,0:T(8,128)}), f32[128,32,128]{2,1,0:T(8,128)S(1)}, u32[]{:S(2)}, u32[]{:S(2)}) async-start(f32[128,32,128]{2,1,0:T(8,128)} %get-tuple-element.22), calls=%async_computation | async-start | bytes 4194304 | tf_op jit(solution)/shard_map/all_to_all | solution.py:447
  18.5 32.4 %collective-permute-start.1 = (f32[392,256]{1,0:T(8,128)}, f32[392,256]{1,0:T(8,128)S(1)}, u32[]{:S(2)}, u32[]{:S(2)}) collective-permute-start(f32[392,256]{1,0:T(8,128)} %get-tuple-element.25), channel_id=1, source_target_pairs={{1,0},{2,1},{3,2},{4,3},{5,4},{6,5},{7,6},{8,7},{9,8},{10,9},{11,1... | collective-permute-start | bytes 1204232 | tf_op jit(solution)/shard_map/ppermute | solution.py:472
  23.3 29.2 %collective-permute-start = (f32[392,256]{1,0:T(8,128)}, f32[392,256]{1,0:T(8,128)S(1)}, u32[]{:S(2)}, u32[]{:S(2)}) collective-permute-start(f32[392,256]{1,0:T(8,128)} %get-tuple-element.24), channel_id=1, source_target_pairs={{0,1},{1,2},{2,3},{3,4},{4,5},{5,6},{6,7},{7,8},{8,9},{9,10},{10,1... | collective-permute-start | bytes 1204232 | tf_op jit(solution)/shard_map/ppermute | solution.py:473
  29.7 23.4 %copy-start.1 = (f32[3,128,256]{2,1,0:T(8,128)S(1)}, f32[3,128,256]{2,1,0:T(8,128)}, u32[]{:S(2)}) copy-start(f32[3,128,256]{2,1,0:T(8,128)} %pts_ref.1) | copy-start | bytes 1179652
  86.7 0.6 copy-start.4
  87.4 0.6 copy-start.7
  88.0 0.7 copy-start.9
  88.7 1.4 copy-start
  88.7 1.4 copy-start.3
  88.7 1.4 copy-start.6
  90.0 55.0 %copy-start.10 = (f32[128,256]{1,0:T(8,128)S(1)}, f32[128,256]{1,0:T(8,128)}, u32[]{:S(2)}) copy-start(f32[128,256]{1,0:T(8,128)} %copy-done.9) | copy-start | bytes 393220
  90.0 59.9 %copy-start.8 = (f32[128,256]{1,0:T(8,128)S(1)}, f32[128,256]{1,0:T(8,128)}, u32[]{:S(2)}) copy-start(f32[128,256]{1,0:T(8,128)} %copy-done.7) | copy-start | bytes 393220
  125.4 39.3 %all-to-all-start.1 = ((f32[128,16,128]{2,1,0:T(8,128)}), f32[128,16,128]{2,1,0:T(8,128)}, u32[]{:S(2)}, u32[]{:S(2)}) async-start(f32[128,16,128]{2,1,0:T(8,128)} %bitcast.14), calls=%async_computation.1 | async-start | bytes 2097152 | tf_op jit(solution)/shard_map/all_to_all | solution.py:447
  145.0 25.2 %copy-start.12 = (f32[16,64,64]{2,1,0:T(8,128)S(1)}, f32[16,64,64]{2,1,0:T(8,128)}, u32[]{:S(2)}) copy-start(f32[16,64,64]{2,1,0:T(8,128)} %param.16) | copy-start | bytes 786436
  145.0 26.2 %copy-start.11 = (f32[128,64,64]{0,2,1:T(8,128)S(1)}, f32[128,64,64]{0,2,1:T(8,128)}, u32[]{:S(2)}) copy-start(f32[128,64,64]{0,2,1:T(8,128)} %param.15) | copy-start | bytes 6291460
  145.1 30.7 %collective-permute-start.2 = (f32[128,256]{1,0:T(8,128)S(1)}, f32[128,256]{1,0:T(8,128)S(1)}, u32[]{:S(2)}, u32[]{:S(2)}) collective-permute-start(f32[128,256]{1,0:T(8,128)S(1)} %copy-done.10), channel_id=1, source_target_pairs={{1,0},{2,1},{3,2},{4,3},{5,4},{6,5},{7,6},{8,7},{9,8},{10,9},{11,1... | collective-permute-start | bytes 393224 | tf_op jit(solution)/shard_map/ppermute | solution.py:482
  150.0 25.8 %collective-permute-start.3 = (f32[128,256]{1,0:T(8,128)S(1)}, f32[128,256]{1,0:T(8,128)S(1)}, u32[]{:S(2)}, u32[]{:S(2)}) collective-permute-start(f32[128,256]{1,0:T(8,128)S(1)} %copy-done.8), channel_id=1, source_target_pairs={{0,1},{1,2},{2,3},{3,4},{4,5},{5,6},{6,7},{7,8},{8,9},{9,10},{10,1... | collective-permute-start | bytes 393224 | tf_op jit(solution)/shard_map/ppermute | solution.py:483
  169.1 2.4 %copy-start.13 = (f32[128,64]{1,0:T(8,128)S(1)}, f32[128,64]{1,0:T(8,128)}, u32[]{:S(2)}) copy-start(f32[128,64]{1,0:T(8,128)} %get-tuple-element.31) | copy-start | bytes 98308
  171.6 4.2 %copy-start.5 = (f32[128,256]{1,0:T(8,128)S(1)}, f32[128,256]{1,0:T(8,128)}, u32[]{:S(2)}) copy-start(f32[128,256]{1,0:T(8,128)} %copy-done.4) | copy-start | bytes 393220
where the time goes:
time: 177 us
  Pallas kernels  80.4 us (45%)
  starting transfers between devices  44.6 us (25%)
  waiting for transfers between devices  30.6 us (17%)
  other arithmetic  15.4 us (9%)
  local copies, waits for them, and re-layouts  5.32 us (3%)
    pallas_call x1, Pallas kernels, far(): pl.pallas_call(far_kernel, out_shape=jax.ShapeDtypeStruct((128 * 16, 128)...  35.4 us
    pallas_call x1, Pallas kernels, near(): pl.pallas_call(near_kernel, out_shape=tuple((jax.ShapeDtypeStruct((128, 2...  33.6 us
    all_to_all x2, starting transfers between devices, swap(): return lax.all_to_all(x, AXES, split_axis=0, concat_axis=0, tiled=True)  31.1 us
    ppermute x1, waiting for transfers between devices, local(): from_right = lax.ppermute(to_left, AXES, down_perm)  16.3 us
    all_to_all x2, waiting for transfers between devices, swap(): return lax.all_to_all(x, AXES, split_axis=0, concat_axis=0, tiled=True)  12.9 us
    pallas_call x1, Pallas kernels, plan(): pl.pallas_call(plan_kernel, out_shape=(jax.ShapeDtypeStruct((128, 32, 128...  7 us
    ppermute x1, starting transfers between devices, local(): back_l = lax.ppermute(near_l, AXES, down_perm)  4.88 us
    ppermute x1, starting transfers between devices, local(): from_right = lax.ppermute(to_left, AXES, down_perm)  4.75 us
  transfers between devices with their start and end apart: 6, of which 3 were waited for; matrix products, arithmetic and copies ran while one was open for 9% of the time, Pallas kernels for 22%

commit v1 on v0

--- a/solution.py
+++ b/solution.py
@@ -11,7 +11,7 @@
 i32 = jnp.int32
 soften = 0.25
 AXES = ("dom", "sub")
-NB = 4
+NB = 8
 TRANS = (((1,), (1,)), ((), ()))
 
 
@@ -161,8 +161,76 @@
         in_specs=[pl.BlockSpec(memory_space=pltpu.SMEM)] + [vm] * 7,
         out_specs=(vm,) * 5,
         scratch_shapes=[pltpu.VMEM((1024, 256), f32)],
+        compiler_params=pltpu.CompilerParams(vmem_limit_bytes=60 << 20),
         name="plan",
     )(me, far_t, far_mid, near_t, nodes_t, nodes_mid, nodes_top, points)
+
+
+def dot3(a, b):
+    return sum(dot(v.astype(bf16), b) for v in split3(a))
+
+
+def moments_kernel(q_ref, lb_hbm, ct_hbm, pt_ref, lm_ref, mm_ref, top_ref, lb_ref, ct_ref, sem):
+    def part(k):
+        rows = pl.ds(k * 16, 16)
+        return pltpu.make_async_copy(lb_hbm.at[rows], lb_ref.at[rows], sem.at[k])
+
+    child = pltpu.make_async_copy(ct_hbm, ct_ref, sem.at[8])
+    for k in range(8):
+        part(k).start()
+    child.start()
+    lane = iota((64, 128), 1)
+    lmt = jnp.zeros((64, 128), f32)
+    for k in range(8):
+        part(k).wait()
+
+        def leaf(it, acc):
+            for u in range(4):
+                n = k * 16 + it * 4 + u
+                prod = lb_ref[n] * q_ref[pl.ds(n, 1), :]
+                col = jnp.sum(prod[:, 0:128] + prod[:, 128:256], axis=1, keepdims=True)
+                acc = jnp.where(lane == n, col, acc)
+            return acc
+
+        lmt = lax.fori_loop(0, 4, leaf, lmt)
+    lm_ref[...] = lmt.T
+    child.wait()
+    rows = []
+    for i in range(64):
+        rows.append(jnp.sum(ct_ref[i] * lmt, axis=0, keepdims=True))
+    per_leaf = jnp.concatenate(rows, axis=0)
+    group = jnp.where((iota((128, 128), 0) >> 3) == iota((128, 128), 1), 1.0, 0.0).astype(bf16)
+    mm = dot3(per_leaf, group).T
+    mm_ref[...] = mm[0:16, :]
+    tops = []
+    for g in range(2):
+        acc = jnp.zeros((64, 64), f32)
+        for c in range(g * 8, g * 8 + 8):
+            acc = acc + pt_ref[c] * mm[c : c + 1, :]
+        tops.append(jnp.broadcast_to(jnp.sum(acc, axis=1, keepdims=True), (64, 128)).T[0:1])
+    top_ref[...] = jnp.concatenate(tops, axis=1)
+
+
+def moments(charges, leaf_basis, child, parent_transfer):
+    vm = pl.BlockSpec(memory_space=pltpu.VMEM)
+    hbm = pl.BlockSpec(memory_space=pl.ANY)
+    return pl.pallas_call(
+        moments_kernel,
+        out_shape=(
+            jax.ShapeDtypeStruct((128, 64), f32),
+            jax.ShapeDtypeStruct((16, 64), f32),
+            jax.ShapeDtypeStruct((1, 128), f32),
+        ),
+        in_specs=[vm, hbm, hbm, vm],
+        out_specs=(vm,) * 3,
+        scratch_shapes=[
+            pltpu.VMEM((128, 64, 256), f32),
+            pltpu.VMEM((64, 64, 128), f32),
+            pltpu.SemaphoreType.DMA((9,)),
+        ],
+        compiler_params=pltpu.CompilerParams(vmem_limit_bytes=60 << 20),
+        name="moments",
+    )(charges, leaf_basis, child, parent_transfer)
 
 
 def tile_rows(x, y, z, a, b):
@@ -194,55 +262,59 @@
     lax.fori_loop(0, 16, prepare, 0)
 
 
-def near_pairs(lst, base, tgt, sf_ref, qb_ref, d_refs, acc_ref):
+def near_pairs(lst, base, tgt, sf_ref, qb_ref, rhs_ref, d_ref, acc_ref):
     def entry(i):
         return lst[base + i], lst[base + 1024 + i]
 
-    def distances(i, u, ref):
-        lv, n = entry(i)
+    def factors(i, u):
+        lv, _ = entry(i)
         lrow = jnp.maximum(lv - 1, 0)
         x = tgt[pl.ds(lrow, 1), :]
         y = tgt[pl.ds(128 + lrow, 1), :]
         z = tgt[pl.ds(256 + lrow, 1), :]
         norm = x * x + y * y + z * z
         h, m, l = split3(tile_rows(-2.0 * x, -2.0 * y, -2.0 * z, norm, jnp.ones_like(x)))
-        rhs = jnp.concatenate([h, h, h, m, m, l], axis=0).astype(bf16)
-        ref[u] = dot(sf_ref[n, :, 0:48], rhs)
-
-    def sums(i, u, ref):
+        rhs_ref[u] = jnp.concatenate([h, h, h, m, m, l], axis=0).astype(bf16)
+
+    def distances(i, u):
+        _, n = entry(i)
+        d_ref[u] = dot(sf_ref[n, :, 0:48], rhs_ref[u])
+
+    def sums(i, u):
         lv, n = entry(i)
         acc = jnp.zeros((8, 256), f32)
         for j in range(0, 256, 64):
-            w = lax.rsqrt(ref[u, j : j + 64, :])
+            w = lax.rsqrt(d_ref[u, j : j + 64, :])
             q = qb_ref[n, j : j + 64, :]
             acc = acc + jnp.sum((w * jnp.concatenate([q, q], axis=1)).reshape(8, 8, 256), axis=0)
         row = jnp.where(lv > 0, lv - 1, 128)
-        acc_ref[pl.ds(row, 1), :] = acc_ref[pl.ds(row, 1), :] + jnp.sum(acc, axis=0, keepdims=True)
-
-    d0, d1 = d_refs
+        return row, jnp.sum(acc, axis=0, keepdims=True)
+
     for u in range(NB):
-        distances(u, u, d0)
+        factors(u, u)
+    for u in range(NB):
+        distances(u, u)
+        factors(NB + u, u)
 
     def step(it, carry):
-        i = it * (2 * NB)
+        i = it * NB
+        got = [sums(i + u, u) for u in range(NB)]
         for u in range(NB):
-            distances(i + NB + u, u, d1)
+            distances(i + NB + u, u)
         for u in range(NB):
-            sums(i + u, u, d0)
-        for u in range(NB):
-            distances(i + 2 * NB + u, u, d0)
-        for u in range(NB):
-            sums(i + NB + u, u, d1)
+            factors(i + 2 * NB + u, u)
+        for row, val in got:
+            acc_ref[pl.ds(row, 1), :] = acc_ref[pl.ds(row, 1), :] + val
         return carry
 
-    lax.fori_loop(0, (lst[base + 896] + 2 * NB - 1) // (2 * NB), step, 0)
-
-
-def near_kernel(lst, tgt_l, tgt_r, pts_ref, q_ref, out_own, out_l, out_r, sf_ref, qb_ref, d0_ref, d1_ref, acc_ref):
+    lax.fori_loop(0, (lst[base + 896] + NB - 1) // NB, step, 0)
+
+
+def near_kernel(lst, tgt_l, tgt_r, pts_ref, q_ref, out_own, out_l, out_r, sf_ref, qb_ref, rhs_ref, d_ref, acc_ref):
     near_tables(pts_ref, q_ref, sf_ref, qb_ref)
     for k, (tgt, out) in enumerate(((pts_ref, out_own), (tgt_l, out_l), (tgt_r, out_r))):
         acc_ref[...] = jnp.zeros((136, 256), f32)
-        near_pairs(lst, k * 2048, tgt, sf_ref, qb_ref, (d0_ref, d1_ref), acc_ref)
+        near_pairs(lst, k * 2048, tgt, sf_ref, qb_ref, rhs_ref, d_ref, acc_ref)
         out[...] = acc_ref[0:128, :]
 
 
@@ -256,11 +328,11 @@
         scratch_shapes=[
             pltpu.VMEM((128, 256, 64), bf16),
             pltpu.VMEM((128, 256, 128), f32),
-            pltpu.VMEM((NB, 256, 256), f32),
+            pltpu.VMEM((NB, 48, 256), bf16),
             pltpu.VMEM((NB, 256, 256), f32),
             pltpu.VMEM((136, 256), f32),
         ],
-        compiler_params=pltpu.CompilerParams(vmem_limit_bytes=40 << 20),
+        compiler_params=pltpu.CompilerParams(vmem_limit_bytes=60 << 20),
         name="near",
     )(lists, *arrays)
 
@@ -287,8 +359,9 @@
     for c in range(8):
         r = iota((128, 128), 0) - c * 16
         k = iota((128, 128), 1)
-        rep_ref[c] = jnp.where(r == (k >> 3), 1.0, 0.0).astype(bf16)
-        one_ref[c] = jnp.where((r >= 0) & (r < 3), 1.0, 0.0).astype(bf16)
+        lanes = slice((c % 2) * 128, (c % 2) * 128 + 128)
+        rep_ref[c // 2, :, lanes] = jnp.where(r == (k >> 3), 1.0, 0.0).astype(bf16)
+        one_ref[c // 2, :, lanes] = jnp.where((r >= 0) & (r < 3), 1.0, 0.0).astype(bf16)
         mask_ref[c] = jnp.where((iota((64, 128), 1) & 7) == c, 1.0, 0.0).astype(bf16)
     u_ref[...] = jnp.zeros((18 * 128, 64), f32)
     leaf = features(nl_ref[0].T, nl_ref[1].T, nl_ref[2].T, True)
@@ -304,16 +377,21 @@
         for f, v in enumerate(split3(src)):
             u_ref[pl.ds(blk * 128 + f, 8, stride=16), :] = v
 
-    def prepare(blk, carry):
-        rows = pl.ds(pl.multiple_of(blk * 128, 128), 128)
-        t = v_ref[rows, :].T.astype(bf16)
-        u = u_ref[rows, :].T.astype(bf16)
-        for i in range(8):
-            ra_ref[blk * 8 + i] = dot(t, rep_ref[i]).astype(bf16)
-            mb_ref[blk * 8 + i] = dot(u, one_ref[i])
+    def prepare(it, carry):
+        for blk in (it * 2, it * 2 + 1):
+            rows = pl.ds(pl.multiple_of(blk * 128, 128), 128)
+            v = v_ref[rows, :].T.astype(bf16)
+            u = u_ref[rows, :].T.astype(bf16)
+            for i in range(4):
+                both = dot(v, rep_ref[i]).astype(bf16)
+                ra_ref[blk * 8 + 2 * i] = both[:, 0:128]
+                ra_ref[blk * 8 + 2 * i + 1] = both[:, 128:256]
+                both = dot(u, one_ref[i])
+                mb_ref[blk * 8 + 2 * i] = both[:, 0:128]
+                mb_ref[blk * 8 + 2 * i + 1] = both[:, 128:256]
         return carry
 
-    lax.fori_loop(0, 18, prepare, 0)
+    lax.fori_loop(0, 9, prepare, 0)
     low = iota((128, 128), 1) < 64
     low64 = iota((64, 128), 1) < 64
 
@@ -332,26 +410,26 @@
 
     def leaf_groups(p, groups):
         rhs = weights(*(r1_ref[pl.ds(pl.multiple_of(p * 32 + 8 * c, 8), 8), :] for c in range(3)))
-        return [(p, g, group(rhs, g, ids_ref[p, g], ids_ref[p, 8 + g])) for g in groups]
-
-    out_ref[...] = jnp.zeros((128 * 16, 128), f32)
-    out_ref[pl.ds(9, 128, stride=16), :] = jnp.broadcast_to(top_ref[...], (128, 128))
+        return [(p, g, group(rhs, g, ids_ref[p * 24 + g], ids_ref[p * 24 + 8 + g])) for g in groups]
+
+    out_ref[...] = jnp.zeros((1280, 128), f32)
+    out_ref[pl.ds(9, 128, stride=10), :] = jnp.broadcast_to(top_ref[...], (128, 128))
 
     def first(it, carry):
         got = []
         for u in range(4):
             got += leaf_groups(it * 4 + u, range(4))
         for p, g, val in got:
-            out_ref[pl.ds(p * 16 + g, 1), :] = val
+            out_ref[pl.ds(p * 10 + g, 1), :] = val
         return carry
 
     lax.fori_loop(0, 32, first, 0)
 
     def second(p, carry):
-        @pl.when(ids_ref[p, 18] > 8)
+        @pl.when(ids_ref[p * 24 + 18] > 8)
         def _():
             for q, g, val in leaf_groups(p, range(4, 8)):
-                out_ref[pl.ds(q * 16 + g, 1), :] = val
+                out_ref[pl.ds(q * 10 + g, 1), :] = val
 
         return carry
 
@@ -364,9 +442,9 @@
             rhs = weights(*(r1_ref[pl.ds(b + c, 8, stride=32), :] for c in range(3)))
             for g in range(8):
                 p = (it * 2 + u) * 8 + g
-                got.append((p, group(rhs, g, 128 + ids_ref[p, 16], 128 + ids_ref[p, 17])))
+                got.append((p, group(rhs, g, 128 + ids_ref[p * 24 + 16], 128 + ids_ref[p * 24 + 17])))
         for p, val in got:
-            out_ref[pl.ds(p * 16 + 8, 1), :] = val
+            out_ref[pl.ds(p * 10 + 8, 1), :] = val
         return carry
 
     lax.fori_loop(0, 8, mids, 0)
@@ -376,71 +454,114 @@
     vm = pl.BlockSpec(memory_space=pltpu.VMEM)
     return pl.pallas_call(
         far_kernel,
-        out_shape=jax.ShapeDtypeStruct((128 * 16, 128), f32),
+        out_shape=jax.ShapeDtypeStruct((1280, 128), f32),
         in_specs=[pl.BlockSpec(memory_space=pltpu.SMEM)] + [vm] * 6,
         out_specs=vm,
         scratch_shapes=[
             pltpu.VMEM((18 * 128, 64), f32),
             pltpu.VMEM((18 * 128, 64), f32),
-            pltpu.VMEM((8, 128, 128), bf16),
-            pltpu.VMEM((8, 128, 128), bf16),
+            pltpu.VMEM((4, 128, 256), bf16),
+            pltpu.VMEM((4, 128, 256), bf16),
             pltpu.VMEM((8, 64, 128), bf16),
             pltpu.VMEM((144, 64, 128), bf16),
             pltpu.VMEM((144, 64, 128), f32),
         ],
-        compiler_params=pltpu.CompilerParams(vmem_limit_bytes=40 << 20),
+        compiler_params=pltpu.CompilerParams(vmem_limit_bytes=60 << 20),
         name="far",
     )(ids, r1, nodes_t, nodes_mid, moments, mid_moments, top_row)
 
 
-def combine_kernel(top_ids, tab_ref, r1_ref, r2_ref, nt_ref, leaf_ref, mid_ref, top_out):
-    acc = [jnp.zeros((128, 128), f32), jnp.zeros((128, 128), f32)]
+def final_kernel(
+    top_ids, tab_ref, r1_ref, r2_ref, nt_ref, pt_ref, near_ref, bl_ref, br_ref, lb_hbm, ct_hbm, out_ref, lb_ref, ct_ref, sem
+):
+    def part(k):
+        rows = pl.ds(k * 16, 16)
+        return pltpu.make_async_copy(lb_hbm.at[rows], lb_ref.at[rows], sem.at[k])
+
+    child = pltpu.make_async_copy(ct_hbm, ct_ref, sem.at[8])
+    child.start()
+    for k in range(8):
+        part(k).start()
     tag = (iota((128, 128), 0) + 1).astype(f32)
-    for g in range(8):
-        parts = [p.astype(bf16) for p in split3(r2_ref[pl.ds(g, 128, stride=16), :])]
+
+    def lines(k, rows):
+        return jnp.where(tab_ref[k : k + 1, :] == tag[0:rows], 1.0, 0.0)
+
+    def two(x):
+        return jnp.concatenate(halves(x), axis=1).astype(bf16)
+
+    acc = [jnp.zeros((128, 256), f32), jnp.zeros((128, 256), f32)]
+    for g in range(0, 8, 2):
+        vals = jnp.concatenate([two(r2_ref[pl.ds(g + k, 128, stride=10), :]) for k in range(2)], axis=0)
         for h in range(2):
-            oh = jnp.where(tab_ref[8 * h + g : 8 * h + g + 1, :] == tag, 1.0, 0.0).astype(bf16)
-            acc[h] = acc[h] + (dot(oh, parts[0]) + dot(oh, parts[1]) + dot(oh, parts[2]))
-    leaf_ref[...] = acc[0][:, 0:64] + acc[1][:, 64:128]
-    parts = [p.astype(bf16) for p in split3(r2_ref[pl.ds(8, 128, stride=16), :])]
-    res = []
-    for h in range(2):
-        oh = jnp.where(tab_ref[16 + h : 17 + h, :] == tag[0:16], 1.0, 0.0).astype(bf16)
-        res.append(dot(oh, parts[0]) + dot(oh, parts[1]) + dot(oh, parts[2]))
-    mid_ref[...] = res[0][:, 0:64] + res[1][:, 64:128]
+            oh = jnp.concatenate([lines(8 * h + g, 128), lines(8 * h + g + 1, 128)], axis=1).astype(bf16)
+            acc[h] = acc[h] + dot(oh, vals)
+    acc = [a[:, 0:128] + a[:, 128:256] for a in acc]
+    local_t = acc[0].T[0:64] + acc[1].T[64:128]
+    vals = two(r2_ref[pl.ds(8, 128, stride=10), :])
+    res = [dot(lines(16 + h, 16).astype(bf16), vals) for h in range(2)]
+    res = [a[:, 0:128] + a[:, 128:256] for a in res]
+    mid_local = res[0][:, 0:64] + res[1][:, 64:128]
     half = iota((1, 128), 1) >> 6
     pad = jnp.zeros((6, 64), f32)
     cols = [jnp.concatenate([nt_ref[c], pad], axis=0).T for c in range(3)]
+    rows = []
     for g in range(2):
         tx, ty, tz = (jnp.broadcast_to(cols[c][:, g : g + 1], (64, 128)) for c in range(3))
 
-        def entry(e, total):
-            t = top_ids[g, e]
-            p = jnp.maximum(t, 0) >> 1
-            h = jnp.where(t < 0, 2, t & 1)
-            m = jnp.where(half == h, r2_ref[pl.ds(p * 16 + 9, 1), :], 0.0)
-            dx = tx - r1_ref[pl.ds(p * 32 + 28, 1), :]
-            dy = ty - r1_ref[pl.ds(p * 32 + 29, 1), :]
-            dz = tz - r1_ref[pl.ds(p * 32 + 30, 1), :]
-            return total + lax.rsqrt(dx * dx + dy * dy + dz * dz + soften) * m
-
-        total = lax.fori_loop(0, 16, entry, jnp.zeros((64, 128), f32))
-        top_out[g * 64 : g * 64 + 64, :] = jnp.broadcast_to(jnp.sum(total, axis=1, keepdims=True), (64, 128))
-
-
-def combine(far_top, tab, r1, r2, nodes_top):
+        def entry(it, total):
+            for u in range(4):
+                t = top_ids[g, it * 4 + u]
+                p = jnp.maximum(t, 0) >> 1
+                h = jnp.where(t < 0, 2, t & 1)
+                m = jnp.where(half == h, r2_ref[pl.ds(p * 10 + 9, 1), :], 0.0)
+                dx = tx - r1_ref[pl.ds(p * 32 + 28, 1), :]
+                dy = ty - r1_ref[pl.ds(p * 32 + 29, 1), :]
+                dz = tz - r1_ref[pl.ds(p * 32 + 30, 1), :]
+                total = total + lax.rsqrt(dx * dx + dy * dy + dz * dz + soften) * m
+            return total
+
+        total = lax.fori_loop(0, 4, entry, jnp.zeros((64, 128), f32))
+        top = jnp.broadcast_to(jnp.sum(total, axis=1, keepdims=True), (64, 64))
+        for c in range(g * 8, g * 8 + 8):
+            rows.append(jnp.sum(pt_ref[c] * top, axis=0, keepdims=True))
+    mid_down = mid_local + jnp.concatenate(rows, axis=0)
+    mid_t = jnp.concatenate([mid_down, jnp.zeros((112, 64), f32)], axis=0).T
+    spread = jnp.where(iota((128, 128), 0) == (iota((128, 128), 1) >> 3), 1.0, 0.0).astype(bf16)
+    mid_t = dot3(mid_t, spread)
+    child.wait()
+    down = local_t
+    for i in range(64):
+        down = down + ct_ref[i] * mid_t[i : i + 1, :]
+    h, m = halves(down)
+    pick = jnp.where((iota((32, 2048), 0) & 15) == (iota((32, 2048), 1) >> 7), 1.0, 0.0).astype(bf16)
+    for k in range(8):
+        part(k).wait()
+        ks = slice(16 * k, 16 * k + 16)
+        cols16 = dot(jnp.concatenate([h[:, ks], m[:, ks]], axis=1).astype(bf16), pick)
+        for u in range(16):
+            d = cols16[:, u * 128 : u * 128 + 128]
+            n = 16 * k + u
+            out_ref[n : n + 1, :] = jnp.sum(lb_ref[n] * jnp.concatenate([d, d], axis=1), axis=0, keepdims=True)
+    out_ref[...] = out_ref[...] + near_ref[...] + bl_ref[...] + br_ref[...]
+
+
+def final(far_top, arrays, leaf_basis, child):
     vm = pl.BlockSpec(memory_space=pltpu.VMEM)
+    hbm = pl.BlockSpec(memory_space=pl.ANY)
     return pl.pallas_call(
-        combine_kernel,
-        out_shape=(
-            jax.ShapeDtypeStruct((128, 64), f32),
-            jax.ShapeDtypeStruct((16, 64), f32),
-            jax.ShapeDtypeStruct((128, 128), f32),
-        ),
-        in_specs=[pl.BlockSpec(memory_space=pltpu.SMEM)] + [vm] * 4,
-        out_specs=(vm,) * 3,
-        name="combine",
-    )(far_top, tab, r1, r2, nodes_top)
+        final_kernel,
+        out_shape=jax.ShapeDtypeStruct((128, 256), f32),
+        in_specs=[pl.BlockSpec(memory_space=pltpu.SMEM)] + [vm] * 8 + [hbm] * 2,
+        out_specs=vm,
+        scratch_shapes=[
+            pltpu.VMEM((128, 64, 256), f32),
+            pltpu.VMEM((64, 64, 128), f32),
+            pltpu.SemaphoreType.DMA((9,)),
+        ],
+        compiler_params=pltpu.CompilerParams(vmem_limit_bytes=60 << 20),
+        name="final",
+    )(far_top, *arrays, leaf_basis, child)
 
 
 def swap(x):
@@ -472,9 +593,8 @@
     from_right = lax.ppermute(to_left, AXES, down_perm)
     from_left = lax.ppermute(to_right, AXES, up_perm)
     r1 = swap(pay)
-    leaf_moments = jnp.sum(leaf_basis * charges[:, None, :], axis=2)
-    mid_moments = jnp.sum(child_transfer * leaf_moments[:, None, :], axis=2).reshape(16, 8, 64).sum(axis=1)
-    top_moments = jnp.sum(parent_transfer * mid_moments[:, None, :], axis=2).reshape(2, 8, 64).sum(axis=1)
+    child = jnp.transpose(child_transfer, (1, 2, 0))
+    leaf_moments, mid_moments, top_moments = moments(charges, leaf_basis, child, parent_transfer)
     lists = jnp.stack([own_list, from_left[384:392].astype(i32), from_right[384:392].astype(i32)])
     lists = jnp.transpose(lists.reshape(3, 8, 2, 128), (0, 2, 1, 3)).reshape(6144)
     flat = points.reshape(384, 256)
@@ -484,16 +604,11 @@
     r1, near_own, leaf_moments, mid_moments, top_moments = lax.optimization_barrier(
         (r1, near_own, leaf_moments, mid_moments, top_moments)
     )
-    ids = r1[:, 27, :].astype(i32)
+    ids = r1[:, 27, 0:24].astype(i32).reshape(3072)
     r1 = r1.reshape(4096, 128)
-    pay2 = far(ids, r1, nodes_t, nodes_mid, leaf_moments, mid_moments, top_moments.reshape(1, 128))
-    r2 = swap(pay2.reshape(128, 16, 128)).reshape(2048, 128)
-    back = back_l + back_r
-    leaf_local, mid_local, top_cols = combine(far_top, tab, r1, r2, nodes_top)
-    top_local = top_cols[:, 0].reshape(2, 64)
-    mid_down = mid_local + jnp.sum(parent_transfer * jnp.repeat(top_local, 8, axis=0)[:, :, None], axis=1)
-    leaf_down = leaf_local + jnp.sum(child_transfer * jnp.repeat(mid_down, 8, axis=0)[:, :, None], axis=1)
-    return jnp.sum(leaf_basis * leaf_down[:, :, None], axis=1) + near_own + back
+    pay2 = far(ids, r1, nodes_t, nodes_mid, leaf_moments, mid_moments, top_moments)
+    r2 = swap(pay2.reshape(128, 5, 2, 128)).reshape(1280, 128)
+    return final(far_top, [tab, r1, r2, nodes_top, parent_transfer, near_own, back_l, back_r], leaf_basis, child)
 
 
 def solution(mesh):

time: 177 us -> 163 us (0.921)
  other arithmetic: 15.4 us -> 0.89 us
  Pallas kernels: 80.4 us -> 87.3 us
  local copies, waits for them, and re-layouts: 5.32 us -> 2.09 us
    reduce_sum x8 -> x0, other arithmetic: 13.3 us -> none  [the longest x1 4.54 us: local(): leaf_moments = jnp.sum(leaf_basis * charges[:, None, :], axis=2)]
    all_to_all x2, waiting for transfers between devices: 12.9 us -> 2.23 us  [swap(): return lax.all_to_all(x, AXES, split_axis=0, concat_axis=0, tiled=True)]
    pallas_call x2 -> x3, Pallas kernels: 39.8 us -> 46.9 us  [the longest x1 32.5 us: far(): pl.pallas_call(far_kernel, out_shape=jax.ShapeDtypeStruct((1280, 128), f3...]
    ppermute x1, waiting for transfers between devices: 0.01 us -> 4.48 us  [local(): back_l = lax.ppermute(near_l, AXES, down_perm)]
    ppermute x1, waiting for transfers between devices: 0.01 us -> 2.46 us  [local(): back_r = lax.ppermute(near_r, AXES, up_perm)]
    ppermute x1, waiting for transfers between devices: 16.3 us -> 18.4 us  [local(): from_right = lax.ppermute(to_left, AXES, down_perm)]
  transfers between devices with their start and end apart: 6 -> 6, of which waited for: 3 -> 5; matrix products, arithmetic and copies ran while one was open for 9% -> 0% of each run, Pallas kernels for 22% -> 25%
where the time goes in v1:
time: 163 us
  Pallas kernels  87.3 us (54%)
  starting transfers between devices  43.4 us (27%)
  waiting for transfers between devices  29.1 us (18%)
  local copies, waits for them, and re-layouts  2.09 us (1%)
    pallas_call x1, Pallas kernels, near(): pl.pallas_call(near_kernel, out_shape=tuple((jax.ShapeDtypeStruct((128, 2...  33.4 us
    pallas_call x1, Pallas kernels, far(): pl.pallas_call(far_kernel, out_shape=jax.ShapeDtypeStruct((1280, 128), f3...  32.5 us
    all_to_all x2, starting transfers between devices, swap(): return lax.all_to_all(x, AXES, split_axis=0, concat_axis=0, tiled=True)  30.1 us
    ppermute x1, waiting for transfers between devices, local(): from_right = lax.ppermute(to_left, AXES, down_perm)  18.4 us
    pallas_call x1, Pallas kernels, moments(): pl.pallas_call(moments_kernel, out_shape=(jax.ShapeDtypeStruct((128, 64),...  7.29 us
    pallas_call x1, Pallas kernels, final(): pl.pallas_call(final_kernel, out_shape=jax.ShapeDtypeStruct((128, 256), f...  7.08 us
    pallas_call x1, Pallas kernels, plan(): pl.pallas_call(plan_kernel, out_shape=(jax.ShapeDtypeStruct((128, 32, 128...  7 us
    ppermute x1, starting transfers between devices, local(): from_right = lax.ppermute(to_left, AXES, down_perm)  4.75 us
  transfers between devices with their start and end apart: 6, of which 5 were waited for; matrix products, arithmetic and copies ran while one was open for 0% of the time, Pallas kernels for 25%

profile of v1, /device:TPU:1, one launch (start us, length us, event | category | flops | bytes accessed | tf_op | source)
XLA Modules:
  0.0 162.9 jit_solution(5877190463851692062)
XLA Ops:
  0.0 7.0 %plan.1 = (f32[128,32,128]{2,1,0:T(8,128)}, f32[32,128]{1,0:T(8,128)}, s32[8,256]{1,0:T(8,128)}, f32[392,256]{1,0:T(8,128)}, f32[392,256]{1,0:T(8,128)}) custom-call(s32[1]{0:T(128)} %bitcast.me_ref, s32[16,128]{1,0:T(8,128)} %bitcast.27, s32[16,16]{1,0:T(8,128)} %mid_ref.1, s32[6,128]{1,0:T(8,128)} %bitcast.29, f32[3,64,128]{2,1,0:T(8,128)} %bitcast.24, ...), custom_call_target="tpu_custom_call" | custom-call | tf_op jit(solution)/shard_map/plan/pallas_call | solution.py:152
  7.0 0.0 copy-start.8
  7.0 0.0 copy-start.7
  7.0 11.5 %all-to-all-start = ((f32[128,32,128]{2,1,0:T(8,128)}), f32[128,32,128]{2,1,0:T(8,128)S(1)}, u32[]{:S(2)}, u32[]{:S(2)}) async-start(f32[128,32,128]{2,1,0:T(8,128)} %get-tuple-element.22), calls=%async_computation | async-start | bytes 4194304 | tf_op jit(solution)/shard_map/all_to_all | solution.py:568
  18.5 0.0 copy-done.8
  18.5 4.8 %collective-permute-start.1 = (f32[392,256]{1,0:T(8,128)S(1)}, f32[392,256]{1,0:T(8,128)S(1)}, u32[]{:S(2)}, u32[]{:S(2)}) collective-permute-start(f32[392,256]{1,0:T(8,128)S(1)} %copy-done.8), channel_id=1, source_target_pairs={{1,0},{2,1},{3,2},{4,3},{5,4},{6,5},{7,6},{8,7},{9,8},{10,9},{11,1... | collective-permute-start | bytes 1204232 | tf_op jit(solution)/shard_map/ppermute | solution.py:593
  23.3 0.0 copy-done.7
  23.3 1.9 %collective-permute-start = (f32[392,256]{1,0:T(8,128)S(1)}, f32[392,256]{1,0:T(8,128)S(1)}, u32[]{:S(2)}, u32[]{:S(2)}) collective-permute-start(f32[392,256]{1,0:T(8,128)S(1)} %copy-done.7), channel_id=1, source_target_pairs={{0,1},{1,2},{2,3},{3,4},{4,5},{5,6},{6,7},{7,8},{8,9},{9,10},{10,1... | collective-permute-start | bytes 1204232 | tf_op jit(solution)/shard_map/ppermute | solution.py:594
  25.2 0.0 copy-start.6
  25.2 7.3 %moments.1 = (f32[128,64]{1,0:T(8,128)}, f32[16,64]{1,0:T(8,128)}, f32[1,128]{1,0:T(1,128)}) custom-call(f32[128,256]{1,0:T(8,128)} %q_ref.3, f32[128,64,256]{2,1,0:T(8,128)} %lb_hbm.3, f32[64,64,128]{2,1,0:T(8,128)} %bitcast.19, f32[16,64,64]{2,1,0:T(8,128)} %pt_ref.3), custom_call_target="tpu_custom_call" | custom-call | tf_op jit(solution)/shard_map/moments/pallas_call | solution.py:217
  32.5 18.4 %collective-permute-done.1.tgt_r = f32[392,256]{1,0:T(8,128)S(1)} collective-permute-done((f32[392,256]{1,0:T(8,128)S(1)}, f32[392,256]{1,0:T(8,128)S(1)}, u32[]{:S(2)}, u32[]{:S(2)}) %collective-permute-start.1) | collective-permute-done | bytes 401440 | tf_op jit(solution)/shard_map/ppermute | solution.py:593
  50.9 0.0 copy-start.2
  50.9 1.5 collective-permute-done.tgt_l
  52.4 0.0 copy-start.3
  52.4 0.0 copy-done.6
  52.4 0.7 pad_add_fusion
  53.1 0.0 copy-done.2
  53.1 0.1 copy-done.3
  53.2 33.4 %near.1 = (f32[128,256]{1,0:T(8,128)}, f32[128,256]{1,0:T(8,128)}, f32[128,256]{1,0:T(8,128)}) custom-call(s32[6144]{0:T(1024)} %bitcast.26, f32[392,256]{1,0:T(8,128)} %copy-done.3, f32[392,256]{1,0:T(8,128)} %copy-done.2, f32[384,256]{1,0:T(8,128)} %bitcast.23, f32[128,256]{1,0:T(8,128)} %q_ref.3), custom_call_target="tpu_custom_call" | custom-call | tf_op jit(solution)/shard_map/near/pallas_call | solution.py:323
  86.6 0.0 all-to-all-done
  86.6 0.0 copy-start
  86.6 0.2 convert_reduce_fusion
  86.8 1.0 convert_element_type.16.ids_ref
  87.8 0.1 copy-done
  88.0 0.0 copy-start.10
  88.0 0.0 copy-start.9
  88.0 32.5 %far.1 = f32[1280,128]{1,0:T(8,128)} custom-call(s32[3072]{0:T(1024)} %convert_element_type.16.ids_ref, f32[4096,128]{1,0:T(8,128)} %bitcast.17, f32[3,64,128]{2,1,0:T(8,128)} %bitcast.25, f32[3,16,64]{2,1,0:T(8,128)} %nm_ref.3, f32[128,64]{1,0:T(8,128)} %get-tuple-element.31.lm_ref, f32[16,64]{1,0:T(8,128)} %get-tuple-element.32.mm_ref, ...), custom_call_target="tpu_custom_call" | custom-call | tf_op jit(solution)/shard_map/far/pallas_call | solution.py:455
  120.5 18.6 %all-to-all-start.1 = ((f32[128,5,2,128]{3,2,1,0:T(2,128)}), f32[128,5,2,128]{3,2,1,0:T(2,128)S(1)}, u32[]{:S(2)}, u32[]{:S(2)}) async-start(f32[128,5,2,128]{3,2,1,0:T(2,128)} %bitcast.22), calls=%async_computation.1 | async-start | bytes 1310720 | tf_op jit(solution)/shard_map/all_to_all | solution.py:568
  139.1 0.0 copy-done.10
  139.1 4.8 %collective-permute-start.2 = (f32[128,256]{1,0:T(8,128)S(1)}, f32[128,256]{1,0:T(8,128)S(1)}, u32[]{:S(2)}, u32[]{:S(2)}) collective-permute-start(f32[128,256]{1,0:T(8,128)S(1)} %copy-done.10), channel_id=1, source_target_pairs={{1,0},{2,1},{3,2},{4,3},{5,4},{6,5},{7,6},{8,7},{9,8},{10,9},{11,1... | collective-permute-start | bytes 393224 | tf_op jit(solution)/shard_map/ppermute | solution.py:602
  143.9 0.0 copy-done.9
  143.9 1.9 %collective-permute-start.3 = (f32[128,256]{1,0:T(8,128)S(1)}, f32[128,256]{1,0:T(8,128)S(1)}, u32[]{:S(2)}, u32[]{:S(2)}) collective-permute-start(f32[128,256]{1,0:T(8,128)S(1)} %copy-done.9), channel_id=1, source_target_pairs={{0,1},{1,2},{2,3},{3,4},{4,5},{5,6},{6,7},{7,8},{8,9},{9,10},{10,1... | collective-permute-start | bytes 393224 | tf_op jit(solution)/shard_map/ppermute | solution.py:603
  145.8 4.5 %collective-permute-done.2.bl_ref = f32[128,256]{1,0:T(8,128)S(1)} collective-permute-done((f32[128,256]{1,0:T(8,128)S(1)}, f32[128,256]{1,0:T(8,128)S(1)}, u32[]{:S(2)}, u32[]{:S(2)}) %collective-permute-start.2) | collective-permute-done | bytes 131104 | tf_op jit(solution)/shard_map/ppermute | solution.py:602
  150.3 0.0 copy-start.4
  150.3 2.5 %collective-permute-done.3.br_ref = f32[128,256]{1,0:T(8,128)S(1)} collective-permute-done((f32[128,256]{1,0:T(8,128)S(1)}, f32[128,256]{1,0:T(8,128)S(1)}, u32[]{:S(2)}, u32[]{:S(2)}) %collective-permute-start.3) | collective-permute-done | bytes 131104 | tf_op jit(solution)/shard_map/ppermute | solution.py:603
  152.8 0.0 copy-start.5
  152.8 2.2 %all-to-all-done.1 = f32[128,5,2,128]{3,2,1,0:T(2,128)S(1)} async-done(((f32[128,5,2,128]{3,2,1,0:T(2,128)}), f32[128,5,2,128]{3,2,1,0:T(2,128)S(1)}, u32[]{:S(2)}, u32[]{:S(2)}) %all-to-all-start.1) | async-done | bytes 655392 | tf_op jit(solution)/shard_map/all_to_all | solution.py:568
  155.0 0.0 copy-start.1
  155.0 0.0 copy-done.4
  155.0 0.0 copy-done.5
  155.0 0.8 copy-done.1
  155.8 7.1 %final.1 = f32[128,256]{1,0:T(8,128)} custom-call(s32[2,16]{1,0:T(2,128)} %top_ids.1, f32[32,128]{1,0:T(8,128)} %get-tuple-element.21.tab_ref, f32[4096,128]{1,0:T(8,128)} %bitcast.18, f32[1280,128]{1,0:T(8,128)} %bitcast.21, f32[3,2,64]{2,1,0:T(2,128)} %nt_ref.3, f32[16,64,64]{2,1,0:T(8,128)} %pt_ref.3, f32[128,256]{1,0:T(8,128)} %get-tuple-element.34.near_ref, ...), custom_call_target="tpu_custom_call" | custom-call | tf_op jit(solution)/shard_map/final/pallas_call | solution.py:552
  (2 shorter events, 0.0 us)
Async XLA Ops:
  7.0 11.5 %copy-start.8 = (f32[392,256]{1,0:T(8,128)S(1)}, f32[392,256]{1,0:T(8,128)}, u32[]{:S(2)}) copy-start(f32[392,256]{1,0:T(8,128)} %get-tuple-element.25) | copy-start | bytes 1204228
  7.0 16.3 %copy-start.7 = (f32[392,256]{1,0:T(8,128)S(1)}, f32[392,256]{1,0:T(8,128)}, u32[]{:S(2)}) copy-start(f32[392,256]{1,0:T(8,128)} %get-tuple-element.24) | copy-start | bytes 1204228
  7.0 79.6 %all-to-all-start = ((f32[128,32,128]{2,1,0:T(8,128)}), f32[128,32,128]{2,1,0:T(8,128)S(1)}, u32[]{:S(2)}, u32[]{:S(2)}) async-start(f32[128,32,128]{2,1,0:T(8,128)} %get-tuple-element.22), calls=%async_computation | async-start | bytes 4194304 | tf_op jit(solution)/shard_map/all_to_all | solution.py:568
  18.5 32.4 %collective-permute-start.1 = (f32[392,256]{1,0:T(8,128)S(1)}, f32[392,256]{1,0:T(8,128)S(1)}, u32[]{:S(2)}, u32[]{:S(2)}) collective-permute-start(f32[392,256]{1,0:T(8,128)S(1)} %copy-done.8), channel_id=1, source_target_pairs={{1,0},{2,1},{3,2},{4,3},{5,4},{6,5},{7,6},{8,7},{9,8},{10,9},{11,1... | collective-permute-start | bytes 1204232 | tf_op jit(solution)/shard_map/ppermute | solution.py:593
  23.3 29.1 %collective-permute-start = (f32[392,256]{1,0:T(8,128)S(1)}, f32[392,256]{1,0:T(8,128)S(1)}, u32[]{:S(2)}, u32[]{:S(2)}) collective-permute-start(f32[392,256]{1,0:T(8,128)S(1)} %copy-done.7), channel_id=1, source_target_pairs={{0,1},{1,2},{2,3},{3,4},{4,5},{5,6},{6,7},{7,8},{8,9},{9,10},{10,1... | collective-permute-start | bytes 1204232 | tf_op jit(solution)/shard_map/ppermute | solution.py:594
  25.2 27.2 %copy-start.6 = (s32[8,256]{1,0:T(8,128)S(1)}, s32[8,256]{1,0:T(8,128)}, u32[]{:S(2)}) copy-start(s32[8,256]{1,0:T(8,128)} %get-tuple-element.23) | copy-start | bytes 24580
  50.9 2.2 %copy-start.2 = (f32[392,256]{1,0:T(8,128)}, f32[392,256]{1,0:T(8,128)S(1)}, u32[]{:S(2)}) copy-start(f32[392,256]{1,0:T(8,128)S(1)} %collective-permute-done.1.tgt_r) | copy-start | bytes 1204228
  52.4 0.8 copy-start.3
  86.6 1.4 copy-start
  88.0 51.1 %copy-start.10 = (f32[128,256]{1,0:T(8,128)S(1)}, f32[128,256]{1,0:T(8,128)}, u32[]{:S(2)}) copy-start(f32[128,256]{1,0:T(8,128)} %get-tuple-element.35) | copy-start | bytes 393220
  88.0 55.9 %copy-start.9 = (f32[128,256]{1,0:T(8,128)S(1)}, f32[128,256]{1,0:T(8,128)}, u32[]{:S(2)}) copy-start(f32[128,256]{1,0:T(8,128)} %get-tuple-element.36) | copy-start | bytes 393220
  120.5 34.5 %all-to-all-start.1 = ((f32[128,5,2,128]{3,2,1,0:T(2,128)}), f32[128,5,2,128]{3,2,1,0:T(2,128)S(1)}, u32[]{:S(2)}, u32[]{:S(2)}) async-start(f32[128,5,2,128]{3,2,1,0:T(2,128)} %bitcast.22), calls=%async_computation.1 | async-start | bytes 1310720 | tf_op jit(solution)/shard_map/all_to_all | solution.py:568
  139.1 11.2 %collective-permute-start.2 = (f32[128,256]{1,0:T(8,128)S(1)}, f32[128,256]{1,0:T(8,128)S(1)}, u32[]{:S(2)}, u32[]{:S(2)}) collective-permute-start(f32[128,256]{1,0:T(8,128)S(1)} %copy-done.10), channel_id=1, source_target_pairs={{1,0},{2,1},{3,2},{4,3},{5,4},{6,5},{7,6},{8,7},{9,8},{10,9},{11,1... | collective-permute-start | bytes 393224 | tf_op jit(solution)/shard_map/ppermute | solution.py:602
  143.9 8.9 %collective-permute-start.3 = (f32[128,256]{1,0:T(8,128)S(1)}, f32[128,256]{1,0:T(8,128)S(1)}, u32[]{:S(2)}, u32[]{:S(2)}) collective-permute-start(f32[128,256]{1,0:T(8,128)S(1)} %copy-done.9), channel_id=1, source_target_pairs={{0,1},{1,2},{2,3},{3,4},{4,5},{5,6},{6,7},{7,8},{8,9},{9,10},{10,1... | collective-permute-start | bytes 393224 | tf_op jit(solution)/shard_map/ppermute | solution.py:603
  150.3 4.7 %copy-start.4 = (f32[128,256]{1,0:T(8,128)}, f32[128,256]{1,0:T(8,128)S(1)}, u32[]{:S(2)}) copy-start(f32[128,256]{1,0:T(8,128)S(1)} %collective-permute-done.2.bl_ref) | copy-start | bytes 393220
  152.8 2.2 %copy-start.5 = (f32[128,256]{1,0:T(8,128)}, f32[128,256]{1,0:T(8,128)S(1)}, u32[]{:S(2)}) copy-start(f32[128,256]{1,0:T(8,128)S(1)} %collective-permute-done.3.br_ref) | copy-start | bytes 393220
  155.0 0.8 copy-start.1

commit v2 on v1

--- a/solution.py
+++ b/solution.py
@@ -354,7 +354,7 @@
 
 
 def far_kernel(
-    ids_ref, r1_ref, nl_ref, nm_ref, lm_ref, mm_ref, top_ref, out_ref, v_ref, u_ref, rep_ref, one_ref, mask_ref, ra_ref, mb_ref
+    ids_ref, r1_ref, nl_ref, nm_ref, lm_ref, mm_ref, top_ref, out_ref, v_ref, u_ref, rep_ref, one_ref, mask_ref, ra_ref, mb_ref, full_ref
 ):
     for c in range(8):
         r = iota((128, 128), 0) - c * 16
@@ -378,7 +378,7 @@
             u_ref[pl.ds(blk * 128 + f, 8, stride=16), :] = v
 
     def prepare(it, carry):
-        for blk in (it * 2, it * 2 + 1):
+        for blk in (it * 3, it * 3 + 1, it * 3 + 2):
             rows = pl.ds(pl.multiple_of(blk * 128, 128), 128)
             v = v_ref[rows, :].T.astype(bf16)
             u = u_ref[rows, :].T.astype(bf16)
@@ -391,7 +391,7 @@
                 mb_ref[blk * 8 + 2 * i + 1] = both[:, 128:256]
         return carry
 
-    lax.fori_loop(0, 9, prepare, 0)
+    lax.fori_loop(0, 6, prepare, 0)
     low = iota((128, 128), 1) < 64
     low64 = iota((64, 128), 1) < 64
 
@@ -425,15 +425,25 @@
 
     lax.fori_loop(0, 32, first, 0)
 
-    def second(p, carry):
-        @pl.when(ids_ref[p * 24 + 18] > 8)
-        def _():
-            for q, g, val in leaf_groups(p, range(4, 8)):
-                out_ref[pl.ds(q * 10 + g, 1), :] = val
-
+    def scan(it, pos):
+        for u in range(8):
+            p = it * 8 + u
+            full_ref[pos] = p
+            pos = pos + (ids_ref[p * 24 + 18] > 8).astype(i32)
+        return pos
+
+    full = lax.fori_loop(0, 16, scan, jnp.int32(0))
+    full_ref[full] = 0
+
+    def second(it, carry):
+        got = []
+        for u in range(2):
+            got += leaf_groups(full_ref[it * 2 + u], range(4, 8))
+        for p, g, val in got:
+            out_ref[pl.ds(p * 10 + g, 1), :] = val
         return carry
 
-    lax.fori_loop(0, 128, second, 0)
+    lax.fori_loop(0, (full + 1) // 2, second, 0)
 
     def mids(it, carry):
         got = []
@@ -465,6 +475,7 @@
             pltpu.VMEM((8, 64, 128), bf16),
             pltpu.VMEM((144, 64, 128), bf16),
             pltpu.VMEM((144, 64, 128), f32),
+            pltpu.SMEM((136,), i32),
         ],
         compiler_params=pltpu.CompilerParams(vmem_limit_bytes=60 << 20),
         name="far",

time: 163 us -> 157 us (0.963)
  Pallas kernels: 87.3 us -> 81.5 us
    pallas_call x1, Pallas kernels: 32.5 us -> 26.7 us  [far(): pl.pallas_call(far_kernel, out_shape=jax.ShapeDtypeStruct((1280, 128), f3...]
  transfers between devices with their start and end apart: 6 -> 6, of which waited for: 5 -> 5; matrix products, arithmetic and copies ran while one was open for 0% -> 0% of each run, Pallas kernels for 25% -> 26%
where the time goes in v2:
time: 157 us
  Pallas kernels  81.5 us (52%)
  starting transfers between devices  43 us (27%)
  waiting for transfers between devices  29.1 us (19%)
  local copies, waits for them, and re-layouts  2.09 us (1%)
    pallas_call x1, Pallas kernels, near(): pl.pallas_call(near_kernel, out_shape=tuple((jax.ShapeDtypeStruct((128, 2...  33.4 us
    all_to_all x2, starting transfers between devices, swap(): return lax.all_to_all(x, AXES, split_axis=0, concat_axis=0, tiled=True)  29.7 us
    pallas_call x1, Pallas kernels, far(): pl.pallas_call(far_kernel, out_shape=jax.ShapeDtypeStruct((1280, 128), f3...  26.7 us
    ppermute x1, waiting for transfers between devices, local(): from_right = lax.ppermute(to_left, AXES, down_perm)  18.4 us
    pallas_call x1, Pallas kernels, moments(): pl.pallas_call(moments_kernel, out_shape=(jax.ShapeDtypeStruct((128, 64),...  7.29 us
    pallas_call x1, Pallas kernels, final(): pl.pallas_call(final_kernel, out_shape=jax.ShapeDtypeStruct((128, 256), f...  7.08 us
    pallas_call x1, Pallas kernels, plan(): pl.pallas_call(plan_kernel, out_shape=(jax.ShapeDtypeStruct((128, 32, 128...  7 us
    ppermute x1, starting transfers between devices, local(): from_right = lax.ppermute(to_left, AXES, down_perm)  4.75 us
  transfers between devices with their start and end apart: 6, of which 5 were waited for; matrix products, arithmetic and copies ran while one was open for 0% of the time, Pallas kernels for 26%

profile of v2, /device:TPU:1, one launch (start us, length us, event | category | flops | bytes accessed | tf_op | source)
XLA Modules:
  0.0 156.7 jit_solution(15583265170699751445)
XLA Ops:
  0.0 7.0 %plan.1 = (f32[128,32,128]{2,1,0:T(8,128)}, f32[32,128]{1,0:T(8,128)}, s32[8,256]{1,0:T(8,128)}, f32[392,256]{1,0:T(8,128)}, f32[392,256]{1,0:T(8,128)}) custom-call(s32[1]{0:T(128)} %bitcast.me_ref, s32[16,128]{1,0:T(8,128)} %bitcast.27, s32[16,16]{1,0:T(8,128)} %mid_ref.1, s32[6,128]{1,0:T(8,128)} %bitcast.29, f32[3,64,128]{2,1,0:T(8,128)} %bitcast.24, ...), custom_call_target="tpu_custom_call" | custom-call | tf_op jit(solution)/shard_map/plan/pallas_call | solution.py:152
  7.0 0.0 copy-start.8
  7.0 0.0 copy-start.7
  7.0 11.5 %all-to-all-start = ((f32[128,32,128]{2,1,0:T(8,128)}), f32[128,32,128]{2,1,0:T(8,128)S(1)}, u32[]{:S(2)}, u32[]{:S(2)}) async-start(f32[128,32,128]{2,1,0:T(8,128)} %get-tuple-element.22), calls=%async_computation | async-start | bytes 4194304 | tf_op jit(solution)/shard_map/all_to_all | solution.py:579
  18.5 0.0 copy-done.8
  18.5 4.8 %collective-permute-start.1 = (f32[392,256]{1,0:T(8,128)S(1)}, f32[392,256]{1,0:T(8,128)S(1)}, u32[]{:S(2)}, u32[]{:S(2)}) collective-permute-start(f32[392,256]{1,0:T(8,128)S(1)} %copy-done.8), channel_id=1, source_target_pairs={{1,0},{2,1},{3,2},{4,3},{5,4},{6,5},{7,6},{8,7},{9,8},{10,9},{11,1... | collective-permute-start | bytes 1204232 | tf_op jit(solution)/shard_map/ppermute | solution.py:604
  23.3 0.0 copy-done.7
  23.3 1.9 %collective-permute-start = (f32[392,256]{1,0:T(8,128)S(1)}, f32[392,256]{1,0:T(8,128)S(1)}, u32[]{:S(2)}, u32[]{:S(2)}) collective-permute-start(f32[392,256]{1,0:T(8,128)S(1)} %copy-done.7), channel_id=1, source_target_pairs={{0,1},{1,2},{2,3},{3,4},{4,5},{5,6},{6,7},{7,8},{8,9},{9,10},{10,1... | collective-permute-start | bytes 1204232 | tf_op jit(solution)/shard_map/ppermute | solution.py:605
  25.2 0.0 copy-start.6
  25.2 7.3 %moments.1 = (f32[128,64]{1,0:T(8,128)}, f32[16,64]{1,0:T(8,128)}, f32[1,128]{1,0:T(1,128)}) custom-call(f32[128,256]{1,0:T(8,128)} %q_ref.3, f32[128,64,256]{2,1,0:T(8,128)} %lb_hbm.3, f32[64,64,128]{2,1,0:T(8,128)} %bitcast.19, f32[16,64,64]{2,1,0:T(8,128)} %pt_ref.3), custom_call_target="tpu_custom_call" | custom-call | tf_op jit(solution)/shard_map/moments/pallas_call | solution.py:217
  32.5 18.4 %collective-permute-done.1.tgt_r = f32[392,256]{1,0:T(8,128)S(1)} collective-permute-done((f32[392,256]{1,0:T(8,128)S(1)}, f32[392,256]{1,0:T(8,128)S(1)}, u32[]{:S(2)}, u32[]{:S(2)}) %collective-permute-start.1) | collective-permute-done | bytes 401440 | tf_op jit(solution)/shard_map/ppermute | solution.py:604
  50.9 0.0 copy-start.2
  50.9 1.5 collective-permute-done.tgt_l
  52.4 0.0 copy-start.3
  52.4 0.0 copy-done.6
  52.4 0.7 pad_add_fusion
  53.1 0.0 copy-done.2
  53.1 0.1 copy-done.3
  53.2 33.4 %near.1 = (f32[128,256]{1,0:T(8,128)}, f32[128,256]{1,0:T(8,128)}, f32[128,256]{1,0:T(8,128)}) custom-call(s32[6144]{0:T(1024)} %bitcast.26, f32[392,256]{1,0:T(8,128)} %copy-done.3, f32[392,256]{1,0:T(8,128)} %copy-done.2, f32[384,256]{1,0:T(8,128)} %bitcast.23, f32[128,256]{1,0:T(8,128)} %q_ref.3), custom_call_target="tpu_custom_call" | custom-call | tf_op jit(solution)/shard_map/near/pallas_call | solution.py:323
  86.6 0.0 all-to-all-done
  86.6 0.0 copy-start
  86.6 0.2 convert_reduce_fusion
  86.8 1.0 convert_element_type.16.ids_ref
  87.8 0.1 copy-done
  88.0 0.0 copy-start.10
  88.0 0.0 copy-start.9
  88.0 26.7 %far.1 = f32[1280,128]{1,0:T(8,128)} custom-call(s32[3072]{0:T(1024)} %convert_element_type.16.ids_ref, f32[4096,128]{1,0:T(8,128)} %bitcast.17, f32[3,64,128]{2,1,0:T(8,128)} %bitcast.25, f32[3,16,64]{2,1,0:T(8,128)} %nm_ref.3, f32[128,64]{1,0:T(8,128)} %get-tuple-element.31.lm_ref, f32[16,64]{1,0:T(8,128)} %get-tuple-element.32.mm_ref, ...), custom_call_target="tpu_custom_call" | custom-call | tf_op jit(solution)/shard_map/far/pallas_call | solution.py:465
  114.6 18.2 %all-to-all-start.1 = ((f32[128,5,2,128]{3,2,1,0:T(2,128)}), f32[128,5,2,128]{3,2,1,0:T(2,128)S(1)}, u32[]{:S(2)}, u32[]{:S(2)}) async-start(f32[128,5,2,128]{3,2,1,0:T(2,128)} %bitcast.22), calls=%async_computation.1 | async-start | bytes 1310720 | tf_op jit(solution)/shard_map/all_to_all | solution.py:579
  132.9 0.0 copy-done.10
  132.9 4.8 %collective-permute-start.2 = (f32[128,256]{1,0:T(8,128)S(1)}, f32[128,256]{1,0:T(8,128)S(1)}, u32[]{:S(2)}, u32[]{:S(2)}) collective-permute-start(f32[128,256]{1,0:T(8,128)S(1)} %copy-done.10), channel_id=1, source_target_pairs={{1,0},{2,1},{3,2},{4,3},{5,4},{6,5},{7,6},{8,7},{9,8},{10,9},{11,1... | collective-permute-start | bytes 393224 | tf_op jit(solution)/shard_map/ppermute | solution.py:613
  137.6 0.0 copy-done.9
  137.6 1.9 %collective-permute-start.3 = (f32[128,256]{1,0:T(8,128)S(1)}, f32[128,256]{1,0:T(8,128)S(1)}, u32[]{:S(2)}, u32[]{:S(2)}) collective-permute-start(f32[128,256]{1,0:T(8,128)S(1)} %copy-done.9), channel_id=1, source_target_pairs={{0,1},{1,2},{2,3},{3,4},{4,5},{5,6},{6,7},{7,8},{8,9},{9,10},{10,1... | collective-permute-start | bytes 393224 | tf_op jit(solution)/shard_map/ppermute | solution.py:614
  139.6 4.5 %collective-permute-done.2.bl_ref = f32[128,256]{1,0:T(8,128)S(1)} collective-permute-done((f32[128,256]{1,0:T(8,128)S(1)}, f32[128,256]{1,0:T(8,128)S(1)}, u32[]{:S(2)}, u32[]{:S(2)}) %collective-permute-start.2) | collective-permute-done | bytes 131104 | tf_op jit(solution)/shard_map/ppermute | solution.py:613
  144.1 0.0 copy-start.4
  144.1 2.5 %collective-permute-done.3.br_ref = f32[128,256]{1,0:T(8,128)S(1)} collective-permute-done((f32[128,256]{1,0:T(8,128)S(1)}, f32[128,256]{1,0:T(8,128)S(1)}, u32[]{:S(2)}, u32[]{:S(2)}) %collective-permute-start.3) | collective-permute-done | bytes 131104 | tf_op jit(solution)/shard_map/ppermute | solution.py:614
  146.5 0.0 copy-start.5
  146.5 2.2 %all-to-all-done.1 = f32[128,5,2,128]{3,2,1,0:T(2,128)S(1)} async-done(((f32[128,5,2,128]{3,2,1,0:T(2,128)}), f32[128,5,2,128]{3,2,1,0:T(2,128)S(1)}, u32[]{:S(2)}, u32[]{:S(2)}) %all-to-all-start.1) | async-done | bytes 655392 | tf_op jit(solution)/shard_map/all_to_all | solution.py:579
  148.7 0.0 copy-start.1
  148.7 0.0 copy-done.4
  148.7 0.0 copy-done.5
  148.8 0.8 copy-done.1
  149.6 7.1 %final.1 = f32[128,256]{1,0:T(8,128)} custom-call(s32[2,16]{1,0:T(2,128)} %top_ids.1, f32[32,128]{1,0:T(8,128)} %get-tuple-element.21.tab_ref, f32[4096,128]{1,0:T(8,128)} %bitcast.18, f32[1280,128]{1,0:T(8,128)} %bitcast.21, f32[3,2,64]{2,1,0:T(2,128)} %nt_ref.3, f32[16,64,64]{2,1,0:T(8,128)} %pt_ref.3, f32[128,256]{1,0:T(8,128)} %get-tuple-element.34.near_ref, ...), custom_call_target="tpu_custom_call" | custom-call | tf_op jit(solution)/shard_map/final/pallas_call | solution.py:563
  (2 shorter events, 0.0 us)
Async XLA Ops:
  7.0 11.5 %copy-start.8 = (f32[392,256]{1,0:T(8,128)S(1)}, f32[392,256]{1,0:T(8,128)}, u32[]{:S(2)}) copy-start(f32[392,256]{1,0:T(8,128)} %get-tuple-element.25) | copy-start | bytes 1204228
  7.0 16.3 %copy-start.7 = (f32[392,256]{1,0:T(8,128)S(1)}, f32[392,256]{1,0:T(8,128)}, u32[]{:S(2)}) copy-start(f32[392,256]{1,0:T(8,128)} %get-tuple-element.24) | copy-start | bytes 1204228
  7.0 79.6 %all-to-all-start = ((f32[128,32,128]{2,1,0:T(8,128)}), f32[128,32,128]{2,1,0:T(8,128)S(1)}, u32[]{:S(2)}, u32[]{:S(2)}) async-start(f32[128,32,128]{2,1,0:T(8,128)} %get-tuple-element.22), calls=%async_computation | async-start | bytes 4194304 | tf_op jit(solution)/shard_map/all_to_all | solution.py:579
  18.5 32.4 %collective-permute-start.1 = (f32[392,256]{1,0:T(8,128)S(1)}, f32[392,256]{1,0:T(8,128)S(1)}, u32[]{:S(2)}, u32[]{:S(2)}) collective-permute-start(f32[392,256]{1,0:T(8,128)S(1)} %copy-done.8), channel_id=1, source_target_pairs={{1,0},{2,1},{3,2},{4,3},{5,4},{6,5},{7,6},{8,7},{9,8},{10,9},{11,1... | collective-permute-start | bytes 1204232 | tf_op jit(solution)/shard_map/ppermute | solution.py:604
  23.3 29.1 %collective-permute-start = (f32[392,256]{1,0:T(8,128)S(1)}, f32[392,256]{1,0:T(8,128)S(1)}, u32[]{:S(2)}, u32[]{:S(2)}) collective-permute-start(f32[392,256]{1,0:T(8,128)S(1)} %copy-done.7), channel_id=1, source_target_pairs={{0,1},{1,2},{2,3},{3,4},{4,5},{5,6},{6,7},{7,8},{8,9},{9,10},{10,1... | collective-permute-start | bytes 1204232 | tf_op jit(solution)/shard_map/ppermute | solution.py:605
  25.2 27.2 %copy-start.6 = (s32[8,256]{1,0:T(8,128)S(1)}, s32[8,256]{1,0:T(8,128)}, u32[]{:S(2)}) copy-start(s32[8,256]{1,0:T(8,128)} %get-tuple-element.23) | copy-start | bytes 24580
  50.9 2.2 %copy-start.2 = (f32[392,256]{1,0:T(8,128)}, f32[392,256]{1,0:T(8,128)S(1)}, u32[]{:S(2)}) copy-start(f32[392,256]{1,0:T(8,128)S(1)} %collective-permute-done.1.tgt_r) | copy-start | bytes 1204228
  52.4 0.8 copy-start.3
  86.6 1.4 copy-start
  88.0 44.9 %copy-start.10 = (f32[128,256]{1,0:T(8,128)S(1)}, f32[128,256]{1,0:T(8,128)}, u32[]{:S(2)}) copy-start(f32[128,256]{1,0:T(8,128)} %get-tuple-element.35) | copy-start | bytes 393220
  88.0 49.7 %copy-start.9 = (f32[128,256]{1,0:T(8,128)S(1)}, f32[128,256]{1,0:T(8,128)}, u32[]{:S(2)}) copy-start(f32[128,256]{1,0:T(8,128)} %get-tuple-element.36) | copy-start | bytes 393220
  114.6 34.1 %all-to-all-start.1 = ((f32[128,5,2,128]{3,2,1,0:T(2,128)}), f32[128,5,2,128]{3,2,1,0:T(2,128)S(1)}, u32[]{:S(2)}, u32[]{:S(2)}) async-start(f32[128,5,2,128]{3,2,1,0:T(2,128)} %bitcast.22), calls=%async_computation.1 | async-start | bytes 1310720 | tf_op jit(solution)/shard_map/all_to_all | solution.py:579
  132.9 11.2 %collective-permute-start.2 = (f32[128,256]{1,0:T(8,128)S(1)}, f32[128,256]{1,0:T(8,128)S(1)}, u32[]{:S(2)}, u32[]{:S(2)}) collective-permute-start(f32[128,256]{1,0:T(8,128)S(1)} %copy-done.10), channel_id=1, source_target_pairs={{1,0},{2,1},{3,2},{4,3},{5,4},{6,5},{7,6},{8,7},{9,8},{10,9},{11,1... | collective-permute-start | bytes 393224 | tf_op jit(solution)/shard_map/ppermute | solution.py:613
  137.6 8.9 %collective-permute-start.3 = (f32[128,256]{1,0:T(8,128)S(1)}, f32[128,256]{1,0:T(8,128)S(1)}, u32[]{:S(2)}, u32[]{:S(2)}) collective-permute-start(f32[128,256]{1,0:T(8,128)S(1)} %copy-done.9), channel_id=1, source_target_pairs={{0,1},{1,2},{2,3},{3,4},{4,5},{5,6},{6,7},{7,8},{8,9},{9,10},{10,1... | collective-permute-start | bytes 393224 | tf_op jit(solution)/shard_map/ppermute | solution.py:614
  144.1 4.7 %copy-start.4 = (f32[128,256]{1,0:T(8,128)}, f32[128,256]{1,0:T(8,128)S(1)}, u32[]{:S(2)}) copy-start(f32[128,256]{1,0:T(8,128)S(1)} %collective-permute-done.2.bl_ref) | copy-start | bytes 393220
  146.5 2.2 %copy-start.5 = (f32[128,256]{1,0:T(8,128)}, f32[128,256]{1,0:T(8,128)S(1)}, u32[]{:S(2)}) copy-start(f32[128,256]{1,0:T(8,128)S(1)} %collective-permute-done.3.br_ref) | copy-start | bytes 393220
  148.7 0.8 copy-start.1

commit v3 on v2

--- a/solution.py
+++ b/solution.py
@@ -170,15 +170,7 @@
     return sum(dot(v.astype(bf16), b) for v in split3(a))
 
 
-def moments_kernel(q_ref, lb_hbm, ct_hbm, pt_ref, lm_ref, mm_ref, top_ref, lb_ref, ct_ref, sem):
-    def part(k):
-        rows = pl.ds(k * 16, 16)
-        return pltpu.make_async_copy(lb_hbm.at[rows], lb_ref.at[rows], sem.at[k])
-
-    child = pltpu.make_async_copy(ct_hbm, ct_ref, sem.at[8])
-    for k in range(8):
-        part(k).start()
-    child.start()
+def moments_tail(part, child, q_ref, pt_ref, lm_ref, mm_ref, top_ref, lb_ref, ct_ref):
     lane = iota((64, 128), 1)
     lmt = jnp.zeros((64, 128), f32)
     for k in range(8):
@@ -211,28 +203,6 @@
     top_ref[...] = jnp.concatenate(tops, axis=1)
 
 
-def moments(charges, leaf_basis, child, parent_transfer):
-    vm = pl.BlockSpec(memory_space=pltpu.VMEM)
-    hbm = pl.BlockSpec(memory_space=pl.ANY)
-    return pl.pallas_call(
-        moments_kernel,
-        out_shape=(
-            jax.ShapeDtypeStruct((128, 64), f32),
-            jax.ShapeDtypeStruct((16, 64), f32),
-            jax.ShapeDtypeStruct((1, 128), f32),
-        ),
-        in_specs=[vm, hbm, hbm, vm],
-        out_specs=(vm,) * 3,
-        scratch_shapes=[
-            pltpu.VMEM((128, 64, 256), f32),
-            pltpu.VMEM((64, 64, 128), f32),
-            pltpu.SemaphoreType.DMA((9,)),
-        ],
-        compiler_params=pltpu.CompilerParams(vmem_limit_bytes=60 << 20),
-        name="moments",
-    )(charges, leaf_basis, child, parent_transfer)
-
-
 def tile_rows(x, y, z, a, b):
     r = iota((8, 256), 0)
     v = jnp.where(r == 0, x, jnp.where(r == 1, y, jnp.where(r == 2, z, jnp.where(r == 3, a, b))))
@@ -262,10 +232,7 @@
     lax.fori_loop(0, 16, prepare, 0)
 
 
-def near_pairs(lst, base, tgt, sf_ref, qb_ref, rhs_ref, d_ref, acc_ref):
-    def entry(i):
-        return lst[base + i], lst[base + 1024 + i]
-
+def near_pairs(entry, total, tgt, sf_ref, qb_ref, rhs_ref, d_ref, acc_ref):
     def factors(i, u):
         lv, _ = entry(i)
         lrow = jnp.maximum(lv - 1, 0)
@@ -307,24 +274,83 @@
             acc_ref[pl.ds(row, 1), :] = acc_ref[pl.ds(row, 1), :] + val
         return carry
 
-    lax.fori_loop(0, (lst[base + 896] + NB - 1) // NB, step, 0)
-
-
-def near_kernel(lst, tgt_l, tgt_r, pts_ref, q_ref, out_own, out_l, out_r, sf_ref, qb_ref, rhs_ref, d_ref, acc_ref):
+    lax.fori_loop(0, (total + NB - 1) // NB, step, 0)
+
+
+def near_kernel(
+    lst, tgt_l, tgt_r, pts_ref, q_ref, pt_ref, lb_hbm, ct_hbm,
+    out_own, out_l, out_r, lm_ref, mm_ref, top_ref,
+    sf_ref, qb_ref, rhs_ref, d_ref, acc_ref, lb_ref, ct_ref, sem,
+):
+    def part(k):
+        rows = pl.ds(k * 16, 16)
+        return pltpu.make_async_copy(lb_hbm.at[rows], lb_ref.at[rows], sem.at[k])
+
+    child = pltpu.make_async_copy(ct_hbm, ct_ref, sem.at[8])
+    for k in range(8):
+        part(k).start()
+    child.start()
     near_tables(pts_ref, q_ref, sf_ref, qb_ref)
     for k, (tgt, out) in enumerate(((pts_ref, out_own), (tgt_l, out_l), (tgt_r, out_r))):
         acc_ref[...] = jnp.zeros((136, 256), f32)
-        near_pairs(lst, k * 2048, tgt, sf_ref, qb_ref, rhs_ref, d_ref, acc_ref)
+        skip = 128 if k == 0 else 0
+
+        def entry(i, first=k * 2048 + skip):
+            return lst[first + i], lst[first + 1024 + i]
+
+        near_pairs(entry, lst[k * 2048 + 896] - skip, tgt, sf_ref, qb_ref, rhs_ref, d_ref, acc_ref)
         out[...] = acc_ref[0:128, :]
-
-
-def near(lists, arrays):
+    moments_tail(part, child, q_ref, pt_ref, lm_ref, mm_ref, top_ref, lb_ref, ct_ref)
+
+
+def near(lists, arrays, leaf_basis, child):
+    vm = pl.BlockSpec(memory_space=pltpu.VMEM)
+    hbm = pl.BlockSpec(memory_space=pl.ANY)
+    return pl.pallas_call(
+        near_kernel,
+        out_shape=tuple(jax.ShapeDtypeStruct((128, 256), f32) for _ in range(3))
+        + (
+            jax.ShapeDtypeStruct((128, 64), f32),
+            jax.ShapeDtypeStruct((16, 64), f32),
+            jax.ShapeDtypeStruct((1, 128), f32),
+        ),
+        in_specs=[pl.BlockSpec(memory_space=pltpu.SMEM)] + [vm] * 5 + [hbm] * 2,
+        out_specs=(vm,) * 6,
+        scratch_shapes=[
+            pltpu.VMEM((128, 256, 64), bf16),
+            pltpu.VMEM((128, 256, 128), f32),
+            pltpu.VMEM((NB, 48, 256), bf16),
+            pltpu.VMEM((NB, 256, 256), f32),
+            pltpu.VMEM((136, 256), f32),
+            pltpu.VMEM((128, 64, 256), f32),
+            pltpu.VMEM((64, 64, 128), f32),
+            pltpu.SemaphoreType.DMA((9,)),
+        ],
+        compiler_params=pltpu.CompilerParams(vmem_limit_bytes=60 << 20),
+        name="near",
+    )(lists, *arrays, leaf_basis, child)
+
+
+def near_self_kernel(pts_ref, q_ref, part_ref, out, sf_ref, qb_ref, rhs_ref, d_ref, acc_ref):
+    near_tables(pts_ref, q_ref, sf_ref, qb_ref)
+    acc_ref[0:128, :] = part_ref[...]
+    acc_ref[128:136, :] = jnp.zeros((8, 256), f32)
+
+    def entry(i):
+        n = jnp.minimum(i, 127)
+        return n + 1, n
+
+    near_pairs(entry, 128, pts_ref, sf_ref, qb_ref, rhs_ref, d_ref, acc_ref)
+    out[...] = acc_ref[0:128, :]
+
+
+def near_self(points, charges, part):
     vm = pl.BlockSpec(memory_space=pltpu.VMEM)
     return pl.pallas_call(
-        near_kernel,
-        out_shape=tuple(jax.ShapeDtypeStruct((128, 256), f32) for _ in range(3)),
-        in_specs=[pl.BlockSpec(memory_space=pltpu.SMEM)] + [vm] * 4,
-        out_specs=(vm,) * 3,
+        near_self_kernel,
+        out_shape=jax.ShapeDtypeStruct((128, 256), f32),
+        in_specs=[vm] * 3,
+        out_specs=vm,
         scratch_shapes=[
             pltpu.VMEM((128, 256, 64), bf16),
             pltpu.VMEM((128, 256, 128), f32),
@@ -333,8 +359,8 @@
             pltpu.VMEM((136, 256), f32),
         ],
         compiler_params=pltpu.CompilerParams(vmem_limit_bytes=60 << 20),
-        name="near",
-    )(lists, *arrays)
+        name="near_self",
+    )(points, charges, part)
 
 
 def halves(x):
@@ -605,11 +631,12 @@
     from_left = lax.ppermute(to_right, AXES, up_perm)
     r1 = swap(pay)
     child = jnp.transpose(child_transfer, (1, 2, 0))
-    leaf_moments, mid_moments, top_moments = moments(charges, leaf_basis, child, parent_transfer)
     lists = jnp.stack([own_list, from_left[384:392].astype(i32), from_right[384:392].astype(i32)])
     lists = jnp.transpose(lists.reshape(3, 8, 2, 128), (0, 2, 1, 3)).reshape(6144)
     flat = points.reshape(384, 256)
-    near_own, near_l, near_r = near(lists, [from_left, from_right, flat, charges])
+    near_own, near_l, near_r, leaf_moments, mid_moments, top_moments = near(
+        lists, [from_left, from_right, flat, charges, parent_transfer], leaf_basis, child
+    )
     back_l = lax.ppermute(near_l, AXES, down_perm)
     back_r = lax.ppermute(near_r, AXES, up_perm)
     r1, near_own, leaf_moments, mid_moments, top_moments = lax.optimization_barrier(
@@ -619,6 +646,7 @@
     r1 = r1.reshape(4096, 128)
     pay2 = far(ids, r1, nodes_t, nodes_mid, leaf_moments, mid_moments, top_moments)
     r2 = swap(pay2.reshape(128, 5, 2, 128)).reshape(1280, 128)
+    near_own = near_self(flat, charges, near_own)
     return final(far_top, [tab, r1, r2, nodes_top, parent_transfer, near_own, back_l, back_r], leaf_basis, child)
 
 

time: 157 us -> 164 us (1.045); the launches traced: 157 us -> 161 us
  Pallas kernels: 81.5 us -> 87.3 us
  waiting for transfers between devices: 29.1 us -> 27.2 us
    pallas_call x1, Pallas kernels: 7.29 us -> 15.5 us  [near_self(): pl.pallas_call(near_self_kernel, out_shape=jax.ShapeDtypeStruct((128, 256...]
    ppermute x1, waiting for transfers between devices: 18.4 us -> 25.7 us  [local(): from_right = lax.ppermute(to_left, AXES, down_perm)]
    ppermute x1, waiting for transfers between devices: 4.48 us -> 0.01 us  [local(): back_l = lax.ppermute(near_l, AXES, down_perm)]
    ppermute x1, waiting for transfers between devices: 2.46 us -> 0.01 us  [local(): back_r = lax.ppermute(near_r, AXES, up_perm)]
    pallas_call x1, Pallas kernels: 33.4 us -> 31 us  [near(): pl.pallas_call(near_kernel, out_shape=tuple((jax.ShapeDtypeStruct((128, 2...]
    all_to_all x2, waiting for transfers between devices: 2.23 us -> 0.01 us  [swap(): return lax.all_to_all(x, AXES, split_axis=0, concat_axis=0, tiled=True)]
  transfers between devices with their start and end apart: 6 -> 6, of which waited for: 5 -> 2; matrix products, arithmetic and copies ran while one was open for 0% -> 0% of each run, Pallas kernels for 26% -> 29%
where the time goes in v3:
time: 164 us; the launch traced here: 161 us
  Pallas kernels  87.3 us (53%)
  starting transfers between devices  43.3 us (26%)
  waiting for transfers between devices  27.2 us (17%)
  local copies, waits for them, and re-layouts  2.08 us (1%)
    pallas_call x1, Pallas kernels, near(): pl.pallas_call(near_kernel, out_shape=tuple((jax.ShapeDtypeStruct((128, 2...  31 us
    all_to_all x2, starting transfers between devices, swap(): return lax.all_to_all(x, AXES, split_axis=0, concat_axis=0, tiled=True)  29.8 us
    pallas_call x1, Pallas kernels, far(): pl.pallas_call(far_kernel, out_shape=jax.ShapeDtypeStruct((1280, 128), f3...  26.7 us
    ppermute x1, waiting for transfers between devices, local(): from_right = lax.ppermute(to_left, AXES, down_perm)  25.7 us
    pallas_call x1, Pallas kernels, near_self(): pl.pallas_call(near_self_kernel, out_shape=jax.ShapeDtypeStruct((128, 256...  15.5 us
    pallas_call x1, Pallas kernels, final(): pl.pallas_call(final_kernel, out_shape=jax.ShapeDtypeStruct((128, 256), f...  7.08 us
    pallas_call x1, Pallas kernels, plan(): pl.pallas_call(plan_kernel, out_shape=(jax.ShapeDtypeStruct((128, 32, 128...  7 us
    ppermute x1, starting transfers between devices, local(): from_right = lax.ppermute(to_left, AXES, down_perm)  4.75 us
  transfers between devices with their start and end apart: 6, of which 2 were waited for; matrix products, arithmetic and copies ran while one was open for 0% of the time, Pallas kernels for 29%

profile of v3, /device:TPU:1, one launch (start us, length us, event | category | flops | bytes accessed | tf_op | source)
XLA Modules:
  0.0 161.1 jit_solution(5199393536125842581)
XLA Ops:
  0.0 7.0 %plan.1 = (f32[128,32,128]{2,1,0:T(8,128)}, f32[32,128]{1,0:T(8,128)}, s32[8,256]{1,0:T(8,128)}, f32[392,256]{1,0:T(8,128)}, f32[392,256]{1,0:T(8,128)}) custom-call(s32[1]{0:T(128)} %bitcast.me_ref, s32[16,128]{1,0:T(8,128)} %bitcast.28, s32[16,16]{1,0:T(8,128)} %mid_ref.1, s32[6,128]{1,0:T(8,128)} %bitcast.30, f32[3,64,128]{2,1,0:T(8,128)} %bitcast.25, ...), custom_call_target="tpu_custom_call" | custom-call | tf_op jit(solution)/shard_map/plan/pallas_call | solution.py:152
  7.0 0.0 copy-start.8
  7.0 0.0 copy-start.7
  7.0 0.0 copy-start.6
  7.0 11.5 %all-to-all-start = ((f32[128,32,128]{2,1,0:T(8,128)}), f32[128,32,128]{2,1,0:T(8,128)S(1)}, u32[]{:S(2)}, u32[]{:S(2)}) async-start(f32[128,32,128]{2,1,0:T(8,128)} %get-tuple-element.22), calls=%async_computation | async-start | bytes 4194304 | tf_op jit(solution)/shard_map/all_to_all | solution.py:605
  18.5 0.0 copy-done.8
  18.5 4.8 %collective-permute-start.1 = (f32[392,256]{1,0:T(8,128)S(1)}, f32[392,256]{1,0:T(8,128)S(1)}, u32[]{:S(2)}, u32[]{:S(2)}) collective-permute-start(f32[392,256]{1,0:T(8,128)S(1)} %copy-done.8), channel_id=1, source_target_pairs={{1,0},{2,1},{3,2},{4,3},{5,4},{6,5},{7,6},{8,7},{9,8},{10,9},{11,1... | collective-permute-start | bytes 1204232 | tf_op jit(solution)/shard_map/ppermute | solution.py:630
  23.3 0.0 copy-done.7
  23.3 1.9 %collective-permute-start = (f32[392,256]{1,0:T(8,128)S(1)}, f32[392,256]{1,0:T(8,128)S(1)}, u32[]{:S(2)}, u32[]{:S(2)}) collective-permute-start(f32[392,256]{1,0:T(8,128)S(1)} %copy-done.7), channel_id=1, source_target_pairs={{0,1},{1,2},{2,3},{3,4},{4,5},{5,6},{6,7},{7,8},{8,9},{9,10},{10,1... | collective-permute-start | bytes 1204232 | tf_op jit(solution)/shard_map/ppermute | solution.py:631
  25.2 25.7 %collective-permute-done.1.tgt_r = f32[392,256]{1,0:T(8,128)S(1)} collective-permute-done((f32[392,256]{1,0:T(8,128)S(1)}, f32[392,256]{1,0:T(8,128)S(1)}, u32[]{:S(2)}, u32[]{:S(2)}) %collective-permute-start.1) | collective-permute-done | bytes 401440 | tf_op jit(solution)/shard_map/ppermute | solution.py:630
  50.9 0.0 copy-start.2
  51.0 1.5 collective-permute-done.tgt_l
  52.4 0.0 copy-start.3
  52.4 0.0 copy-done.6
  52.5 0.7 pad_add_fusion
  53.1 0.0 copy-done.2
  53.1 0.1 copy-done.3
  53.2 31.0 %near.1 = (f32[128,256]{1,0:T(8,128)}, f32[128,256]{1,0:T(8,128)}, f32[128,256]{1,0:T(8,128)}, f32[128,64]{1,0:T(8,128)}, f32[16,64]{1,0:T(8,128)}, /*index=5*/f32[1,128]{1,0:T(1,128)}) custom-call(s32[6144]{0:T(1024)} %bitcast.27, f32[392,256]{1,0:T(8,128)} %copy-done.3, f32[392,256]{1,0:T(8,128)} %copy-done.2, f32[384,256]{1,0:T(8,128)} %bitcast.21, ...), custom_call_target="tpu_custom_call" | custom-call | tf_op jit(solution)/shard_map/near/pallas_call | solution.py:309
  84.2 0.0 all-to-all-done
  84.2 0.0 copy-start
  84.2 0.2 convert_reduce_fusion
  84.5 1.0 convert_element_type.16.ids_ref
  85.5 0.1 copy-done
  85.6 0.0 copy-start.10
  85.6 0.0 copy-start.9
  85.6 26.7 %far.1 = f32[1280,128]{1,0:T(8,128)} custom-call(s32[3072]{0:T(1024)} %convert_element_type.16.ids_ref, f32[4096,128]{1,0:T(8,128)} %bitcast.17, f32[3,64,128]{2,1,0:T(8,128)} %bitcast.26, f32[3,16,64]{2,1,0:T(8,128)} %nm_ref.3, f32[128,64]{1,0:T(8,128)} %get-tuple-element.31.lm_ref, f32[16,64]{1,0:T(8,128)} %get-tuple-element.32.mm_ref, ...), custom_call_target="tpu_custom_call" | custom-call | tf_op jit(solution)/shard_map/far/pallas_call | solution.py:491
  112.2 18.3 %all-to-all-start.1 = ((f32[128,5,2,128]{3,2,1,0:T(2,128)}), f32[128,5,2,128]{3,2,1,0:T(2,128)S(1)}, u32[]{:S(2)}, u32[]{:S(2)}) async-start(f32[128,5,2,128]{3,2,1,0:T(2,128)} %bitcast.24), calls=%async_computation.1 | async-start | bytes 1310720 | tf_op jit(solution)/shard_map/all_to_all | solution.py:605
  130.5 0.0 copy-done.10
  130.5 4.8 %collective-permute-start.2 = (f32[128,256]{1,0:T(8,128)S(1)}, f32[128,256]{1,0:T(8,128)S(1)}, u32[]{:S(2)}, u32[]{:S(2)}) collective-permute-start(f32[128,256]{1,0:T(8,128)S(1)} %copy-done.10), channel_id=1, source_target_pairs={{1,0},{2,1},{3,2},{4,3},{5,4},{6,5},{7,6},{8,7},{9,8},{10,9},{11,1... | collective-permute-start | bytes 393224 | tf_op jit(solution)/shard_map/ppermute | solution.py:640
  135.3 0.0 copy-done.9
  135.3 2.1 %collective-permute-start.3 = (f32[128,256]{1,0:T(8,128)S(1)}, f32[128,256]{1,0:T(8,128)S(1)}, u32[]{:S(2)}, u32[]{:S(2)}) collective-permute-start(f32[128,256]{1,0:T(8,128)S(1)} %copy-done.9), channel_id=1, source_target_pairs={{0,1},{1,2},{2,3},{3,4},{4,5},{5,6},{6,7},{7,8},{8,9},{9,10},{10,1... | collective-permute-start | bytes 393224 | tf_op jit(solution)/shard_map/ppermute | solution.py:641
  137.4 15.5 %near_self.1.near_ref = f32[128,256]{1,0:T(8,128)} custom-call(f32[384,256]{1,0:T(8,128)} %bitcast.22, f32[128,256]{1,0:T(8,128)} %q_ref.3, f32[128,256]{1,0:T(8,128)} %get-tuple-element.34.part_ref), custom_call_target="tpu_custom_call" | custom-call | tf_op jit(solution)/shard_map/near_self/pallas_call | solution.py:349
  152.9 0.0 collective-permute-done.2.bl_ref
  153.0 0.0 copy-start.4
  153.0 0.0 collective-permute-done.3.br_ref
  153.0 0.0 copy-start.5
  153.0 0.0 all-to-all-done.1
  153.0 0.0 copy-start.1
  153.0 0.6 copy-done.4
  153.6 0.0 copy-done.5
  153.6 0.2 copy-done.1
  153.9 7.1 %final.1 = f32[128,256]{1,0:T(8,128)} custom-call(s32[2,16]{1,0:T(2,128)} %top_ids.1, f32[32,128]{1,0:T(8,128)} %get-tuple-element.21.tab_ref, f32[4096,128]{1,0:T(8,128)} %bitcast.18, f32[1280,128]{1,0:T(8,128)} %bitcast.23, f32[3,2,64]{2,1,0:T(2,128)} %nt_ref.3, f32[16,64,64]{2,1,0:T(8,128)} %pt_ref.3, f32[128,256]{1,0:T(8,128)} %near_self.1.near_ref, ...), custom_call_target="tpu_custom_call" | custom-call | tf_op jit(solution)/shard_map/final/pallas_call | solution.py:589
  (2 shorter events, 0.0 us)
Async XLA Ops:
  7.0 11.5 %copy-start.8 = (f32[392,256]{1,0:T(8,128)S(1)}, f32[392,256]{1,0:T(8,128)}, u32[]{:S(2)}) copy-start(f32[392,256]{1,0:T(8,128)} %get-tuple-element.25) | copy-start | bytes 1204228
  7.0 16.3 %copy-start.7 = (f32[392,256]{1,0:T(8,128)S(1)}, f32[392,256]{1,0:T(8,128)}, u32[]{:S(2)}) copy-start(f32[392,256]{1,0:T(8,128)} %get-tuple-element.24) | copy-start | bytes 1204228
  7.0 45.4 %copy-start.6 = (s32[8,256]{1,0:T(8,128)S(1)}, s32[8,256]{1,0:T(8,128)}, u32[]{:S(2)}) copy-start(s32[8,256]{1,0:T(8,128)} %get-tuple-element.23) | copy-start | bytes 24580
  7.0 77.2 %all-to-all-start = ((f32[128,32,128]{2,1,0:T(8,128)}), f32[128,32,128]{2,1,0:T(8,128)S(1)}, u32[]{:S(2)}, u32[]{:S(2)}) async-start(f32[128,32,128]{2,1,0:T(8,128)} %get-tuple-element.22), calls=%async_computation | async-start | bytes 4194304 | tf_op jit(solution)/shard_map/all_to_all | solution.py:605
  18.5 32.4 %collective-permute-start.1 = (f32[392,256]{1,0:T(8,128)S(1)}, f32[392,256]{1,0:T(8,128)S(1)}, u32[]{:S(2)}, u32[]{:S(2)}) collective-permute-start(f32[392,256]{1,0:T(8,128)S(1)} %copy-done.8), channel_id=1, source_target_pairs={{1,0},{2,1},{3,2},{4,3},{5,4},{6,5},{7,6},{8,7},{9,8},{10,9},{11,1... | collective-permute-start | bytes 1204232 | tf_op jit(solution)/shard_map/ppermute | solution.py:630
  23.3 29.1 %collective-permute-start = (f32[392,256]{1,0:T(8,128)S(1)}, f32[392,256]{1,0:T(8,128)S(1)}, u32[]{:S(2)}, u32[]{:S(2)}) collective-permute-start(f32[392,256]{1,0:T(8,128)S(1)} %copy-done.7), channel_id=1, source_target_pairs={{0,1},{1,2},{2,3},{3,4},{4,5},{5,6},{6,7},{7,8},{8,9},{9,10},{10,1... | collective-permute-start | bytes 1204232 | tf_op jit(solution)/shard_map/ppermute | solution.py:631
  50.9 2.2 %copy-start.2 = (f32[392,256]{1,0:T(8,128)}, f32[392,256]{1,0:T(8,128)S(1)}, u32[]{:S(2)}) copy-start(f32[392,256]{1,0:T(8,128)S(1)} %collective-permute-done.1.tgt_r) | copy-start | bytes 1204228
  52.4 0.8 copy-start.3
  84.2 1.3 copy-start
  85.6 45.0 %copy-start.10 = (f32[128,256]{1,0:T(8,128)S(1)}, f32[128,256]{1,0:T(8,128)}, u32[]{:S(2)}) copy-start(f32[128,256]{1,0:T(8,128)} %get-tuple-element.35) | copy-start | bytes 393220
  85.6 49.8 %copy-start.9 = (f32[128,256]{1,0:T(8,128)S(1)}, f32[128,256]{1,0:T(8,128)}, u32[]{:S(2)}) copy-start(f32[128,256]{1,0:T(8,128)} %get-tuple-element.36) | copy-start | bytes 393220
  112.2 40.7 %all-to-all-start.1 = ((f32[128,5,2,128]{3,2,1,0:T(2,128)}), f32[128,5,2,128]{3,2,1,0:T(2,128)S(1)}, u32[]{:S(2)}, u32[]{:S(2)}) async-start(f32[128,5,2,128]{3,2,1,0:T(2,128)} %bitcast.24), calls=%async_computation.1 | async-start | bytes 1310720 | tf_op jit(solution)/shard_map/all_to_all | solution.py:605
  130.5 22.4 %collective-permute-start.2 = (f32[128,256]{1,0:T(8,128)S(1)}, f32[128,256]{1,0:T(8,128)S(1)}, u32[]{:S(2)}, u32[]{:S(2)}) collective-permute-start(f32[128,256]{1,0:T(8,128)S(1)} %copy-done.10), channel_id=1, source_target_pairs={{1,0},{2,1},{3,2},{4,3},{5,4},{6,5},{7,6},{8,7},{9,8},{10,9},{11,1... | collective-permute-start | bytes 393224 | tf_op jit(solution)/shard_map/ppermute | solution.py:640
  135.3 17.6 %collective-permute-start.3 = (f32[128,256]{1,0:T(8,128)S(1)}, f32[128,256]{1,0:T(8,128)S(1)}, u32[]{:S(2)}, u32[]{:S(2)}) collective-permute-start(f32[128,256]{1,0:T(8,128)S(1)} %copy-done.9), channel_id=1, source_target_pairs={{0,1},{1,2},{2,3},{3,4},{4,5},{5,6},{6,7},{7,8},{8,9},{9,10},{10,1... | collective-permute-start | bytes 393224 | tf_op jit(solution)/shard_map/ppermute | solution.py:641
  153.0 0.6 copy-start.4
  153.0 0.7 copy-start.5
  153.0 0.9 copy-start.1

commit v4 on v3

--- a/solution.py
+++ b/solution.py
@@ -12,6 +12,7 @@
 soften = 0.25
 AXES = ("dom", "sub")
 NB = 8
+SELF = 32
 TRANS = (((1,), (1,)), ((), ()))
 
 
@@ -209,27 +210,34 @@
     return jnp.where(r < 5, v, 0.0)
 
 
-def near_tables(pts_ref, q_ref, sf_ref, qb_ref):
+def near_tables(pts_ref, q_ref, sf_ref, qb_ref, count):
     r = iota((64, 128), 0)
     spread = jnp.where((r >= 48) & (r < 51), 1.0, 0.0).astype(bf16)
     r8 = iota((8, 256), 0)
 
+    def factors(n):
+        x = pts_ref[pl.ds(n, 1), :]
+        y = pts_ref[pl.ds(128 + n, 1), :]
+        z = pts_ref[pl.ds(256 + n, 1), :]
+        norm = x * x + y * y + z * z + soften
+        h, m, l = split3(tile_rows(x, y, z, jnp.ones_like(x), norm))
+        qh, qm, ql = split3(jnp.broadcast_to(q_ref[pl.ds(n, 1), :], (8, 256)))
+        q = jnp.where(r8 == 0, qh, jnp.where(r8 == 1, qm, jnp.where(r8 == 2, ql, 0.0)))
+        return jnp.concatenate([h, m, l, h, m, h, q, jnp.zeros_like(q)], axis=0).T.astype(bf16)
+
+    for n in range(8):
+        sf_ref[n] = factors(n)
+
     def prepare(it, carry):
         for u in range(8):
-            n = it * 8 + u
-            x = pts_ref[pl.ds(n, 1), :]
-            y = pts_ref[pl.ds(128 + n, 1), :]
-            z = pts_ref[pl.ds(256 + n, 1), :]
-            norm = x * x + y * y + z * z + soften
-            h, m, l = split3(tile_rows(x, y, z, jnp.ones_like(x), norm))
-            qh, qm, ql = split3(jnp.broadcast_to(q_ref[pl.ds(n, 1), :], (8, 256)))
-            q = jnp.where(r8 == 0, qh, jnp.where(r8 == 1, qm, jnp.where(r8 == 2, ql, 0.0)))
-            t = jnp.concatenate([h, m, l, h, m, h, q, jnp.zeros_like(q)], axis=0).T.astype(bf16)
-            sf_ref[n] = t
-            qb_ref[n] = dot(t, spread)
+            qb_ref[it * 8 + u] = dot(sf_ref[it * 8 + u], spread)
+        ahead = jnp.minimum(it + 1, count // 8 - 1)
+        made = [factors(ahead * 8 + u) for u in range(8)]
+        for u in range(8):
+            sf_ref[ahead * 8 + u] = made[u]
         return carry
 
-    lax.fori_loop(0, 16, prepare, 0)
+    lax.fori_loop(0, count // 8, prepare, 0)
 
 
 def near_pairs(entry, total, tgt, sf_ref, qb_ref, rhs_ref, d_ref, acc_ref):
@@ -290,10 +298,10 @@
     for k in range(8):
         part(k).start()
     child.start()
-    near_tables(pts_ref, q_ref, sf_ref, qb_ref)
+    near_tables(pts_ref, q_ref, sf_ref, qb_ref, 128)
     for k, (tgt, out) in enumerate(((pts_ref, out_own), (tgt_l, out_l), (tgt_r, out_r))):
         acc_ref[...] = jnp.zeros((136, 256), f32)
-        skip = 128 if k == 0 else 0
+        skip = SELF if k == 0 else 0
 
         def entry(i, first=k * 2048 + skip):
             return lst[first + i], lst[first + 1024 + i]
@@ -332,15 +340,15 @@
 
 
 def near_self_kernel(pts_ref, q_ref, part_ref, out, sf_ref, qb_ref, rhs_ref, d_ref, acc_ref):
-    near_tables(pts_ref, q_ref, sf_ref, qb_ref)
+    near_tables(pts_ref, q_ref, sf_ref, qb_ref, SELF)
     acc_ref[0:128, :] = part_ref[...]
     acc_ref[128:136, :] = jnp.zeros((8, 256), f32)
 
     def entry(i):
-        n = jnp.minimum(i, 127)
+        n = jnp.minimum(i, SELF - 1)
         return n + 1, n
 
-    near_pairs(entry, 128, pts_ref, sf_ref, qb_ref, rhs_ref, d_ref, acc_ref)
+    near_pairs(entry, SELF, pts_ref, sf_ref, qb_ref, rhs_ref, d_ref, acc_ref)
     out[...] = acc_ref[0:128, :]
 
 
@@ -352,8 +360,8 @@
         in_specs=[vm] * 3,
         out_specs=vm,
         scratch_shapes=[
-            pltpu.VMEM((128, 256, 64), bf16),
-            pltpu.VMEM((128, 256, 128), f32),
+            pltpu.VMEM((SELF, 256, 64), bf16),
+            pltpu.VMEM((SELF, 256, 128), f32),
             pltpu.VMEM((NB, 48, 256), bf16),
             pltpu.VMEM((NB, 256, 256), f32),
             pltpu.VMEM((136, 256), f32),
@@ -637,8 +645,6 @@
     near_own, near_l, near_r, leaf_moments, mid_moments, top_moments = near(
         lists, [from_left, from_right, flat, charges, parent_transfer], leaf_basis, child
     )
-    back_l = lax.ppermute(near_l, AXES, down_perm)
-    back_r = lax.ppermute(near_r, AXES, up_perm)
     r1, near_own, leaf_moments, mid_moments, top_moments = lax.optimization_barrier(
         (r1, near_own, leaf_moments, mid_moments, top_moments)
     )
@@ -646,6 +652,8 @@
     r1 = r1.reshape(4096, 128)
     pay2 = far(ids, r1, nodes_t, nodes_mid, leaf_moments, mid_moments, top_moments)
     r2 = swap(pay2.reshape(128, 5, 2, 128)).reshape(1280, 128)
+    back_l = lax.ppermute(near_l, AXES, down_perm)
+    back_r = lax.ppermute(near_r, AXES, up_perm)
     near_own = near_self(flat, charges, near_own)
     return final(far_top, [tab, r1, r2, nodes_top, parent_transfer, near_own, back_l, back_r], leaf_basis, child)
 

time: 164 us -> 158 us (0.963); the launches traced: 161 us -> 158 us
  Pallas kernels: 87.3 us -> 80.6 us
  waiting for transfers between devices: 27.2 us -> 30.9 us
    pallas_call x1, Pallas kernels: 15.5 us -> 5.31 us  [near_self(): pl.pallas_call(near_self_kernel, out_shape=jax.ShapeDtypeStruct((128, 256...]
    pallas_call x1, Pallas kernels: 31 us -> 34.5 us  [near(): pl.pallas_call(near_kernel, out_shape=tuple((jax.ShapeDtypeStruct((128, 2...]
    all_to_all x2, waiting for transfers between devices: 0.01 us -> 2.23 us  [swap(): return lax.all_to_all(x, AXES, split_axis=0, concat_axis=0, tiled=True)]
  transfers between devices with their start and end apart: 6 -> 6, of which waited for: 2 -> 4; matrix products, arithmetic and copies ran while one was open for 0% -> 0% of each run, Pallas kernels for 29% -> 25%
where the time goes in v4:
time: 158 us
  Pallas kernels  80.6 us (51%)
  starting transfers between devices  43.3 us (27%)
  waiting for transfers between devices  30.9 us (20%)
  local copies, waits for them, and re-layouts  2.03 us (1%)
    pallas_call x1, Pallas kernels, near(): pl.pallas_call(near_kernel, out_shape=tuple((jax.ShapeDtypeStruct((128, 2...  34.5 us
    all_to_all x2, starting transfers between devices, swap(): return lax.all_to_all(x, AXES, split_axis=0, concat_axis=0, tiled=True)  29.8 us
    pallas_call x1, Pallas kernels, far(): pl.pallas_call(far_kernel, out_shape=jax.ShapeDtypeStruct((1280, 128), f3...  26.7 us
    ppermute x1, waiting for transfers between devices, local(): from_right = lax.ppermute(to_left, AXES, down_perm)  25.7 us
    pallas_call x1, Pallas kernels, final(): pl.pallas_call(final_kernel, out_shape=jax.ShapeDtypeStruct((128, 256), f...  7.07 us
    pallas_call x1, Pallas kernels, plan(): pl.pallas_call(plan_kernel, out_shape=(jax.ShapeDtypeStruct((128, 32, 128...  7 us
    pallas_call x1, Pallas kernels, near_self(): pl.pallas_call(near_self_kernel, out_shape=jax.ShapeDtypeStruct((128, 256...  5.31 us
    ppermute x1, starting transfers between devices, local(): from_right = lax.ppermute(to_left, AXES, down_perm)  4.75 us
  transfers between devices with their start and end apart: 6, of which 4 were waited for; matrix products, arithmetic and copies ran while one was open for 0% of the time, Pallas kernels for 25%

profile of v4, /device:TPU:1, one launch (start us, length us, event | category | flops | bytes accessed | tf_op | source)
XLA Modules:
  0.0 158.0 jit_solution(12956771708182363816)
XLA Ops:
  0.0 7.0 %plan.1 = (f32[128,32,128]{2,1,0:T(8,128)}, f32[32,128]{1,0:T(8,128)}, s32[8,256]{1,0:T(8,128)}, f32[392,256]{1,0:T(8,128)}, f32[392,256]{1,0:T(8,128)}) custom-call(s32[1]{0:T(128)} %bitcast.me_ref, s32[16,128]{1,0:T(8,128)} %bitcast.28, s32[16,16]{1,0:T(8,128)} %mid_ref.1, s32[6,128]{1,0:T(8,128)} %bitcast.30, f32[3,64,128]{2,1,0:T(8,128)} %bitcast.25, ...), custom_call_target="tpu_custom_call" | custom-call | tf_op jit(solution)/shard_map/plan/pallas_call | solution.py:153
  7.0 0.0 copy-start.8
  7.0 0.0 copy-start.7
  7.0 0.0 copy-start.6
  7.0 11.5 %all-to-all-start = ((f32[128,32,128]{2,1,0:T(8,128)}), f32[128,32,128]{2,1,0:T(8,128)S(1)}, u32[]{:S(2)}, u32[]{:S(2)}) async-start(f32[128,32,128]{2,1,0:T(8,128)} %get-tuple-element.22), calls=%async_computation | async-start | bytes 4194304 | tf_op jit(solution)/shard_map/all_to_all | solution.py:613
  18.5 0.0 copy-done.8
  18.5 4.8 %collective-permute-start.1 = (f32[392,256]{1,0:T(8,128)S(1)}, f32[392,256]{1,0:T(8,128)S(1)}, u32[]{:S(2)}, u32[]{:S(2)}) collective-permute-start(f32[392,256]{1,0:T(8,128)S(1)} %copy-done.8), channel_id=1, source_target_pairs={{1,0},{2,1},{3,2},{4,3},{5,4},{6,5},{7,6},{8,7},{9,8},{10,9},{11,1... | collective-permute-start | bytes 1204232 | tf_op jit(solution)/shard_map/ppermute | solution.py:638
  23.3 0.0 copy-done.7
  23.3 1.9 %collective-permute-start = (f32[392,256]{1,0:T(8,128)S(1)}, f32[392,256]{1,0:T(8,128)S(1)}, u32[]{:S(2)}, u32[]{:S(2)}) collective-permute-start(f32[392,256]{1,0:T(8,128)S(1)} %copy-done.7), channel_id=1, source_target_pairs={{0,1},{1,2},{2,3},{3,4},{4,5},{5,6},{6,7},{7,8},{8,9},{9,10},{10,1... | collective-permute-start | bytes 1204232 | tf_op jit(solution)/shard_map/ppermute | solution.py:639
  25.2 25.7 %collective-permute-done.1.tgt_r = f32[392,256]{1,0:T(8,128)S(1)} collective-permute-done((f32[392,256]{1,0:T(8,128)S(1)}, f32[392,256]{1,0:T(8,128)S(1)}, u32[]{:S(2)}, u32[]{:S(2)}) %collective-permute-start.1) | collective-permute-done | bytes 401440 | tf_op jit(solution)/shard_map/ppermute | solution.py:638
  50.9 0.0 copy-start.2
  51.0 1.5 collective-permute-done.tgt_l
  52.4 0.0 copy-start.3
  52.4 0.0 copy-done.6
  52.5 0.7 pad_add_fusion
  53.1 0.0 copy-done.2
  53.1 0.1 copy-done.3
  53.2 34.5 %near.1 = (f32[128,256]{1,0:T(8,128)}, f32[128,256]{1,0:T(8,128)}, f32[128,256]{1,0:T(8,128)}, f32[128,64]{1,0:T(8,128)}, f32[16,64]{1,0:T(8,128)}, /*index=5*/f32[1,128]{1,0:T(1,128)}) custom-call(s32[6144]{0:T(1024)} %bitcast.27, f32[392,256]{1,0:T(8,128)} %copy-done.3, f32[392,256]{1,0:T(8,128)} %copy-done.2, f32[384,256]{1,0:T(8,128)} %bitcast.21, ...), custom_call_target="tpu_custom_call" | custom-call | tf_op jit(solution)/shard_map/near/pallas_call | solution.py:317
  87.7 0.0 all-to-all-done
  87.7 0.0 copy-start
  87.7 0.2 convert_reduce_fusion
  88.0 1.0 convert_element_type.16.ids_ref
  89.0 0.1 copy-done
  89.1 0.0 copy-start.10
  89.1 0.0 copy-start.9
  89.1 26.7 %far.1 = f32[1280,128]{1,0:T(8,128)} custom-call(s32[3072]{0:T(1024)} %convert_element_type.16.ids_ref, f32[4096,128]{1,0:T(8,128)} %bitcast.17, f32[3,64,128]{2,1,0:T(8,128)} %bitcast.26, f32[3,16,64]{2,1,0:T(8,128)} %nm_ref.3, f32[128,64]{1,0:T(8,128)} %get-tuple-element.31.lm_ref, f32[16,64]{1,0:T(8,128)} %get-tuple-element.32.mm_ref, ...), custom_call_target="tpu_custom_call" | custom-call | tf_op jit(solution)/shard_map/far/pallas_call | solution.py:499
  115.7 18.3 %all-to-all-start.1 = ((f32[128,5,2,128]{3,2,1,0:T(2,128)}), f32[128,5,2,128]{3,2,1,0:T(2,128)S(1)}, u32[]{:S(2)}, u32[]{:S(2)}) async-start(f32[128,5,2,128]{3,2,1,0:T(2,128)} %bitcast.24), calls=%async_computation.1 | async-start | bytes 1310720 | tf_op jit(solution)/shard_map/all_to_all | solution.py:613
  134.1 0.0 copy-done.10
  134.1 4.8 %collective-permute-start.2 = (f32[128,256]{1,0:T(8,128)S(1)}, f32[128,256]{1,0:T(8,128)S(1)}, u32[]{:S(2)}, u32[]{:S(2)}) collective-permute-start(f32[128,256]{1,0:T(8,128)S(1)} %copy-done.10), channel_id=1, source_target_pairs={{1,0},{2,1},{3,2},{4,3},{5,4},{6,5},{7,6},{8,7},{9,8},{10,9},{11,1... | collective-permute-start | bytes 393224 | tf_op jit(solution)/shard_map/ppermute | solution.py:655
  138.8 0.0 copy-done.9
  138.8 2.1 %collective-permute-start.3 = (f32[128,256]{1,0:T(8,128)S(1)}, f32[128,256]{1,0:T(8,128)S(1)}, u32[]{:S(2)}, u32[]{:S(2)}) collective-permute-start(f32[128,256]{1,0:T(8,128)S(1)} %copy-done.9), channel_id=1, source_target_pairs={{0,1},{1,2},{2,3},{3,4},{4,5},{5,6},{6,7},{7,8},{8,9},{9,10},{10,1... | collective-permute-start | bytes 393224 | tf_op jit(solution)/shard_map/ppermute | solution.py:656
  140.9 5.3 %near_self.1.near_ref = f32[128,256]{1,0:T(8,128)} custom-call(f32[384,256]{1,0:T(8,128)} %bitcast.22, f32[128,256]{1,0:T(8,128)} %q_ref.3, f32[128,256]{1,0:T(8,128)} %get-tuple-element.34.part_ref), custom_call_target="tpu_custom_call" | custom-call | tf_op jit(solution)/shard_map/near_self/pallas_call | solution.py:357
  146.3 0.0 collective-permute-done.2.bl_ref
  146.3 0.0 copy-start.4
  146.3 1.4 collective-permute-done.3.br_ref
  147.7 0.0 copy-start.5
  147.7 2.2 %all-to-all-done.1 = f32[128,5,2,128]{3,2,1,0:T(2,128)S(1)} async-done(((f32[128,5,2,128]{3,2,1,0:T(2,128)}), f32[128,5,2,128]{3,2,1,0:T(2,128)S(1)}, u32[]{:S(2)}, u32[]{:S(2)}) %all-to-all-start.1) | async-done | bytes 655392 | tf_op jit(solution)/shard_map/all_to_all | solution.py:613
  149.9 0.0 copy-start.1
  149.9 0.0 copy-done.4
  149.9 0.0 copy-done.5
  149.9 0.8 copy-done.1
  150.8 7.1 %final.1 = f32[128,256]{1,0:T(8,128)} custom-call(s32[2,16]{1,0:T(2,128)} %top_ids.1, f32[32,128]{1,0:T(8,128)} %get-tuple-element.21.tab_ref, f32[4096,128]{1,0:T(8,128)} %bitcast.18, f32[1280,128]{1,0:T(8,128)} %bitcast.23, f32[3,2,64]{2,1,0:T(2,128)} %nt_ref.3, f32[16,64,64]{2,1,0:T(8,128)} %pt_ref.3, f32[128,256]{1,0:T(8,128)} %near_self.1.near_ref, ...), custom_call_target="tpu_custom_call" | custom-call | tf_op jit(solution)/shard_map/final/pallas_call | solution.py:597
  (2 shorter events, 0.0 us)
Async XLA Ops:
  7.0 11.5 %copy-start.8 = (f32[392,256]{1,0:T(8,128)S(1)}, f32[392,256]{1,0:T(8,128)}, u32[]{:S(2)}) copy-start(f32[392,256]{1,0:T(8,128)} %get-tuple-element.25) | copy-start | bytes 1204228
  7.0 16.3 %copy-start.7 = (f32[392,256]{1,0:T(8,128)S(1)}, f32[392,256]{1,0:T(8,128)}, u32[]{:S(2)}) copy-start(f32[392,256]{1,0:T(8,128)} %get-tuple-element.24) | copy-start | bytes 1204228
  7.0 45.4 %copy-start.6 = (s32[8,256]{1,0:T(8,128)S(1)}, s32[8,256]{1,0:T(8,128)}, u32[]{:S(2)}) copy-start(s32[8,256]{1,0:T(8,128)} %get-tuple-element.23) | copy-start | bytes 24580
  7.0 80.7 %all-to-all-start = ((f32[128,32,128]{2,1,0:T(8,128)}), f32[128,32,128]{2,1,0:T(8,128)S(1)}, u32[]{:S(2)}, u32[]{:S(2)}) async-start(f32[128,32,128]{2,1,0:T(8,128)} %get-tuple-element.22), calls=%async_computation | async-start | bytes 4194304 | tf_op jit(solution)/shard_map/all_to_all | solution.py:613
  18.5 32.4 %collective-permute-start.1 = (f32[392,256]{1,0:T(8,128)S(1)}, f32[392,256]{1,0:T(8,128)S(1)}, u32[]{:S(2)}, u32[]{:S(2)}) collective-permute-start(f32[392,256]{1,0:T(8,128)S(1)} %copy-done.8), channel_id=1, source_target_pairs={{1,0},{2,1},{3,2},{4,3},{5,4},{6,5},{7,6},{8,7},{9,8},{10,9},{11,1... | collective-permute-start | bytes 1204232 | tf_op jit(solution)/shard_map/ppermute | solution.py:638
  23.3 29.1 %collective-permute-start = (f32[392,256]{1,0:T(8,128)S(1)}, f32[392,256]{1,0:T(8,128)S(1)}, u32[]{:S(2)}, u32[]{:S(2)}) collective-permute-start(f32[392,256]{1,0:T(8,128)S(1)} %copy-done.7), channel_id=1, source_target_pairs={{0,1},{1,2},{2,3},{3,4},{4,5},{5,6},{6,7},{7,8},{8,9},{9,10},{10,1... | collective-permute-start | bytes 1204232 | tf_op jit(solution)/shard_map/ppermute | solution.py:639
  50.9 2.2 %copy-start.2 = (f32[392,256]{1,0:T(8,128)}, f32[392,256]{1,0:T(8,128)S(1)}, u32[]{:S(2)}) copy-start(f32[392,256]{1,0:T(8,128)S(1)} %collective-permute-done.1.tgt_r) | copy-start | bytes 1204228
  52.4 0.8 copy-start.3
  87.7 1.3 copy-start
  89.1 45.0 %copy-start.10 = (f32[128,256]{1,0:T(8,128)S(1)}, f32[128,256]{1,0:T(8,128)}, u32[]{:S(2)}) copy-start(f32[128,256]{1,0:T(8,128)} %get-tuple-element.35) | copy-start | bytes 393220
  89.1 49.8 %copy-start.9 = (f32[128,256]{1,0:T(8,128)S(1)}, f32[128,256]{1,0:T(8,128)}, u32[]{:S(2)}) copy-start(f32[128,256]{1,0:T(8,128)} %get-tuple-element.36) | copy-start | bytes 393220
  115.7 34.2 %all-to-all-start.1 = ((f32[128,5,2,128]{3,2,1,0:T(2,128)}), f32[128,5,2,128]{3,2,1,0:T(2,128)S(1)}, u32[]{:S(2)}, u32[]{:S(2)}) async-start(f32[128,5,2,128]{3,2,1,0:T(2,128)} %bitcast.24), calls=%async_computation.1 | async-start | bytes 1310720 | tf_op jit(solution)/shard_map/all_to_all | solution.py:613
  134.1 12.2 %collective-permute-start.2 = (f32[128,256]{1,0:T(8,128)S(1)}, f32[128,256]{1,0:T(8,128)S(1)}, u32[]{:S(2)}, u32[]{:S(2)}) collective-permute-start(f32[128,256]{1,0:T(8,128)S(1)} %copy-done.10), channel_id=1, source_target_pairs={{1,0},{2,1},{3,2},{4,3},{5,4},{6,5},{7,6},{8,7},{9,8},{10,9},{11,1... | collective-permute-start | bytes 393224 | tf_op jit(solution)/shard_map/ppermute | solution.py:655
  138.8 8.9 %collective-permute-start.3 = (f32[128,256]{1,0:T(8,128)S(1)}, f32[128,256]{1,0:T(8,128)S(1)}, u32[]{:S(2)}, u32[]{:S(2)}) collective-permute-start(f32[128,256]{1,0:T(8,128)S(1)} %copy-done.9), channel_id=1, source_target_pairs={{0,1},{1,2},{2,3},{3,4},{4,5},{5,6},{6,7},{7,8},{8,9},{9,10},{10,1... | collective-permute-start | bytes 393224 | tf_op jit(solution)/shard_map/ppermute | solution.py:656
  146.3 3.7 %copy-start.4 = (f32[128,256]{1,0:T(8,128)}, f32[128,256]{1,0:T(8,128)S(1)}, u32[]{:S(2)}) copy-start(f32[128,256]{1,0:T(8,128)S(1)} %collective-permute-done.2.bl_ref) | copy-start | bytes 393220
  147.7 2.2 %copy-start.5 = (f32[128,256]{1,0:T(8,128)}, f32[128,256]{1,0:T(8,128)S(1)}, u32[]{:S(2)}) copy-start(f32[128,256]{1,0:T(8,128)S(1)} %collective-permute-done.3.br_ref) | copy-start | bytes 393220
  149.9 0.8 copy-start.1

commit v5 on v4

--- a/solution.py
+++ b/solution.py
@@ -339,7 +339,7 @@
     )(lists, *arrays, leaf_basis, child)
 
 
-def near_self_kernel(pts_ref, q_ref, part_ref, out, sf_ref, qb_ref, rhs_ref, d_ref, acc_ref):
+def near_self(pts_ref, q_ref, part_ref, sf_ref, qb_ref, rhs_ref, d_ref, acc_ref):
     near_tables(pts_ref, q_ref, sf_ref, qb_ref, SELF)
     acc_ref[0:128, :] = part_ref[...]
     acc_ref[128:136, :] = jnp.zeros((8, 256), f32)
@@ -349,26 +349,6 @@
         return n + 1, n
 
     near_pairs(entry, SELF, pts_ref, sf_ref, qb_ref, rhs_ref, d_ref, acc_ref)
-    out[...] = acc_ref[0:128, :]
-
-
-def near_self(points, charges, part):
-    vm = pl.BlockSpec(memory_space=pltpu.VMEM)
-    return pl.pallas_call(
-        near_self_kernel,
-        out_shape=jax.ShapeDtypeStruct((128, 256), f32),
-        in_specs=[vm] * 3,
-        out_specs=vm,
-        scratch_shapes=[
-            pltpu.VMEM((SELF, 256, 64), bf16),
-            pltpu.VMEM((SELF, 256, 128), f32),
-            pltpu.VMEM((NB, 48, 256), bf16),
-            pltpu.VMEM((NB, 256, 256), f32),
-            pltpu.VMEM((136, 256), f32),
-        ],
-        compiler_params=pltpu.CompilerParams(vmem_limit_bytes=60 << 20),
-        name="near_self",
-    )(points, charges, part)
 
 
 def halves(x):
@@ -517,7 +497,9 @@
 
 
 def final_kernel(
-    top_ids, tab_ref, r1_ref, r2_ref, nt_ref, pt_ref, near_ref, bl_ref, br_ref, lb_hbm, ct_hbm, out_ref, lb_ref, ct_ref, sem
+    top_ids, tab_ref, r1_ref, r2_ref, nt_ref, pt_ref, near_ref, bl_ref, br_ref, pts_ref, q_ref, lb_hbm, ct_hbm,
+    out_ref,
+    lb_ref, ct_ref, sf_ref, qb_ref, rhs_ref, d_ref, acc_ref, sem,
 ):
     def part(k):
         rows = pl.ds(k * 16, 16)
@@ -527,6 +509,7 @@
     child.start()
     for k in range(8):
         part(k).start()
+    near_self(pts_ref, q_ref, near_ref, sf_ref, qb_ref, rhs_ref, d_ref, acc_ref)
     tag = (iota((128, 128), 0) + 1).astype(f32)
 
     def lines(k, rows):
@@ -588,7 +571,7 @@
             d = cols16[:, u * 128 : u * 128 + 128]
             n = 16 * k + u
             out_ref[n : n + 1, :] = jnp.sum(lb_ref[n] * jnp.concatenate([d, d], axis=1), axis=0, keepdims=True)
-    out_ref[...] = out_ref[...] + near_ref[...] + bl_ref[...] + br_ref[...]
+    out_ref[...] = out_ref[...] + acc_ref[0:128, :] + bl_ref[...] + br_ref[...]
 
 
 def final(far_top, arrays, leaf_basis, child):
@@ -597,11 +580,16 @@
     return pl.pallas_call(
         final_kernel,
         out_shape=jax.ShapeDtypeStruct((128, 256), f32),
-        in_specs=[pl.BlockSpec(memory_space=pltpu.SMEM)] + [vm] * 8 + [hbm] * 2,
+        in_specs=[pl.BlockSpec(memory_space=pltpu.SMEM)] + [vm] * 10 + [hbm] * 2,
         out_specs=vm,
         scratch_shapes=[
             pltpu.VMEM((128, 64, 256), f32),
             pltpu.VMEM((64, 64, 128), f32),
+            pltpu.VMEM((SELF, 256, 64), bf16),
+            pltpu.VMEM((SELF, 256, 128), f32),
+            pltpu.VMEM((NB, 48, 256), bf16),
+            pltpu.VMEM((NB, 256, 256), f32),
+            pltpu.VMEM((136, 256), f32),
             pltpu.SemaphoreType.DMA((9,)),
         ],
         compiler_params=pltpu.CompilerParams(vmem_limit_bytes=60 << 20),
@@ -654,8 +642,7 @@
     r2 = swap(pay2.reshape(128, 5, 2, 128)).reshape(1280, 128)
     back_l = lax.ppermute(near_l, AXES, down_perm)
     back_r = lax.ppermute(near_r, AXES, up_perm)
-    near_own = near_self(flat, charges, near_own)
-    return final(far_top, [tab, r1, r2, nodes_top, parent_transfer, near_own, back_l, back_r], leaf_basis, child)
+    return final(far_top, [tab, r1, r2, nodes_top, parent_transfer, near_own, back_l, back_r, flat, charges], leaf_basis, child)
 
 
 def solution(mesh):

time: 158 us -> 162 us (1.025)
  waiting for transfers between devices: 30.9 us -> 36.2 us
  Pallas kernels: 80.6 us -> 78.7 us
    pallas_call x1 -> x0, Pallas kernels: 5.31 us -> none  [near_self(): pl.pallas_call(near_self_kernel, out_shape=jax.ShapeDtypeStruct((128, 256...]
    ppermute x1, waiting for transfers between devices: 0.01 us -> 4.3 us  [local(): back_l = lax.ppermute(near_l, AXES, down_perm)]
    pallas_call x1, Pallas kernels: 7.07 us -> 10.5 us  [final(): pl.pallas_call(final_kernel, out_shape=jax.ShapeDtypeStruct((128, 256), f...]
  transfers between devices with their start and end apart: 6 -> 6, of which waited for: 4 -> 5; matrix products, arithmetic and copies ran while one was open for 0% -> 0% of each run, Pallas kernels for 25% -> 21%
where the time goes in v5:
time: 162 us; the launch traced here: 161 us
  Pallas kernels  78.7 us (49%)
  starting transfers between devices  43.3 us (27%)
  waiting for transfers between devices  36.2 us (22%)
  local copies, waits for them, and re-layouts  2.03 us (1%)
    pallas_call x1, Pallas kernels, near(): pl.pallas_call(near_kernel, out_shape=tuple((jax.ShapeDtypeStruct((128, 2...  34.5 us
    all_to_all x2, starting transfers between devices, swap(): return lax.all_to_all(x, AXES, split_axis=0, concat_axis=0, tiled=True)  29.8 us
    pallas_call x1, Pallas kernels, far(): pl.pallas_call(far_kernel, out_shape=jax.ShapeDtypeStruct((1280, 128), f3...  26.7 us
    ppermute x1, waiting for transfers between devices, local(): from_right = lax.ppermute(to_left, AXES, down_perm)  25.7 us
    pallas_call x1, Pallas kernels, final(): pl.pallas_call(final_kernel, out_shape=jax.ShapeDtypeStruct((128, 256), f...  10.5 us
    pallas_call x1, Pallas kernels, plan(): pl.pallas_call(plan_kernel, out_shape=(jax.ShapeDtypeStruct((128, 32, 128...  7 us
    ppermute x1, starting transfers between devices, local(): from_right = lax.ppermute(to_left, AXES, down_perm)  4.75 us
    ppermute x1, starting transfers between devices, local(): back_l = lax.ppermute(near_l, AXES, down_perm)  4.75 us
  transfers between devices with their start and end apart: 6, of which 5 were waited for; matrix products, arithmetic and copies ran while one was open for 0% of the time, Pallas kernels for 21%

profile of v5, /device:TPU:1, one launch (start us, length us, event | category | flops | bytes accessed | tf_op | source)
XLA Modules:
  0.0 161.4 jit_solution(9801782116819967101)
XLA Ops:
  0.0 7.0 %plan.1 = (f32[128,32,128]{2,1,0:T(8,128)}, f32[32,128]{1,0:T(8,128)}, s32[8,256]{1,0:T(8,128)}, f32[392,256]{1,0:T(8,128)}, f32[392,256]{1,0:T(8,128)}) custom-call(s32[1]{0:T(128)} %bitcast.me_ref, s32[16,128]{1,0:T(8,128)} %bitcast.28, s32[16,16]{1,0:T(8,128)} %mid_ref.1, s32[6,128]{1,0:T(8,128)} %bitcast.30, f32[3,64,128]{2,1,0:T(8,128)} %bitcast.25, ...), custom_call_target="tpu_custom_call" | custom-call | tf_op jit(solution)/shard_map/plan/pallas_call | solution.py:153
  7.0 0.0 copy-start.8
  7.0 0.0 copy-start.7
  7.0 0.0 copy-start.6
  7.0 11.5 %all-to-all-start = ((f32[128,32,128]{2,1,0:T(8,128)}), f32[128,32,128]{2,1,0:T(8,128)S(1)}, u32[]{:S(2)}, u32[]{:S(2)}) async-start(f32[128,32,128]{2,1,0:T(8,128)} %get-tuple-element.22), calls=%async_computation | async-start | bytes 4194304 | tf_op jit(solution)/shard_map/all_to_all | solution.py:601
  18.5 0.0 copy-done.8
  18.5 4.8 %collective-permute-start.1 = (f32[392,256]{1,0:T(8,128)S(1)}, f32[392,256]{1,0:T(8,128)S(1)}, u32[]{:S(2)}, u32[]{:S(2)}) collective-permute-start(f32[392,256]{1,0:T(8,128)S(1)} %copy-done.8), channel_id=1, source_target_pairs={{1,0},{2,1},{3,2},{4,3},{5,4},{6,5},{7,6},{8,7},{9,8},{10,9},{11,1... | collective-permute-start | bytes 1204232 | tf_op jit(solution)/shard_map/ppermute | solution.py:626
  23.3 0.0 copy-done.7
  23.3 1.9 %collective-permute-start = (f32[392,256]{1,0:T(8,128)S(1)}, f32[392,256]{1,0:T(8,128)S(1)}, u32[]{:S(2)}, u32[]{:S(2)}) collective-permute-start(f32[392,256]{1,0:T(8,128)S(1)} %copy-done.7), channel_id=1, source_target_pairs={{0,1},{1,2},{2,3},{3,4},{4,5},{5,6},{6,7},{7,8},{8,9},{9,10},{10,1... | collective-permute-start | bytes 1204232 | tf_op jit(solution)/shard_map/ppermute | solution.py:627
  25.2 25.7 %collective-permute-done.1.tgt_r = f32[392,256]{1,0:T(8,128)S(1)} collective-permute-done((f32[392,256]{1,0:T(8,128)S(1)}, f32[392,256]{1,0:T(8,128)S(1)}, u32[]{:S(2)}, u32[]{:S(2)}) %collective-permute-start.1) | collective-permute-done | bytes 401440 | tf_op jit(solution)/shard_map/ppermute | solution.py:626
  50.9 0.0 copy-start.2
  51.0 1.5 collective-permute-done.tgt_l
  52.4 0.0 copy-start.3
  52.4 0.0 copy-done.6
  52.5 0.7 pad_add_fusion
  53.1 0.0 copy-done.2
  53.1 0.1 copy-done.3
  53.2 34.5 %near.1 = (f32[128,256]{1,0:T(8,128)}, f32[128,256]{1,0:T(8,128)}, f32[128,256]{1,0:T(8,128)}, f32[128,64]{1,0:T(8,128)}, f32[16,64]{1,0:T(8,128)}, /*index=5*/f32[1,128]{1,0:T(1,128)}) custom-call(s32[6144]{0:T(1024)} %bitcast.27, f32[392,256]{1,0:T(8,128)} %copy-done.3, f32[392,256]{1,0:T(8,128)} %copy-done.2, f32[384,256]{1,0:T(8,128)} %bitcast.21, ...), custom_call_target="tpu_custom_call" | custom-call | tf_op jit(solution)/shard_map/near/pallas_call | solution.py:317
  87.7 0.0 all-to-all-done
  87.7 0.0 copy-start
  87.7 0.2 convert_reduce_fusion
  88.0 1.0 convert_element_type.16.ids_ref
  89.0 0.1 copy-done
  89.1 0.0 copy-start.10
  89.1 0.0 copy-start.9
  89.1 26.7 %far.1 = f32[1280,128]{1,0:T(8,128)} custom-call(s32[3072]{0:T(1024)} %convert_element_type.16.ids_ref, f32[4096,128]{1,0:T(8,128)} %bitcast.17, f32[3,64,128]{2,1,0:T(8,128)} %bitcast.26, f32[3,16,64]{2,1,0:T(8,128)} %nm_ref.3, f32[128,64]{1,0:T(8,128)} %get-tuple-element.31.lm_ref, f32[16,64]{1,0:T(8,128)} %get-tuple-element.32.mm_ref, ...), custom_call_target="tpu_custom_call" | custom-call | tf_op jit(solution)/shard_map/far/pallas_call | solution.py:479
  115.7 18.3 %all-to-all-start.1 = ((f32[128,5,2,128]{3,2,1,0:T(2,128)}), f32[128,5,2,128]{3,2,1,0:T(2,128)S(1)}, u32[]{:S(2)}, u32[]{:S(2)}) async-start(f32[128,5,2,128]{3,2,1,0:T(2,128)} %bitcast.24), calls=%async_computation.1 | async-start | bytes 1310720 | tf_op jit(solution)/shard_map/all_to_all | solution.py:601
  134.1 0.0 copy-done.10
  134.1 4.8 %collective-permute-start.2 = (f32[128,256]{1,0:T(8,128)S(1)}, f32[128,256]{1,0:T(8,128)S(1)}, u32[]{:S(2)}, u32[]{:S(2)}) collective-permute-start(f32[128,256]{1,0:T(8,128)S(1)} %copy-done.10), channel_id=1, source_target_pairs={{1,0},{2,1},{3,2},{4,3},{5,4},{6,5},{7,6},{8,7},{9,8},{10,9},{11,1... | collective-permute-start | bytes 393224 | tf_op jit(solution)/shard_map/ppermute | solution.py:643
  138.8 0.0 copy-done.9
  138.8 2.1 %collective-permute-start.3 = (f32[128,256]{1,0:T(8,128)S(1)}, f32[128,256]{1,0:T(8,128)S(1)}, u32[]{:S(2)}, u32[]{:S(2)}) collective-permute-start(f32[128,256]{1,0:T(8,128)S(1)} %copy-done.9), channel_id=1, source_target_pairs={{0,1},{1,2},{2,3},{3,4},{4,5},{5,6},{6,7},{7,8},{8,9},{9,10},{10,1... | collective-permute-start | bytes 393224 | tf_op jit(solution)/shard_map/ppermute | solution.py:644
  140.9 4.3 %collective-permute-done.2.bl_ref = f32[128,256]{1,0:T(8,128)S(1)} collective-permute-done((f32[128,256]{1,0:T(8,128)S(1)}, f32[128,256]{1,0:T(8,128)S(1)}, u32[]{:S(2)}, u32[]{:S(2)}) %collective-permute-start.2) | collective-permute-done | bytes 131104 | tf_op jit(solution)/shard_map/ppermute | solution.py:643
  145.2 0.0 copy-start.4
  145.2 2.5 %collective-permute-done.3.br_ref = f32[128,256]{1,0:T(8,128)S(1)} collective-permute-done((f32[128,256]{1,0:T(8,128)S(1)}, f32[128,256]{1,0:T(8,128)S(1)}, u32[]{:S(2)}, u32[]{:S(2)}) %collective-permute-start.3) | collective-permute-done | bytes 131104 | tf_op jit(solution)/shard_map/ppermute | solution.py:644
  147.7 0.0 copy-start.5
  147.7 2.2 %all-to-all-done.1 = f32[128,5,2,128]{3,2,1,0:T(2,128)S(1)} async-done(((f32[128,5,2,128]{3,2,1,0:T(2,128)}), f32[128,5,2,128]{3,2,1,0:T(2,128)S(1)}, u32[]{:S(2)}, u32[]{:S(2)}) %all-to-all-start.1) | async-done | bytes 655392 | tf_op jit(solution)/shard_map/all_to_all | solution.py:601
  149.9 0.0 copy-start.1
  149.9 0.0 copy-done.4
  149.9 0.0 copy-done.5
  149.9 0.8 copy-done.1
  150.8 10.5 %final.1 = f32[128,256]{1,0:T(8,128)} custom-call(s32[2,16]{1,0:T(2,128)} %top_ids.1, f32[32,128]{1,0:T(8,128)} %get-tuple-element.21.tab_ref, f32[4096,128]{1,0:T(8,128)} %bitcast.18, f32[1280,128]{1,0:T(8,128)} %bitcast.23, f32[3,2,64]{2,1,0:T(2,128)} %nt_ref.3, f32[16,64,64]{2,1,0:T(8,128)} %pt_ref.3, f32[128,256]{1,0:T(8,128)} %get-tuple-element.34.near_ref, ...), custom_call_target="tpu_custom_call" | custom-call | tf_op jit(solution)/shard_map/final/pallas_call | solution.py:580
  (2 shorter events, 0.0 us)
Async XLA Ops:
  7.0 11.5 %copy-start.8 = (f32[392,256]{1,0:T(8,128)S(1)}, f32[392,256]{1,0:T(8,128)}, u32[]{:S(2)}) copy-start(f32[392,256]{1,0:T(8,128)} %get-tuple-element.25) | copy-start | bytes 1204228
  7.0 16.3 %copy-start.7 = (f32[392,256]{1,0:T(8,128)S(1)}, f32[392,256]{1,0:T(8,128)}, u32[]{:S(2)}) copy-start(f32[392,256]{1,0:T(8,128)} %get-tuple-element.24) | copy-start | bytes 1204228
  7.0 45.4 %copy-start.6 = (s32[8,256]{1,0:T(8,128)S(1)}, s32[8,256]{1,0:T(8,128)}, u32[]{:S(2)}) copy-start(s32[8,256]{1,0:T(8,128)} %get-tuple-element.23) | copy-start | bytes 24580
  7.0 80.7 %all-to-all-start = ((f32[128,32,128]{2,1,0:T(8,128)}), f32[128,32,128]{2,1,0:T(8,128)S(1)}, u32[]{:S(2)}, u32[]{:S(2)}) async-start(f32[128,32,128]{2,1,0:T(8,128)} %get-tuple-element.22), calls=%async_computation | async-start | bytes 4194304 | tf_op jit(solution)/shard_map/all_to_all | solution.py:601
  18.5 32.4 %collective-permute-start.1 = (f32[392,256]{1,0:T(8,128)S(1)}, f32[392,256]{1,0:T(8,128)S(1)}, u32[]{:S(2)}, u32[]{:S(2)}) collective-permute-start(f32[392,256]{1,0:T(8,128)S(1)} %copy-done.8), channel_id=1, source_target_pairs={{1,0},{2,1},{3,2},{4,3},{5,4},{6,5},{7,6},{8,7},{9,8},{10,9},{11,1... | collective-permute-start | bytes 1204232 | tf_op jit(solution)/shard_map/ppermute | solution.py:626
  23.3 29.1 %collective-permute-start = (f32[392,256]{1,0:T(8,128)S(1)}, f32[392,256]{1,0:T(8,128)S(1)}, u32[]{:S(2)}, u32[]{:S(2)}) collective-permute-start(f32[392,256]{1,0:T(8,128)S(1)} %copy-done.7), channel_id=1, source_target_pairs={{0,1},{1,2},{2,3},{3,4},{4,5},{5,6},{6,7},{7,8},{8,9},{9,10},{10,1... | collective-permute-start | bytes 1204232 | tf_op jit(solution)/shard_map/ppermute | solution.py:627
  50.9 2.2 %copy-start.2 = (f32[392,256]{1,0:T(8,128)}, f32[392,256]{1,0:T(8,128)S(1)}, u32[]{:S(2)}) copy-start(f32[392,256]{1,0:T(8,128)S(1)} %collective-permute-done.1.tgt_r) | copy-start | bytes 1204228
  52.4 0.8 copy-start.3
  87.7 1.3 copy-start
  89.1 45.0 %copy-start.10 = (f32[128,256]{1,0:T(8,128)S(1)}, f32[128,256]{1,0:T(8,128)}, u32[]{:S(2)}) copy-start(f32[128,256]{1,0:T(8,128)} %get-tuple-element.35) | copy-start | bytes 393220
  89.1 49.8 %copy-start.9 = (f32[128,256]{1,0:T(8,128)S(1)}, f32[128,256]{1,0:T(8,128)}, u32[]{:S(2)}) copy-start(f32[128,256]{1,0:T(8,128)} %get-tuple-element.36) | copy-start | bytes 393220
  115.7 34.2 %all-to-all-start.1 = ((f32[128,5,2,128]{3,2,1,0:T(2,128)}), f32[128,5,2,128]{3,2,1,0:T(2,128)S(1)}, u32[]{:S(2)}, u32[]{:S(2)}) async-start(f32[128,5,2,128]{3,2,1,0:T(2,128)} %bitcast.24), calls=%async_computation.1 | async-start | bytes 1310720 | tf_op jit(solution)/shard_map/all_to_all | solution.py:601
  134.1 11.2 %collective-permute-start.2 = (f32[128,256]{1,0:T(8,128)S(1)}, f32[128,256]{1,0:T(8,128)S(1)}, u32[]{:S(2)}, u32[]{:S(2)}) collective-permute-start(f32[128,256]{1,0:T(8,128)S(1)} %copy-done.10), channel_id=1, source_target_pairs={{1,0},{2,1},{3,2},{4,3},{5,4},{6,5},{7,6},{8,7},{9,8},{10,9},{11,1... | collective-permute-start | bytes 393224 | tf_op jit(solution)/shard_map/ppermute | solution.py:643
  138.8 8.9 %collective-permute-start.3 = (f32[128,256]{1,0:T(8,128)S(1)}, f32[128,256]{1,0:T(8,128)S(1)}, u32[]{:S(2)}, u32[]{:S(2)}) collective-permute-start(f32[128,256]{1,0:T(8,128)S(1)} %copy-done.9), channel_id=1, source_target_pairs={{0,1},{1,2},{2,3},{3,4},{4,5},{5,6},{6,7},{7,8},{8,9},{9,10},{10,1... | collective-permute-start | bytes 393224 | tf_op jit(solution)/shard_map/ppermute | solution.py:644
  145.2 4.7 %copy-start.4 = (f32[128,256]{1,0:T(8,128)}, f32[128,256]{1,0:T(8,128)S(1)}, u32[]{:S(2)}) copy-start(f32[128,256]{1,0:T(8,128)S(1)} %collective-permute-done.2.bl_ref) | copy-start | bytes 393220
  147.7 2.2 %copy-start.5 = (f32[128,256]{1,0:T(8,128)}, f32[128,256]{1,0:T(8,128)S(1)}, u32[]{:S(2)}) copy-start(f32[128,256]{1,0:T(8,128)S(1)} %collective-permute-done.3.br_ref) | copy-start | bytes 393220
  149.9 0.8 copy-start.1

commit v6 on v4

--- a/solution.py
+++ b/solution.py
@@ -388,7 +388,7 @@
 
 
 def far_kernel(
-    ids_ref, r1_ref, nl_ref, nm_ref, lm_ref, mm_ref, top_ref, out_ref, v_ref, u_ref, rep_ref, one_ref, mask_ref, ra_ref, mb_ref, full_ref
+    ids_ref, r1_ref, nl_ref, nm_ref, lm_ref, mm_ref, top_ref, out_ref, tops_ref, v_ref, u_ref, rep_ref, one_ref, mask_ref, ra_ref, mb_ref, full_ref
 ):
     for c in range(8):
         r = iota((128, 128), 0) - c * 16
@@ -446,6 +446,8 @@
         rhs = weights(*(r1_ref[pl.ds(pl.multiple_of(p * 32 + 8 * c, 8), 8), :] for c in range(3)))
         return [(p, g, group(rhs, g, ids_ref[p * 24 + g], ids_ref[p * 24 + 8 + g])) for g in groups]
 
+    for c in range(3):
+        tops_ref[c * 128 : (c + 1) * 128, :] = r1_ref[pl.ds(28 + c, 128, stride=32), :]
     out_ref[...] = jnp.zeros((1280, 128), f32)
     out_ref[pl.ds(9, 128, stride=10), :] = jnp.broadcast_to(top_ref[...], (128, 128))
 
@@ -498,9 +500,9 @@
     vm = pl.BlockSpec(memory_space=pltpu.VMEM)
     return pl.pallas_call(
         far_kernel,
-        out_shape=jax.ShapeDtypeStruct((1280, 128), f32),
+        out_shape=(jax.ShapeDtypeStruct((1280, 128), f32), jax.ShapeDtypeStruct((384, 128), f32)),
         in_specs=[pl.BlockSpec(memory_space=pltpu.SMEM)] + [vm] * 6,
-        out_specs=vm,
+        out_specs=(vm, vm),
         scratch_shapes=[
             pltpu.VMEM((18 * 128, 64), f32),
             pltpu.VMEM((18 * 128, 64), f32),
@@ -517,7 +519,7 @@
 
 
 def final_kernel(
-    top_ids, tab_ref, r1_ref, r2_ref, nt_ref, pt_ref, near_ref, bl_ref, br_ref, lb_hbm, ct_hbm, out_ref, lb_ref, ct_ref, sem
+    top_ids, tab_ref, tops_ref, r2_ref, nt_ref, pt_ref, near_ref, bl_ref, br_ref, lb_hbm, ct_hbm, out_ref, lb_ref, ct_ref, sem
 ):
     def part(k):
         rows = pl.ds(k * 16, 16)
@@ -560,9 +562,9 @@
                 p = jnp.maximum(t, 0) >> 1
                 h = jnp.where(t < 0, 2, t & 1)
                 m = jnp.where(half == h, r2_ref[pl.ds(p * 10 + 9, 1), :], 0.0)
-                dx = tx - r1_ref[pl.ds(p * 32 + 28, 1), :]
-                dy = ty - r1_ref[pl.ds(p * 32 + 29, 1), :]
-                dz = tz - r1_ref[pl.ds(p * 32 + 30, 1), :]
+                dx = tx - tops_ref[pl.ds(p, 1), :]
+                dy = ty - tops_ref[pl.ds(128 + p, 1), :]
+                dz = tz - tops_ref[pl.ds(256 + p, 1), :]
                 total = total + lax.rsqrt(dx * dx + dy * dy + dz * dz + soften) * m
             return total
 
@@ -650,12 +652,12 @@
     )
     ids = r1[:, 27, 0:24].astype(i32).reshape(3072)
     r1 = r1.reshape(4096, 128)
-    pay2 = far(ids, r1, nodes_t, nodes_mid, leaf_moments, mid_moments, top_moments)
+    pay2, tops = far(ids, r1, nodes_t, nodes_mid, leaf_moments, mid_moments, top_moments)
     r2 = swap(pay2.reshape(128, 5, 2, 128)).reshape(1280, 128)
     back_l = lax.ppermute(near_l, AXES, down_perm)
     back_r = lax.ppermute(near_r, AXES, up_perm)
     near_own = near_self(flat, charges, near_own)
-    return final(far_top, [tab, r1, r2, nodes_top, parent_transfer, near_own, back_l, back_r], leaf_basis, child)
+    return final(far_top, [tab, tops, r2, nodes_top, parent_transfer, near_own, back_l, back_r], leaf_basis, child)
 
 
 def solution(mesh):

time: 158 us -> 159 us (level)
  no operation moved by 1% of the time
where the time goes in v6:
time: 159 us; the launch traced here: 158 us
  Pallas kernels  80.3 us (51%)
  starting transfers between devices  43.8 us (28%)
  waiting for transfers between devices  30.9 us (19%)
  local copies, waits for them, and re-layouts  2.08 us (1%)
    pallas_call x1, Pallas kernels, near(): pl.pallas_call(near_kernel, out_shape=tuple((jax.ShapeDtypeStruct((128, 2...  34.5 us
    all_to_all x2, starting transfers between devices, swap(): return lax.all_to_all(x, AXES, split_axis=0, concat_axis=0, tiled=True)  30.3 us
    pallas_call x1, Pallas kernels, far(): pl.pallas_call(far_kernel, out_shape=(jax.ShapeDtypeStruct((1280, 128), f...  26.8 us
    ppermute x1, waiting for transfers between devices, local(): from_right = lax.ppermute(to_left, AXES, down_perm)  25.7 us
    pallas_call x1, Pallas kernels, plan(): pl.pallas_call(plan_kernel, out_shape=(jax.ShapeDtypeStruct((128, 32, 128...  7 us
    pallas_call x1, Pallas kernels, final(): pl.pallas_call(final_kernel, out_shape=jax.ShapeDtypeStruct((128, 256), f...  6.58 us
    pallas_call x1, Pallas kernels, near_self(): pl.pallas_call(near_self_kernel, out_shape=jax.ShapeDtypeStruct((128, 256...  5.34 us
    ppermute x1, starting transfers between devices, local(): from_right = lax.ppermute(to_left, AXES, down_perm)  4.75 us
  transfers between devices with their start and end apart: 6, of which 4 were waited for; matrix products, arithmetic and copies ran while one was open for 0% of the time, Pallas kernels for 25%

profile of v6, /device:TPU:1, one launch (start us, length us, event | category | flops | bytes accessed | tf_op | source)
XLA Modules:
  0.0 158.2 jit_solution(4649866084720383107)
XLA Ops:
  0.0 7.0 %plan.1 = (f32[128,32,128]{2,1,0:T(8,128)}, f32[32,128]{1,0:T(8,128)}, s32[8,256]{1,0:T(8,128)}, f32[392,256]{1,0:T(8,128)}, f32[392,256]{1,0:T(8,128)}) custom-call(s32[1]{0:T(128)} %bitcast.me_ref, s32[16,128]{1,0:T(8,128)} %bitcast.27, s32[16,16]{1,0:T(8,128)} %mid_ref.1, s32[6,128]{1,0:T(8,128)} %bitcast.29, f32[3,64,128]{2,1,0:T(8,128)} %bitcast.24, ...), custom_call_target="tpu_custom_call" | custom-call | tf_op jit(solution)/shard_map/plan/pallas_call | solution.py:153
  7.0 0.0 copy-start.8
  7.0 0.0 copy-start.7
  7.0 0.0 copy-start.6
  7.0 11.5 %all-to-all-start = ((f32[128,32,128]{2,1,0:T(8,128)}), f32[128,32,128]{2,1,0:T(8,128)S(1)}, u32[]{:S(2)}, u32[]{:S(2)}) async-start(f32[128,32,128]{2,1,0:T(8,128)} %get-tuple-element.24), calls=%async_computation | async-start | bytes 4194304 | tf_op jit(solution)/shard_map/all_to_all | solution.py:615
  18.5 0.0 copy-done.8
  18.5 4.8 %collective-permute-start.1 = (f32[392,256]{1,0:T(8,128)S(1)}, f32[392,256]{1,0:T(8,128)S(1)}, u32[]{:S(2)}, u32[]{:S(2)}) collective-permute-start(f32[392,256]{1,0:T(8,128)S(1)} %copy-done.8), channel_id=1, source_target_pairs={{1,0},{2,1},{3,2},{4,3},{5,4},{6,5},{7,6},{8,7},{9,8},{10,9},{11,1... | collective-permute-start | bytes 1204232 | tf_op jit(solution)/shard_map/ppermute | solution.py:640
  23.3 0.0 copy-done.7
  23.3 1.9 %collective-permute-start = (f32[392,256]{1,0:T(8,128)S(1)}, f32[392,256]{1,0:T(8,128)S(1)}, u32[]{:S(2)}, u32[]{:S(2)}) collective-permute-start(f32[392,256]{1,0:T(8,128)S(1)} %copy-done.7), channel_id=1, source_target_pairs={{0,1},{1,2},{2,3},{3,4},{4,5},{5,6},{6,7},{7,8},{8,9},{9,10},{10,1... | collective-permute-start | bytes 1204232 | tf_op jit(solution)/shard_map/ppermute | solution.py:641
  25.2 25.7 %collective-permute-done.1.tgt_r = f32[392,256]{1,0:T(8,128)S(1)} collective-permute-done((f32[392,256]{1,0:T(8,128)S(1)}, f32[392,256]{1,0:T(8,128)S(1)}, u32[]{:S(2)}, u32[]{:S(2)}) %collective-permute-start.1) | collective-permute-done | bytes 401440 | tf_op jit(solution)/shard_map/ppermute | solution.py:640
  50.9 0.0 copy-start.2
  50.9 1.5 collective-permute-done.tgt_l
  52.4 0.0 copy-start.3
  52.4 0.0 copy-done.6
  52.4 0.6 pad_add_fusion
  53.1 0.0 copy-done.2
  53.1 0.1 copy-done.3
  53.2 34.5 %near.1 = (f32[128,256]{1,0:T(8,128)}, f32[128,256]{1,0:T(8,128)}, f32[128,256]{1,0:T(8,128)}, f32[128,64]{1,0:T(8,128)}, f32[16,64]{1,0:T(8,128)}, /*index=5*/f32[1,128]{1,0:T(1,128)}) custom-call(s32[6144]{0:T(1024)} %bitcast.26, f32[392,256]{1,0:T(8,128)} %copy-done.3, f32[392,256]{1,0:T(8,128)} %copy-done.2, f32[384,256]{1,0:T(8,128)} %bitcast.20, ...), custom_call_target="tpu_custom_call" | custom-call | tf_op jit(solution)/shard_map/near/pallas_call | solution.py:317
  87.7 0.0 copy-start.10
  87.7 0.0 copy-start.9
  87.7 0.0 all-to-all-done
  87.8 0.0 copy-start
  87.8 0.2 convert_reduce_fusion
  88.0 0.7 convert_element_type.16.ids_ref
  88.7 0.4 copy-done
  89.1 26.8 %far.1 = (f32[1280,128]{1,0:T(8,128)}, f32[384,128]{1,0:T(8,128)}) custom-call(s32[3072]{0:T(1024)} %convert_element_type.16.ids_ref, f32[4096,128]{1,0:T(8,128)} %bitcast.17, f32[3,64,128]{2,1,0:T(8,128)} %bitcast.25, f32[3,16,64]{2,1,0:T(8,128)} %nm_ref.3, f32[128,64]{1,0:T(8,128)} %get-tuple-element.33.lm_ref, f32[16,64]{1,0:T(8,128)} %get-tuple-element.34.mm_ref, ...), custom_call_target="tpu_custom_call" | custom-call | tf_op jit(solution)/shard_map/far/pallas_call | solution.py:501
  115.9 18.8 %all-to-all-start.1 = ((f32[128,5,2,128]{3,2,1,0:T(2,128)}), f32[128,5,2,128]{3,2,1,0:T(2,128)S(1)}, u32[]{:S(2)}, u32[]{:S(2)}) async-start(f32[128,5,2,128]{3,2,1,0:T(2,128)} %bitcast.23), calls=%async_computation.1 | async-start | bytes 1310720 | tf_op jit(solution)/shard_map/all_to_all | solution.py:615
  134.8 0.0 copy-done.10
  134.8 4.8 %collective-permute-start.2 = (f32[128,256]{1,0:T(8,128)S(1)}, f32[128,256]{1,0:T(8,128)S(1)}, u32[]{:S(2)}, u32[]{:S(2)}) collective-permute-start(f32[128,256]{1,0:T(8,128)S(1)} %copy-done.10), channel_id=1, source_target_pairs={{1,0},{2,1},{3,2},{4,3},{5,4},{6,5},{7,6},{8,7},{9,8},{10,9},{11,1... | collective-permute-start | bytes 393224 | tf_op jit(solution)/shard_map/ppermute | solution.py:657
  139.5 0.0 copy-done.9
  139.5 2.1 %collective-permute-start.3 = (f32[128,256]{1,0:T(8,128)S(1)}, f32[128,256]{1,0:T(8,128)S(1)}, u32[]{:S(2)}, u32[]{:S(2)}) collective-permute-start(f32[128,256]{1,0:T(8,128)S(1)} %copy-done.9), channel_id=1, source_target_pairs={{0,1},{1,2},{2,3},{3,4},{4,5},{5,6},{6,7},{7,8},{8,9},{9,10},{10,1... | collective-permute-start | bytes 393224 | tf_op jit(solution)/shard_map/ppermute | solution.py:658
  141.7 5.3 %near_self.1.near_ref = f32[128,256]{1,0:T(8,128)} custom-call(f32[384,256]{1,0:T(8,128)} %bitcast.21, f32[128,256]{1,0:T(8,128)} %q_ref.3, f32[128,256]{1,0:T(8,128)} %get-tuple-element.38.part_ref), custom_call_target="tpu_custom_call" | custom-call | tf_op jit(solution)/shard_map/near_self/pallas_call | solution.py:357
  147.0 0.0 collective-permute-done.2.bl_ref
  147.0 0.0 copy-start.4
  147.0 1.4 collective-permute-done.3.br_ref
  148.4 0.0 copy-start.5
  148.4 2.2 %all-to-all-done.1 = f32[128,5,2,128]{3,2,1,0:T(2,128)S(1)} async-done(((f32[128,5,2,128]{3,2,1,0:T(2,128)}), f32[128,5,2,128]{3,2,1,0:T(2,128)S(1)}, u32[]{:S(2)}, u32[]{:S(2)}) %all-to-all-start.1) | async-done | bytes 655392 | tf_op jit(solution)/shard_map/all_to_all | solution.py:615
  150.6 0.0 copy-start.1
  150.6 0.0 copy-done.4
  150.6 0.0 copy-done.5
  150.6 0.8 copy-done.1
  151.5 6.6 %final.1 = f32[128,256]{1,0:T(8,128)} custom-call(s32[2,16]{1,0:T(2,128)} %top_ids.1, f32[32,128]{1,0:T(8,128)} %get-tuple-element.23.tab_ref, f32[384,128]{1,0:T(8,128)} %get-tuple-element.36.tops_ref, f32[1280,128]{1,0:T(8,128)} %bitcast.22, f32[3,2,64]{2,1,0:T(2,128)} %nt_ref.3, f32[16,64,64]{2,1,0:T(8,128)} %pt_ref.3, f32[128,256]{1,0:T(8,128)} %near_self.1.near_ref, ...), custom_call_target="tpu_custom_call" | custom-call | tf_op jit(solution)/shard_map/final/pallas_call | solution.py:599
  (2 shorter events, 0.0 us)
Async XLA Ops:
  7.0 11.5 %copy-start.8 = (f32[392,256]{1,0:T(8,128)S(1)}, f32[392,256]{1,0:T(8,128)}, u32[]{:S(2)}) copy-start(f32[392,256]{1,0:T(8,128)} %get-tuple-element.27) | copy-start | bytes 1204228
  7.0 16.3 %copy-start.7 = (f32[392,256]{1,0:T(8,128)S(1)}, f32[392,256]{1,0:T(8,128)}, u32[]{:S(2)}) copy-start(f32[392,256]{1,0:T(8,128)} %get-tuple-element.26) | copy-start | bytes 1204228
  7.0 45.4 %copy-start.6 = (s32[8,256]{1,0:T(8,128)S(1)}, s32[8,256]{1,0:T(8,128)}, u32[]{:S(2)}) copy-start(s32[8,256]{1,0:T(8,128)} %get-tuple-element.25) | copy-start | bytes 24580
  7.0 80.7 %all-to-all-start = ((f32[128,32,128]{2,1,0:T(8,128)}), f32[128,32,128]{2,1,0:T(8,128)S(1)}, u32[]{:S(2)}, u32[]{:S(2)}) async-start(f32[128,32,128]{2,1,0:T(8,128)} %get-tuple-element.24), calls=%async_computation | async-start | bytes 4194304 | tf_op jit(solution)/shard_map/all_to_all | solution.py:615
  18.5 32.4 %collective-permute-start.1 = (f32[392,256]{1,0:T(8,128)S(1)}, f32[392,256]{1,0:T(8,128)S(1)}, u32[]{:S(2)}, u32[]{:S(2)}) collective-permute-start(f32[392,256]{1,0:T(8,128)S(1)} %copy-done.8), channel_id=1, source_target_pairs={{1,0},{2,1},{3,2},{4,3},{5,4},{6,5},{7,6},{8,7},{9,8},{10,9},{11,1... | collective-permute-start | bytes 1204232 | tf_op jit(solution)/shard_map/ppermute | solution.py:640
  23.3 29.1 %collective-permute-start = (f32[392,256]{1,0:T(8,128)S(1)}, f32[392,256]{1,0:T(8,128)S(1)}, u32[]{:S(2)}, u32[]{:S(2)}) collective-permute-start(f32[392,256]{1,0:T(8,128)S(1)} %copy-done.7), channel_id=1, source_target_pairs={{0,1},{1,2},{2,3},{3,4},{4,5},{5,6},{6,7},{7,8},{8,9},{9,10},{10,1... | collective-permute-start | bytes 1204232 | tf_op jit(solution)/shard_map/ppermute | solution.py:641
  50.9 2.2 %copy-start.2 = (f32[392,256]{1,0:T(8,128)}, f32[392,256]{1,0:T(8,128)S(1)}, u32[]{:S(2)}) copy-start(f32[392,256]{1,0:T(8,128)S(1)} %collective-permute-done.1.tgt_r) | copy-start | bytes 1204228
  52.4 0.8 copy-start.3
  87.7 47.0 %copy-start.10 = (f32[128,256]{1,0:T(8,128)S(1)}, f32[128,256]{1,0:T(8,128)}, u32[]{:S(2)}) copy-start(f32[128,256]{1,0:T(8,128)} %get-tuple-element.39) | copy-start | bytes 393220
  87.7 51.8 %copy-start.9 = (f32[128,256]{1,0:T(8,128)S(1)}, f32[128,256]{1,0:T(8,128)}, u32[]{:S(2)}) copy-start(f32[128,256]{1,0:T(8,128)} %get-tuple-element.40) | copy-start | bytes 393220
  87.8 1.3 copy-start
  115.9 34.7 %all-to-all-start.1 = ((f32[128,5,2,128]{3,2,1,0:T(2,128)}), f32[128,5,2,128]{3,2,1,0:T(2,128)S(1)}, u32[]{:S(2)}, u32[]{:S(2)}) async-start(f32[128,5,2,128]{3,2,1,0:T(2,128)} %bitcast.23), calls=%async_computation.1 | async-start | bytes 1310720 | tf_op jit(solution)/shard_map/all_to_all | solution.py:615
  134.8 12.2 %collective-permute-start.2 = (f32[128,256]{1,0:T(8,128)S(1)}, f32[128,256]{1,0:T(8,128)S(1)}, u32[]{:S(2)}, u32[]{:S(2)}) collective-permute-start(f32[128,256]{1,0:T(8,128)S(1)} %copy-done.10), channel_id=1, source_target_pairs={{1,0},{2,1},{3,2},{4,3},{5,4},{6,5},{7,6},{8,7},{9,8},{10,9},{11,1... | collective-permute-start | bytes 393224 | tf_op jit(solution)/shard_map/ppermute | solution.py:657
  139.5 8.9 %collective-permute-start.3 = (f32[128,256]{1,0:T(8,128)S(1)}, f32[128,256]{1,0:T(8,128)S(1)}, u32[]{:S(2)}, u32[]{:S(2)}) collective-permute-start(f32[128,256]{1,0:T(8,128)S(1)} %copy-done.9), channel_id=1, source_target_pairs={{0,1},{1,2},{2,3},{3,4},{4,5},{5,6},{6,7},{7,8},{8,9},{9,10},{10,1... | collective-permute-start | bytes 393224 | tf_op jit(solution)/shard_map/ppermute | solution.py:658
  147.0 3.6 %copy-start.4 = (f32[128,256]{1,0:T(8,128)}, f32[128,256]{1,0:T(8,128)S(1)}, u32[]{:S(2)}) copy-start(f32[128,256]{1,0:T(8,128)S(1)} %collective-permute-done.2.bl_ref) | copy-start | bytes 393220
  148.4 2.2 %copy-start.5 = (f32[128,256]{1,0:T(8,128)}, f32[128,256]{1,0:T(8,128)S(1)}, u32[]{:S(2)}) copy-start(f32[128,256]{1,0:T(8,128)S(1)} %collective-permute-done.3.br_ref) | copy-start | bytes 393220
  150.6 0.9 copy-start.1
